TPU v7x, 32 devices: a whole 2x2x4 slice. The times are simulated.
32 devices in a mesh: dp: 32 (over z, y, x, core).
Axes of the slice: x: 2, y: 2, z: 4, core: 2. Of those that a mesh axis runs over, the one named last changes fastest.
Arguments:
- latents: bfloat16 [32, 256, 768], P('dp'), may hold values from -6 to 6
- conditioning: bfloat16 [32, 768], P('dp'), may hold values from -3 to 3
- cotangent: bfloat16 [32, 256, 768], P('dp'), may hold values from -6 to 6
- weights: float32 [18, 768, 768], P(None, 'dp'), may hold values from -1 to 1
- biases: float32 [14, 768], P(None, 'dp'), may hold values from -1.8 to 1.8
- momenta: float32 [18, 768, 768], P(None, 'dp'), may hold values from -0.3 to 0.3
- bias_momenta: float32 [14, 768], P(None, 'dp'), may hold values from -1.8 to 1.8
- counts: int32 [32], replicated, may hold values from 0 to 1, as said below
Outputs:
- output: bfloat16 [32, 256, 768], P('dp')
- input_grad: float32 [32, 256, 768], P('dp')
- cond_grad: float32 [32, 768], P('dp')
- weight_grads: float32 [18, 768, 768], P(None, 'dp')
- bias_grads: float32 [14, 768], P(None, 'dp')
- new_weights: float32 [18, 768, 768], P(None, 'dp')
- new_momenta: float32 [18, 768, 768], P(None, 'dp')
- new_biases: float32 [14, 768], P(None, 'dp')
- new_bias_momenta: float32 [14, 768], P(None, 'dp')
Inputs may be any that keep to these rules, and one draw needn't show every extreme that they name: Device d's first counts[d] of its 1 slots are live. Exactly 18 devices hold no live latent, every other device holds at least one, and some device holds 1.
All inputs are finite; a program needn't handle non-finite values.
Results may differ from a plain program's by a relative error of at most 0.01.
The roundings to bfloat16 on the way count: a program that leaves them out, or rounds other values in their place, can miss the bound.
Values may be sent and summed in bfloat16 or wider, within the bound.
No kernel may reach another device: no remote copies, remote signals or barrier semaphores. Data moves between devices by JAX's collectives and lax.ppermute only.
A program may use at most 256 MiB of HBM per device.

v0:
```python
import functools

import jax
import jax.numpy as jnp
from jax import lax
from jax.experimental import pallas as pl
from jax.experimental.pallas import tpu as pltpu
from jax.sharding import PartitionSpec as P


HEADS = 12
NS_ITERS = 2
ADA = 6
COLOURS = 3

COEF_FIRST = 3.4445
COEF_SECOND = -4.775
COEF_THIRD = 2.0315
BETA_WEIGHT = 0.95
BETA_BIAS = 0.9
RATE_WEIGHT = 1.0
RATE_BIAS = 0.1
NORM_EPS = 1e-06


def product(spec, left, right):
    return jnp.einsum(spec, left, right, preferred_element_type=jnp.float32)


def flip(values, bit):
    devices = lax.axis_size("dp")
    return lax.ppermute(values, "dp", [(i, i ^ (1 << bit)) for i in range(devices)])


def bit_of(myself, bit):
    return (myself >> bit) & 1


def joined(values, other, taken, axis):
    return jnp.where(
        taken == 1, jnp.stack([other, values], axis), jnp.stack([values, other], axis)
    )


def gather_all(groups, orders, myself, first_too, last_too):
    carried = first_too
    for stage in range(len(orders[0])):
        others = [flip(group, order[stage]) for group, order in zip(groups, orders)]
        if stage == len(orders[0]) - 1:
            carried = last_too(carried)
        if stage in (0, len(orders[0]) - 1):
            others[-1], carried = lax.optimization_barrier((others[-1], carried))
        for index, order in enumerate(orders):
            bit = order[stage]
            groups[index] = joined(groups[index], others[index], bit_of(myself, bit), 0)
    return groups, carried


def split_bit(values, mine, position, sent_as):
    send = lax.dynamic_index_in_dim(values, 1 - mine, position, keepdims=False)
    keep = lax.dynamic_index_in_dim(values, mine, position, keepdims=False)
    return keep, send.astype(sent_as)


def scatter_all(halves, orders, myself, axis, spread, between):
    left = [sorted(order, reverse=True) for order in orders]
    carried = None
    totals = []
    for stage in range(len(orders[0])):
        others = [flip(send, order[stage]) for (_, send), order in zip(halves, orders)]
        if stage in between:
            carried = between[stage](carried)
            others[-1], carried = lax.optimization_barrier((others[-1], carried))
        totals = [
            keep + other.astype(jnp.float32) for (keep, _), other in zip(halves, others)
        ]
        for index, order in enumerate(orders):
            left[index].remove(order[stage])
            if stage == 0:
                totals[index] = spread(totals[index], len(left[index]))
            if left[index]:
                bit = order[stage + 1]
                position = axis + left[index].index(bit)
                halves[index] = split_bit(
                    totals[index], bit_of(myself, bit), position, jnp.bfloat16
                )
    return totals, carried


def index_bits(devices):
    return devices.bit_length() - 1


def colour_orders(devices):
    chip_bits = list(range(1, index_bits(devices)))
    rest, last = chip_bits[:-1], chip_bits[-1:]
    shifts = [(colour * len(rest)) // COLOURS for colour in range(COLOURS)]
    return [tuple(rest[shift:] + rest[:shift] + last) for shift in shifts]


def contract(left, right, left_dim, right_dim):
    return lax.dot_general(
        left, right, (((left_dim,), (right_dim,)), ((), ())), preferred_element_type=jnp.float32
    )


def layer_norm(stream):
    centred = stream - jnp.mean(stream, axis=-1, keepdims=True)
    inverse = lax.rsqrt(jnp.mean(centred * centred, axis=-1, keepdims=True) + NORM_EPS)
    return (centred * inverse, inverse)


def norm_back(normed, inverse, upstream):
    return inverse * (
        upstream
        - jnp.mean(upstream, axis=-1, keepdims=True)
        - normed * jnp.mean(upstream * normed, axis=-1, keepdims=True)
    )


def column_sum(values):
    return jnp.sum(values, axis=0, keepdims=True)


def scores_of(query, keys, width):
    return contract(query, keys, 1, 1) * width ** (-0.5)


def chunk_places(order):
    count = len(order)
    return [
        sum(((chip >> (bit - 1)) & 1) << place for place, bit in enumerate(order))
        for chip in range(1 << count)
    ]


def whole_weight(mine_ref, other_ref, index, core, order):
    places = chunk_places(order) if order else [0]
    mine, other = [
        jnp.concatenate([ref[place, index] for place in places], axis=0)
        for ref in (mine_ref, other_ref)
    ]
    return jnp.concatenate(
        [jnp.where(core == 1, other, mine), jnp.where(core == 1, mine, other)], axis=1
    )


def attention_forward(
    order,
    place_ref,
    source_ref,
    mod_ref,
    offsets_ref,
    mine_ref,
    other_ref,
    lefts_ref,
    qkv_ref,
    attn_ref,
    middle_ref,
):
    core = place_ref[0]
    seqlen, features = source_ref.shape
    width = features // HEADS
    stream = source_ref[...].astype(jnp.float32)
    normed, _ = layer_norm(stream)
    attn_input = (normed * (1.0 + mod_ref[1:2]) + mod_ref[0:1]).astype(jnp.bfloat16)
    lefts_ref[0] = attn_input
    qkv_ref[0] = (contract(attn_input, whole_weight(mine_ref, other_ref, 0, core, order), 1, 0) + offsets_ref[6:7]).astype(
        jnp.bfloat16
    )
    qkv_ref[1] = contract(attn_input, whole_weight(mine_ref, other_ref, 1, core, order), 1, 0).astype(jnp.bfloat16)
    qkv_ref[2] = (contract(attn_input, whole_weight(mine_ref, other_ref, 2, core, order), 1, 0) + offsets_ref[7:8]).astype(
        jnp.bfloat16
    )
    first = lax.broadcasted_iota(jnp.int32, (seqlen, 2 * width), 1) < width
    for pair in range(HEADS // 2):
        columns = slice(2 * width * pair, 2 * width * (pair + 1))
        query, keys, values = qkv_ref[0, :, columns], qkv_ref[1, :, columns], qkv_ref[2, :, columns]
        halves = []
        for mask in (first, jnp.logical_not(first)):
            scores = scores_of(jnp.where(mask, query, jnp.zeros_like(query)), keys, width)
            log_total = jnp.log(jnp.sum(jnp.exp(scores), axis=-1, keepdims=True))
            probs = jnp.exp(scores - log_total).astype(jnp.bfloat16)
            halves.append(contract(probs, values, 1, 0))
        lefts_ref[1, :, columns] = jnp.where(first, *halves).astype(jnp.bfloat16)
    attn_out = contract(lefts_ref[1], whole_weight(mine_ref, other_ref, 3, core, order), 1, 0) + offsets_ref[8:9]
    attn_ref[...] = attn_out
    middle = stream + mod_ref[2:3] * attn_out
    middle_ref[...] = middle
    normed_two, _ = layer_norm(middle)
    lefts_ref[2] = (normed_two * (1.0 + mod_ref[4:5]) + mod_ref[3:4]).astype(jnp.bfloat16)


def split_columns(values, core):
    width = values.shape[-1] // 2
    low, high = values[:, :width], values[:, width:]
    return (jnp.where(core == 1, high, low), jnp.where(core == 1, low, high))


def mlp_both_ways(
    up_order,
    down_order,
    place_ref,
    lefts_ref,
    middle_ref,
    attn_ref,
    upstream_ref,
    mod_ref,
    offsets_ref,
    up_ref,
    up_other_ref,
    down_ref,
    down_other_ref,
    output_ref,
    hidden_ref,
    keep_ref,
    send_ref,
    grad_middle_ref,
    grad_attn_ref,
    rows_ref,
    total_ref,
    grad_total_ref,
    grad_mlp_ref,
):
    step = pl.program_id(0)
    last = pl.num_programs(0) - 1
    core, live = place_ref[0], place_ref[1] > 0
    scale = 0.7978845608028654

    @pl.when(step == 0)
    def _():
        total_ref[...] = jnp.zeros_like(total_ref)
        grad_total_ref[...] = jnp.zeros_like(grad_total_ref)
        grad_mlp = jnp.where(live, upstream_ref[...].astype(jnp.float32) * mod_ref[5:6], 0.0)
        grad_mlp_b = grad_mlp.astype(jnp.bfloat16)
        grad_mlp_ref[...] = grad_mlp_b
        keep_ref[0], send_ref[0] = split_columns(grad_mlp_b, core)
        rows_ref[...] = jnp.zeros_like(rows_ref)
        rows_ref[pl.ds(10 + last, 1)] = column_sum(grad_mlp)

    up_w = whole_weight(up_ref, up_other_ref, 0, core, up_order)
    down_w = whole_weight(down_ref, down_other_ref, 0, core, down_order)
    before = contract(lefts_ref[0], up_w, 1, 0) + offsets_ref[pl.ds(9 + step, 1)]
    square = before * before
    bend = jnp.tanh(scale * (before + 0.044715 * square * before))
    hidden = (0.5 * before * (1.0 + bend)).astype(jnp.bfloat16)
    hidden_ref[0] = hidden
    total_ref[...] += contract(hidden, down_w, 1, 0)
    slope = 0.5 * (1.0 + bend) + 0.5 * before * (1.0 - bend * bend) * scale * (
        1.0 + 3.0 * 0.044715 * square
    )
    grad_pre = jnp.where(live, contract(grad_mlp_ref[...], down_w, 1, 1) * slope, 0.0)
    grad_pre_b = grad_pre.astype(jnp.bfloat16)
    keep_ref[step + 1], send_ref[step + 1] = split_columns(grad_pre_b, core)
    rows_ref[pl.ds(9 + step, 1)] = column_sum(grad_pre)
    grad_total_ref[...] += contract(grad_pre_b, up_w, 1, 1)

    @pl.when(step == last)
    def _():
        middle = middle_ref[...]
        grad_out = upstream_ref[...].astype(jnp.float32)
        mlp_out = total_ref[...] + offsets_ref[pl.ds(10 + last, 1)]
        output = middle + mod_ref[5:6] * mlp_out
        output_ref[...] = jnp.where(live, output, 0.0).astype(jnp.bfloat16)
        rows_ref[5:6] = jnp.where(live, column_sum(grad_out * mlp_out), 0.0)
        normed, inverse = layer_norm(middle)
        grad_in = grad_total_ref[...]
        rows_ref[3:4] = column_sum(grad_in)
        rows_ref[4:5] = column_sum(grad_in * normed)
        grad_middle = grad_out + norm_back(normed, inverse, grad_in * (1.0 + mod_ref[4:5]))
        grad_middle = jnp.where(live, grad_middle, 0.0)
        grad_middle_ref[...] = grad_middle
        rows_ref[2:3] = column_sum(grad_middle * attn_ref[...])
        grad_attn = grad_middle * mod_ref[2:3]
        grad_attn_ref[...] = grad_attn.astype(jnp.bfloat16)
        rows_ref[8:9] = column_sum(grad_attn)


def attention_backward(
    order,
    place_ref,
    source_ref,
    mod_ref,
    mine_ref,
    other_ref,
    qkv_ref,
    grad_middle_ref,
    grad_attn_ref,
    rows_in_ref,
    grad_source_ref,
    keep_ref,
    send_ref,
    rows_ref,
    grads_ref,
    context_ref,
):
    seqlen, features = source_ref.shape
    width = features // HEADS
    core, live = place_ref[0], place_ref[1] > 0
    rows_ref[...] = rows_in_ref[...]
    grad_attn = grad_attn_ref[...]
    keep_ref[3], send_ref[3] = split_columns(grad_attn, core)
    context_ref[...] = contract(
        grad_attn, whole_weight(mine_ref, other_ref, 3, core, order), 1, 1
    ).astype(jnp.bfloat16)
    first = lax.broadcasted_iota(jnp.int32, (seqlen, 2 * width), 1) < width
    for pair in range(HEADS // 2):
        columns = slice(2 * width * pair, 2 * width * (pair + 1))
        query, keys, values = qkv_ref[0, :, columns], qkv_ref[1, :, columns], qkv_ref[2, :, columns]
        upstream = context_ref[:, columns]
        parts = []
        for mask in (first, jnp.logical_not(first)):
            scores = scores_of(jnp.where(mask, query, jnp.zeros_like(query)), keys, width)
            log_total = jnp.log(jnp.sum(jnp.exp(scores), axis=-1, keepdims=True))
            probs = jnp.exp(scores - log_total)
            grad_values = contract(probs.astype(jnp.bfloat16), upstream, 0, 0)
            grad_probs = contract(
                jnp.where(mask, upstream, jnp.zeros_like(upstream)), values, 1, 1
            )
            row_dot = jnp.sum(probs * grad_probs, axis=-1, keepdims=True)
            grad_scores = (probs * (grad_probs - row_dot) * width ** (-0.5)).astype(jnp.bfloat16)
            parts.append(
                (
                    contract(grad_scores, keys, 1, 0),
                    contract(grad_scores, query, 0, 0),
                    grad_values,
                )
            )
        for index in range(3):
            merged = jnp.where(live, jnp.where(first, parts[0][index], parts[1][index]), 0.0)
            grads_ref[index, :, columns] = merged.astype(jnp.bfloat16)
            if index != 1:
                row = 6 if index == 0 else 7
                rows_ref[row : row + 1, columns] = column_sum(merged)
    grad_in = jnp.zeros((seqlen, features), jnp.float32)
    for index in range(3):
        grads = grads_ref[index]
        keep_ref[index], send_ref[index] = split_columns(grads, core)
        grad_in += contract(grads, whole_weight(mine_ref, other_ref, index, core, order), 1, 1)
    normed, inverse = layer_norm(source_ref[...].astype(jnp.float32))
    rows_ref[0:1] = column_sum(grad_in)
    rows_ref[1:2] = column_sum(grad_in * normed)
    grad_source_ref[...] = jnp.where(
        live,
        grad_middle_ref[...] + norm_back(normed, inverse, grad_in * (1.0 + mod_ref[1:2])),
        0.0,
    )


def pair_products(
    chunk, mine_ref, left_ref, left_other_ref, right_ref, right_other_ref, keep_ref, send_ref
):
    total = contract(left_ref[0], right_ref[0], 0, 0) + contract(
        left_other_ref[0], right_other_ref[0], 0, 0
    )
    for start in range(0, total.shape[0] // 2, chunk):
        low = total[2 * start : 2 * start + chunk]
        high = total[2 * start + chunk : 2 * start + 2 * chunk]
        mine = mine_ref[0] == 1
        keep_ref[0, start : start + chunk] = jnp.where(mine, high, low)
        send_ref[0, start : start + chunk] = jnp.where(mine, low, high).astype(jnp.bfloat16)


def plain_products(left_ref, left_other_ref, right_ref, right_other_ref, out_ref):
    out_ref[0] = contract(left_ref[0], right_ref[0], 0, 0) + contract(
        left_other_ref[0], right_other_ref[0], 0, 0
    )


def struct(shape, dtype):
    return jax.ShapeDtypeStruct(shape, dtype)


VMEM = pl.BlockSpec(memory_space=pltpu.VMEM)
SMEM = pl.BlockSpec(memory_space=pltpu.SMEM)


def resident(shape):
    zeros = (0,) * len(shape)
    return pl.BlockSpec(shape, lambda step: zeros)


def run_attention_forward(order, place, source, modulation, offsets, attn_w, attn_w_other):
    seqlen, features = source.shape
    return pl.pallas_call(
        functools.partial(attention_forward, order),
        name="attention_forward",
        out_shape=(
            struct((3, seqlen, features), jnp.bfloat16),
            struct((3, seqlen, features), jnp.bfloat16),
            struct((seqlen, features), jnp.float32),
            struct((seqlen, features), jnp.float32),
        ),
        in_specs=[SMEM] + [VMEM] * 5,
        out_specs=(VMEM,) * 4,
        compiler_params=pltpu.CompilerParams(vmem_limit_bytes=24 << 20),
        cost_estimate=pl.CostEstimate(
            flops=8 * seqlen * features * features + 8 * HEADS * seqlen * seqlen * 128,
            bytes_accessed=attn_w.size * 4 + source.size * 20,
            transcendentals=2 * HEADS * seqlen * seqlen,
        ),
    )(place, source, modulation, offsets, attn_w, attn_w_other)


def run_mlp(mlp_orders, place, lefts, middle, attn_out, upstream, modulation, offsets, up_ws, down_ws):
    seqlen, features = middle.shape
    chips, steps, rows, _ = up_ws[0].shape
    half = features // 2
    whole = (seqlen, features)
    return pl.pallas_call(
        functools.partial(mlp_both_ways, *mlp_orders),
        name="mlp_both_ways",
        grid=(steps,),
        out_shape=(
            struct(whole, jnp.bfloat16),
            struct((steps,) + whole, jnp.bfloat16),
            struct((steps + 1, seqlen, half), jnp.bfloat16),
            struct((steps + 1, seqlen, half), jnp.bfloat16),
            struct(whole, jnp.float32),
            struct(whole, jnp.bfloat16),
            struct(offsets.shape, jnp.float32),
        ),
        in_specs=[
            SMEM,
            pl.BlockSpec((1,) + whole, lambda step: (2, 0, 0)),
            resident(whole),
            resident(whole),
            resident(whole),
            resident(modulation.shape),
            resident(offsets.shape),
        ]
        + [pl.BlockSpec((chips, 1, rows, half), lambda step: (0, step, 0, 0))] * 4,
        out_specs=(
            resident(whole),
            pl.BlockSpec((1,) + whole, lambda step: (step, 0, 0)),
            resident((steps + 1, seqlen, half)),
            resident((steps + 1, seqlen, half)),
            resident(whole),
            resident(whole),
            resident(offsets.shape),
        ),
        scratch_shapes=[
            pltpu.VMEM(whole, jnp.float32),
            pltpu.VMEM(whole, jnp.float32),
            pltpu.VMEM(whole, jnp.bfloat16),
        ],
        compiler_params=pltpu.CompilerParams(vmem_limit_bytes=28 << 20),
        cost_estimate=pl.CostEstimate(
            flops=8 * seqlen * features * features * steps,
            bytes_accessed=up_ws[0].size * 8 + seqlen * features * 40,
            transcendentals=seqlen * features * steps,
        ),
    )(place, lefts, middle, attn_out, upstream, modulation, offsets, *up_ws, *down_ws)


def run_attention_backward(
    order, place, source, modulation, attn_w, attn_w_other, qkv, grad_middle, grad_attn, rows
):
    seqlen, features = source.shape
    half = features // 2
    return pl.pallas_call(
        functools.partial(attention_backward, order),
        name="attention_backward",
        out_shape=(
            struct((seqlen, features), jnp.float32),
            struct((4, seqlen, half), jnp.bfloat16),
            struct((4, seqlen, half), jnp.bfloat16),
            struct(rows.shape, jnp.float32),
        ),
        in_specs=[SMEM] + [VMEM] * 8,
        out_specs=(VMEM,) * 4,
        scratch_shapes=[
            pltpu.VMEM((3, seqlen, features), jnp.bfloat16),
            pltpu.VMEM((seqlen, features), jnp.bfloat16),
        ],
        compiler_params=pltpu.CompilerParams(vmem_limit_bytes=24 << 20),
        cost_estimate=pl.CostEstimate(
            flops=8 * seqlen * features * features + 20 * HEADS * seqlen * seqlen * 128,
            bytes_accessed=attn_w.size * 4 + source.size * 24,
            transcendentals=2 * HEADS * seqlen * seqlen,
        ),
    )(place, source, modulation, attn_w, attn_w_other, qkv, grad_middle, grad_attn, rows)


def run_products(lefts, lefts_other, rights, rights_other, left_at, right_at, count, mine, chunk):
    _, seqlen, features = lefts.shape
    width = rights.shape[-1]
    left_spec = pl.BlockSpec((1, seqlen, features), lambda step: (left_at(step), 0, 0))
    right_spec = pl.BlockSpec((1, seqlen, width), lambda step: (right_at(step), 0, 0))
    specs = [left_spec, left_spec, right_spec, right_spec]
    cost = pl.CostEstimate(
        flops=4 * count * seqlen * features * width,
        bytes_accessed=count * features * width * 6,
        transcendentals=0,
    )
    if chunk % 16:
        total = pl.pallas_call(
            plain_products,
            name="plain_products",
            grid=(count,),
            out_shape=struct((count, features, width), jnp.float32),
            in_specs=specs,
            out_specs=pl.BlockSpec((1, features, width), lambda step: (step, 0, 0)),
            cost_estimate=cost,
        )(lefts, lefts_other, rights, rights_other)
        keep, send = split_bit(
            total.reshape(count, features // (2 * chunk), 2, chunk, width), mine, 2, jnp.bfloat16
        )
        shape = (count, features // 2, width)
        return keep.reshape(shape), send.reshape(shape)
    half_spec = pl.BlockSpec((1, features // 2, width), lambda step: (step, 0, 0))
    return pl.pallas_call(
        functools.partial(pair_products, chunk),
        name="pair_products",
        grid=(count,),
        out_shape=(
            struct((count, features // 2, width), jnp.float32),
            struct((count, features // 2, width), jnp.bfloat16),
        ),
        in_specs=[SMEM] + specs,
        out_specs=(half_spec, half_spec),
        cost_estimate=cost,
    )(mine[None], lefts, lefts_other, rights, rights_other)


def orthogonalize(block_ref, out_ref):
    values = block_ref[...].astype(jnp.float32)
    scaled = (values / (jnp.sqrt(jnp.sum(values * values)) + 1e-07)).astype(jnp.bfloat16)
    for _ in range(NS_ITERS):
        gram = contract(scaled, scaled, 1, 1).astype(jnp.bfloat16)
        square = contract(gram, gram, 1, 0)
        mixed = (COEF_SECOND * gram.astype(jnp.float32) + COEF_THIRD * square).astype(jnp.bfloat16)
        scaled = (
            COEF_FIRST * scaled.astype(jnp.float32) + contract(mixed, scaled, 1, 0)
        ).astype(jnp.bfloat16)
    out_ref[...] = scaled


def run_orthogonalize(block):
    return pl.pallas_call(
        orthogonalize,
        name="orthogonalize",
        out_shape=struct(block.shape, block.dtype),
        in_specs=[VMEM],
        out_specs=VMEM,
        compiler_params=pltpu.CompilerParams(vmem_limit_bytes=24 << 20),
        cost_estimate=pl.CostEstimate(
            flops=6 * NS_ITERS * block.shape[0] ** 3,
            bytes_accessed=4 * block.size,
            transcendentals=0,
        ),
    )(block)


def all_to_all(values):
    return lax.all_to_all(values, "dp", split_axis=0, concat_axis=0, tiled=True)


def to_all(row):
    devices = lax.axis_size("dp")
    return all_to_all(jnp.broadcast_to(row[None], (devices,) + row.shape))


def on_device(latents, conditioning, cotangent, weights, biases, momenta, bias_momenta, counts):
    _, seqlen, features = latents.shape
    block_count, share, _ = weights.shape
    hidden_blocks = (block_count - 10) // 2
    bias_count = biases.shape[0]
    devices = lax.axis_size("dp")
    myself = lax.axis_index("dp")
    core = bit_of(myself, 0)
    bits = index_bits(devices)
    orders = colour_orders(devices)
    ranks = jnp.arange(devices, dtype=jnp.int32)
    live_here = jnp.sum(jnp.where(ranks == myself, counts, 0)) > 0

    lowered = weights.astype(jnp.bfloat16)
    ada_w = lowered[:ADA]
    condition = conditioning[0].astype(jnp.float32)
    silu_cond = jax.nn.silu(condition).astype(jnp.bfloat16)

    half = features // 2
    rest = lowered[ADA:]
    columns_mine = lax.dynamic_slice_in_dim(rest, core * half, half, 2)
    columns_other = lax.dynamic_slice_in_dim(rest, (1 - core) * half, half, 2)
    columns_other = flip(columns_other, 0)
    chip_rows = jnp.where(
        core == 1,
        jnp.concatenate([columns_other, columns_mine], axis=1),
        jnp.concatenate([columns_mine, columns_other], axis=1),
    )
    bounds = [0, 10 - ADA, 10 - ADA + hidden_blocks, block_count - ADA]
    stages = bits - 1
    small_all = to_all(
        jnp.concatenate([silu_cond, biases.astype(jnp.bfloat16).reshape(-1)])
    )

    def modulations(small_all):
        silu_rows = lax.dynamic_slice_in_dim(small_all[:, :features], myself * share, share, 1)
        mod_parts = product("ld,kde->lke", silu_rows, ada_w).reshape(devices, ADA * features)
        return small_all, silu_rows, all_to_all(mod_parts)

    groups, (small_all, silu_rows, mod_sums) = gather_all(
        [chip_rows[low:high] for low, high in zip(bounds[:-1], bounds[1:])],
        [tuple(reversed(order)) for order in orders],
        myself,
        small_all,
        modulations,
    )
    offsets = (
        small_all[:, features:]
        .reshape(devices, bias_count, share)
        .transpose(1, 0, 2)
        .reshape(bias_count, features)
        .astype(jnp.float32)
    )
    modulation = jnp.sum(mod_sums, axis=0).reshape(ADA, features) + offsets[:ADA]
    rows = 2 * share
    held_orders = [tuple(reversed(order)) for order in orders]
    pairs = []
    for index, order in enumerate(held_orders):
        group = groups[index].reshape(devices // 2, -1, rows, half)
        if rows % 16:
            group = jnp.stack([group[place] for place in chunk_places(order)], axis=1)
            group = group.reshape(1, -1, features, half)
            held_orders[index] = ()
        pairs.append((group, flip(group, 0)))
    attn_ws, up_ws, down_ws = pairs

    place = jnp.stack([core, live_here.astype(jnp.int32)]).astype(jnp.int32)
    lefts, qkv, attn_out, middle = run_attention_forward(
        held_orders[0], place, latents[0], modulation, offsets, *attn_ws
    )
    lefts_other = flip(lefts, 0)
    output, hidden, mlp_keep, mlp_send, grad_middle, grad_attn, rows = run_mlp(
        held_orders[1:], place, lefts, middle, attn_out, cotangent[0], modulation, offsets, up_ws, down_ws
    )
    hidden_other = flip(hidden, 0)
    mlp_other = flip(mlp_send, 0)

    def spread(mats, count):
        return mats.reshape((mats.shape[0],) + (2,) * count + (2 * share, half))

    def products(left, left_other, right, right_other, left_at, right_at, count, order):
        return run_products(
            left,
            left_other,
            right,
            right_other,
            left_at,
            right_at,
            count,
            bit_of(myself, order[0]),
            share << order[0],
        )

    down_halves = products(
        hidden, hidden_other, mlp_keep, mlp_other, lambda b: b, lambda b: 0, hidden_blocks, orders[0]
    )
    up_halves = products(
        lefts, lefts_other, mlp_keep, mlp_other, lambda b: 2, lambda b: b + 1, hidden_blocks, orders[1]
    )
    input_grad, attn_keep, attn_send, grad_offsets = run_attention_backward(
        held_orders[0], place, latents[0], modulation, *attn_ws, qkv, grad_middle, grad_attn, rows
    )
    attn_other = flip(attn_send, 0)
    attn_halves = products(
        lefts, lefts_other, attn_keep, attn_other, lambda b: b // 3, lambda b: b, 4, orders[2]
    )

    grad_mod_b = grad_offsets[:ADA].astype(jnp.bfloat16).reshape(-1)
    by_holder = (
        grad_offsets.reshape(bias_count, devices, share)
        .transpose(1, 0, 2)
        .reshape(devices, bias_count * share)
    )
    coarse = lax.reduce_precision(by_holder, 8, 7)
    mod_and_offsets = jnp.concatenate(
        [
            jnp.broadcast_to(grad_mod_b[None], (devices, ADA * features)),
            coarse.astype(jnp.bfloat16),
            (by_holder - coarse).astype(jnp.bfloat16),
        ],
        axis=1,
    )
    mod_and_offsets = all_to_all(mod_and_offsets)

    def conditioning_grads(mod_and_offsets):
        mod_all = mod_and_offsets[:, : ADA * features].reshape(devices, ADA, features)
        silu_parts = product("lke,kde->ld", mod_all, ada_w)
        return mod_and_offsets, mod_all, all_to_all(silu_parts)

    sums, (mod_and_offsets, mod_all, grad_silu) = scatter_all(
        [attn_halves, up_halves, down_halves],
        [orders[2], orders[1], orders[0]],
        myself,
        1,
        spread,
        {stages - 1: lambda _: conditioning_grads(mod_and_offsets)},
    )
    chip_rows = jnp.concatenate(sums, axis=0)
    rows_mine = lax.dynamic_slice_in_dim(chip_rows, core * share, share, 1)
    rows_other = flip(lax.dynamic_slice_in_dim(chip_rows, (1 - core) * share, share, 1), 0)
    rest_share = jnp.where(
        core == 1,
        jnp.concatenate([rows_other, rows_mine], axis=2),
        jnp.concatenate([rows_mine, rows_other], axis=2),
    )

    ada_share = product("ld,lke->kde", silu_rows, mod_all)
    offset_share = jnp.sum(
        mod_and_offsets[:, ADA * features :]
        .astype(jnp.float32)
        .reshape(devices * 2, bias_count, share),
        axis=0,
    )

    grad_scale = lax.rsqrt((seqlen * jnp.sum(counts)).astype(jnp.float32))
    weight_grads = jnp.concatenate([ada_share, rest_share], axis=0) * grad_scale
    bias_grads = offset_share * grad_scale
    new_momenta = BETA_WEIGHT * momenta + weight_grads
    new_bias_momenta = BETA_BIAS * bias_momenta + bias_grads
    new_biases = biases - RATE_BIAS * new_bias_momenta

    outgoing = jnp.pad(
        new_momenta.astype(jnp.bfloat16), ((0, devices - block_count), (0, 0), (0, 0))
    )
    ortho = run_orthogonalize(all_to_all(outgoing).reshape(features, features))
    ortho_local = all_to_all(ortho.reshape(devices, share, features))[:block_count]
    silu_back = jax.vjp(jax.nn.silu, condition)[1]
    cond_grad = silu_back(grad_silu.reshape(features))[0] * seqlen ** (-0.5)
    new_weights = weights - RATE_WEIGHT * ortho_local.astype(jnp.float32)
    cond_grad = jnp.where(live_here, cond_grad, jnp.zeros_like(cond_grad))[None]
    return (
        output[None],
        input_grad[None],
        cond_grad,
        weight_grads,
        bias_grads,
        new_weights,
        new_momenta,
        new_biases,
        new_bias_momenta,
    )


def solution(mesh):
    return jax.shard_map(
        on_device,
        mesh=mesh,
        in_specs=(
            P("dp", None, None),
            P("dp", None),
            P("dp", None, None),
            P(None, "dp", None),
            P(None, "dp"),
            P(None, "dp", None),
            P(None, "dp"),
            P(),
        ),
        out_specs=(
            P("dp", None, None),
            P("dp", None, None),
            P("dp", None),
            P(None, "dp", None),
            P(None, "dp"),
            P(None, "dp", None),
            P(None, "dp", None),
            P(None, "dp"),
            P(None, "dp"),
        ),
        check_vma=False,
    )
```

profile of v0, /device:TPU:0, one launch (start us, length us, event | category | flops | bytes accessed | tf_op | source)
XLA Modules:
  0.0 358.4 jit_solution(3035588416390896447)
XLA Ops:
  4.8 3.9 %collective-permute-start.10 = (bf16[4,48,384]{2,1,0:T(8,128)(2,1)S(1)}, bf16[4,48,384]{2,1,0:T(8,128)(2,1)S(1)}, u32[]{:S(2)}, u32[]{:S(2)}) collective-permute-start(bf16[4,48,384]{2,1,0:T(8,128)(2,1)S(1)} %get-tuple-element.87), channel_id=1, source_target_pairs={{0,16},{1,17},{2,18},{3,19},{4,20},{5,21},{6,22},{7,23},{8,24},{9,... | collective-permute-start | bytes 442376 | tf_op jit(solution)/shard_map/ppermute | solution.py:32
  11.2 3.8 %all-to-all-start = ((bf16[32,2,552]{2,1,0:T(2,128)(2,1)}), bf16[32,2,552]{2,1,0:T(2,128)(2,1)S(1)}, u32[]{:S(2)}, u32[]{:S(2)}) async-start(bf16[32,2,552]{2,1,0:T(2,128)(2,1)} %reshape.1007), calls=%async_computation | async-start | bytes 163840 | tf_op jit(solution)/shard_map/all_to_all | solution.py:556
  15.1 7.6 %all-to-all-done = bf16[32,2,552]{2,1,0:T(2,128)(2,1)S(1)} async-done(((bf16[32,2,552]{2,1,0:T(2,128)(2,1)}), bf16[32,2,552]{2,1,0:T(2,128)(2,1)S(1)}, u32[]{:S(2)}, u32[]{:S(2)}) %all-to-all-start) | async-done | bytes 70688 | tf_op jit(solution)/shard_map/all_to_all | solution.py:556
  23.8 2.2 collective-permute-start.5
  27.3 8.3 %collective-permute-done.1 = bf16[4,48,384]{2,1,0:T(8,128)(2,1)S(1)} collective-permute-done((bf16[4,48,384]{2,1,0:T(8,128)(2,1)S(1)}, bf16[4,48,384]{2,1,0:T(8,128)(2,1)S(1)}, u32[]{:S(2)}, u32[]{:S(2)}) %collective-permute-start.1) | collective-permute-done | bytes 147488 | tf_op jit(solution)/shard_map/ppermute | solution.py:32
  42.0 3.6 %all-to-all-start.1 = ((f32[32,1,4608]{2,1,0:T(1,128)}), f32[32,1,4608]{2,1,0:T(1,128)S(1)}, u32[]{:S(2)}, u32[]{:S(2)}) async-start(f32[32,1,4608]{2,1,0:T(1,128)} %all_to_all.49), calls=%async_computation.1 | async-start | bytes 1179648 | tf_op jit(solution)/shard_map/all_to_all | solution.py:556
  45.7 1.9 collective-permute-start.12
  47.8 1.5 collective-permute-start.3
  49.4 1.5 collective-permute-start.7
  51.3 19.3 %collective-permute-done.12 = bf16[2,2,4,48,384]{4,3,2,1,0:T(8,128)(2,1)S(1)} collective-permute-done((bf16[2,2,4,48,384]{4,3,2,1,0:T(8,128)(2,1)S(1)}, bf16[2,2,4,48,384]{4,3,2,1,0:T(8,128)(2,1)S(1)}, u32[]{:S(2)}, u32[]{:S(2)}) %collective-permute-start.12) | collective-permute-done | bytes 589856 | tf_op jit(solution)/shard_map/ppermute | solution.py:32
  81.6 18.1 %collective-permute-done.13 = bf16[2,2,2,4,48,384]{5,4,3,2,1,0:T(8,128)(2,1)} collective-permute-done((bf16[2,2,2,4,48,384]{5,4,3,2,1,0:T(8,128)(2,1)}, bf16[2,2,2,4,48,384]{5,4,3,2,1,0:T(8,128)(2,1)}, u32[]{:S(2)}, u32[]{:S(2)}) %collective-permute-start.13) | collective-permute-done | bytes 1179680 | tf_op jit(solution)/shard_map/ppermute | solution.py:32
  99.8 2.1 maximum_select_fusion.1
  103.5 3.4 maximum_select_fusion
  106.9 3.5 maximum_select_fusion.2
  116.3 6.9 %attention_forward.1 = (bf16[3,256,768]{2,1,0:T(8,128)(2,1)}, bf16[3,256,768]{2,1,0:T(8,128)(2,1)S(1)}, f32[256,768]{1,0:T(8,128)S(1)}, f32[256,768]{1,0:T(8,128)S(1)}) custom-call(s32[2]{0:T(128)S(1)} %pad_add_fusion.place_ref, bf16[256,768]{1,0:T(8,128)(2,1)S(1)} %bitcast.130, f32[6,768]{1,0:T(8,128)S(1)} %add.117.mod_ref, ...), custom_call_target="tpu_custom_call" | custom-call | flops 2013265920 | bytes 8650752 | tf_op jit(solution)/shard_map/attention_forward/pallas_call | solution.py:385
  123.2 11.2 %mlp_both_ways.1 = (bf16[256,768]{1,0:T(8,128)(2,1)}, bf16[4,256,768]{2,1,0:T(8,128)(2,1)}, bf16[5,256,384]{2,1,0:T(8,128)(2,1)S(1)}, bf16[5,256,384]{2,1,0:T(8,...) custom-call(s32[2]{0:T(128)S(1)} %pad_add_fusion.place_ref, ...), custom_call_target="tpu_custom_call" | custom-call | flops 4831838208 | bytes 17301504 | tf_op jit(solution)/shard_map/mlp_both_ways/pallas_call | solution.py:410
  134.4 11.9 %attention_backward.1 = (f32[256,768]{1,0:T(8,128)}, bf16[4,256,384]{2,1,0:T(8,128)(2,1)S(1)}, bf16[4,256,384]{2,1,0:T(8,128)(2,1)S(1)}, f32[14,768]{1,0:T(8,128)S(1)}) custom-call(s32[2]{0:T(128)S(1)} %pad_add_fusion.place_ref, bf16[256,768]{1,0:T(8,128)(2,1)S(1)} %bitcast.131, f32[6,768]{1,0:T(8,128)S(1)} %add.117.mod_ref, ...), custom_call_target="tpu_custom_call" | custom-call | flops 3221225472 | bytes 9437184 | tf_op jit(solution)/shard_map/attention_backward/pallas_call | solution.py:461
  149.0 1.8 copy.56
  152.0 5.6 %pair_products.4 = (f32[4,384,384]{2,1,0:T(8,128)}, bf16[4,384,384]{2,1,0:T(8,128)(2,1)}) custom-call(s32[1]{0:T(128)} %bitcast.60.mine_ref, bf16[3,256,768]{2,1,0:T(8,128)(2,1)} %get-tuple-element.44.lefts_ref.left_ref, bf16[3,256,768]{2,1,0:T(8,128)(2,1)} %collective-permute-done.22.left_other_ref, bf16[4,256,384]{2,1,0:T(8,128)(2,1)} %copy-done.4, ...), custom_call_target="tpu_custom_call" | custom-call | flops 1207959552 | bytes 7077888 | tf_op jit(solution)/shard_map/pair_products/pallas_call | solution.py:512
  157.6 1.5 collective-permute-start.24
  161.1 4.1 %all-to-all-start.2 = ((bf16[32,2,2640]{2,1,0:T(2,128)(2,1)}), bf16[32,2,2640]{2,1,0:T(2,128)(2,1)}, u32[]{:S(2)}, u32[]{:S(2)}) async-start(bf16[32,2,2640]{2,1,0:T(2,128)(2,1)} %reshape.1009), calls=%async_computation.2 | async-start | bytes 688128 | tf_op jit(solution)/shard_map/all_to_all | solution.py:556
  165.2 5.5 %pair_products.5 = (f32[4,384,384]{2,1,0:T(8,128)}, bf16[4,384,384]{2,1,0:T(8,128)(2,1)}) custom-call(s32[1]{0:T(128)} %bitcast.68.mine_ref, bf16[3,256,768]{2,1,0:T(8,128)(2,1)} %get-tuple-element.44.lefts_ref.left_ref, bf16[3,256,768]{2,1,0:T(8,128)(2,1)} %collective-permute-done.22.left_other_ref, bf16[5,256,384]{2,1,0:T(8,128)(2,1)} %copy-done, ...), custom_call_target="tpu_custom_call" | custom-call | flops 1207959552 | bytes 7077888 | tf_op jit(solution)/shard_map/pair_products/pallas_call | solution.py:512
  170.7 1.7 collective-permute-start.28
  172.4 20.8 %all-to-all-done.2 = bf16[32,2,2640]{2,1,0:T(2,128)(2,1)} async-done(((bf16[32,2,2640]{2,1,0:T(2,128)(2,1)}), bf16[32,2,2640]{2,1,0:T(2,128)(2,1)}, u32[]{:S(2)}, u32[]{:S(2)}) %all-to-all-start.2) | async-done | bytes 337952 | tf_op jit(solution)/shard_map/all_to_all | solution.py:556
  193.2 2.7 reshape.1010
  197.6 5.6 %pair_products.3 = (f32[4,384,384]{2,1,0:T(8,128)}, bf16[4,384,384]{2,1,0:T(8,128)(2,1)}) custom-call(s32[1]{0:T(128)} %bitcast.46.mine_ref, bf16[4,256,768]{2,1,0:T(8,128)(2,1)} %get-tuple-element.54.left_ref, bf16[4,256,768]{2,1,0:T(8,128)(2,1)} %copy-done.13, bf16[5,256,384]{2,1,0:T(8,128)(2,1)} %copy-done, ...), custom_call_target="tpu_custom_call" | custom-call | flops 1207959552 | bytes 7077888 | tf_op jit(solution)/shard_map/pair_products/pallas_call | solution.py:512
  203.2 1.5 collective-permute-start.18
  204.7 1.7 fusion.6
  206.5 3.6 all-to-all-start.3
  210.1 1.6 convert_add_fusion.1
  211.8 1.9 collective-permute-start.25
  213.7 1.7 convert_add_fusion
  215.5 1.5 collective-permute-start.29
  217.0 15.5 %collective-permute-done.18 = bf16[4,384,384]{2,1,0:T(8,128)(2,1)} collective-permute-done((bf16[4,384,384]{2,1,0:T(8,128)(2,1)}, bf16[4,384,384]{2,1,0:T(8,128)(2,1)}, u32[]{:S(2)}, u32[]{:S(2)}) %collective-permute-start.18) | collective-permute-done | bytes 1179680 | tf_op jit(solution)/shard_map/ppermute | solution.py:32
  232.5 1.5 convert_add_fusion.2
  234.1 1.9 collective-permute-start.19
  236.0 8.9 %collective-permute-done.25 = bf16[4,2,2,48,384]{4,3,0,1,2:T(8,128)(2,1)S(1)} collective-permute-done((bf16[4,2,2,48,384]{4,3,0,1,2:T(8,128)(2,1)S(1)}, bf16[4,2,2,48,384]{4,3,0,1,2:T(8,128)(2,1)S(1)}, u32[]{:S(2)}, u32[]{:S(2)}) %collective-permute-start.25) | collective-permute-done | bytes 589856 | tf_op jit(solution)/shard_map/ppermute | solution.py:32
  245.7 1.6 collective-permute-start.30
  247.3 8.2 %collective-permute-done.26 = bf16[4,2,48,384]{3,2,0,1:T(8,128)(2,1)S(1)} collective-permute-done((bf16[4,2,48,384]{3,2,0,1:T(8,128)(2,1)S(1)}, bf16[4,2,48,384]{3,2,0,1:T(8,128)(2,1)S(1)}, u32[]{:S(2)}, u32[]{:S(2)}) %collective-permute-start.26) | collective-permute-done | bytes 294944 | tf_op jit(solution)/shard_map/ppermute | solution.py:32
  257.4 1.6 collective-permute-start.31
  259.0 4.7 %collective-permute-done.27 = bf16[4,48,384]{2,1,0:T(8,128)(2,1)S(1)} collective-permute-done((bf16[4,48,384]{2,1,0:T(8,128)(2,1)S(1)}, bf16[4,48,384]{2,1,0:T(8,128)(2,1)S(1)}, u32[]{:S(2)}, u32[]{:S(2)}) %collective-permute-start.27) | collective-permute-done | bytes 147488 | tf_op jit(solution)/shard_map/ppermute | solution.py:32
  263.8 6.3 %collective-permute-done.20 = bf16[4,2,48,384]{3,2,0,1:T(8,128)(2,1)S(1)} collective-permute-done((bf16[4,2,48,384]{3,2,0,1:T(8,128)(2,1)S(1)}, bf16[4,2,48,384]{3,2,0,1:T(8,128)(2,1)S(1)}, u32[]{:S(2)}, u32[]{:S(2)}) %collective-permute-start.20) | collective-permute-done | bytes 294944 | tf_op jit(solution)/shard_map/ppermute | solution.py:32
  270.3 7.4 %collective-permute-done.21 = bf16[4,48,384]{2,1,0:T(8,128)(2,1)S(1)} collective-permute-done((bf16[4,48,384]{2,1,0:T(8,128)(2,1)S(1)}, bf16[4,48,384]{2,1,0:T(8,128)(2,1)S(1)}, u32[]{:S(2)}, u32[]{:S(2)}) %collective-permute-start.21) | collective-permute-done | bytes 147488 | tf_op jit(solution)/shard_map/ppermute | solution.py:32
  281.2 1.8 fusion.26
  283.0 34.5 %all_to_all.56 = bf16[32,24,768]{2,1,0:T(8,128)(2,1)S(1)} all-to-all(bf16[32,24,768]{2,1,0:T(8,128)(2,1)S(1)} %pad.4), channel_id=1, replica_groups=mesh['dp'=32] {'dp'}, dimensions={0} | all-to-all | bytes 2359296 | tf_op jit(solution)/shard_map/all_to_all | solution.py:556
  317.5 7.7 %orthogonalize.1 = bf16[768,768]{1,0:T(8,128)(2,1)} custom-call(bf16[768,768]{1,0:T(8,128)(2,1)S(1)} %bitcast.128), custom_call_target="tpu_custom_call" | custom-call | flops 5435817984 | bytes 2359296 | tf_op jit(solution)/shard_map/orthogonalize/pallas_call | solution.py:540
  325.2 2.8 all-to-all-start.5
  329.8 27.2 %all-to-all-done.5 = bf16[32,24,768]{2,1,0:T(8,128)(2,1)S(1)} async-done(((bf16[32,24,768]{2,1,0:T(8,128)(2,1)}), bf16[32,24,768]{2,1,0:T(8,128)(2,1)S(1)}, u32[]{:S(2)}, u32[]{:S(2)}) %all-to-all-start.5) | async-done | bytes 1179680 | tf_op jit(solution)/shard_map/all_to_all | solution.py:556
  (188 shorter events, 49.9 us)
Async XLA Ops:
  2.0 35.6 %copy-start.8 = (bf16[18,24,768]{2,1,0:T(8,128)(2,1)}, bf16[18,24,768]{2,1,0:T(8,128)(2,1)S(1)}, u32[]{:S(2)}) copy-start(bf16[18,24,768]{2,1,0:T(8,128)(2,1)S(1)} %convert_element_type.137) | copy-start | bytes 1990660
  2.2 1.7 collective-permute-start
  4.8 21.2 %collective-permute-start.10 = (bf16[4,48,384]{2,1,0:T(8,128)(2,1)S(1)}, bf16[4,48,384]{2,1,0:T(8,128)(2,1)S(1)}, u32[]{:S(2)}, u32[]{:S(2)}) collective-permute-start(bf16[4,48,384]{2,1,0:T(8,128)(2,1)S(1)} %get-tuple-element.87), channel_id=1, source_target_pairs={{0,16},{1,17},{2,18},{3,19},{4,20},{5,21},{6,22},{7,23},{8,24},{9,... | collective-permute-start | bytes 442376 | tf_op jit(solution)/shard_map/ppermute | solution.py:32
  11.2 11.4 %all-to-all-start = ((bf16[32,2,552]{2,1,0:T(2,128)(2,1)}), bf16[32,2,552]{2,1,0:T(2,128)(2,1)S(1)}, u32[]{:S(2)}, u32[]{:S(2)}) async-start(bf16[32,2,552]{2,1,0:T(2,128)(2,1)} %reshape.1007), calls=%async_computation | async-start | bytes 163840 | tf_op jit(solution)/shard_map/all_to_all | solution.py:556
  23.0 14.9 %copy-start.16 = (bf16[32,1,1104]{0,2,1:T(8,128)(2,1)}, bf16[32,1,1104]{0,2,1:T(8,128)(2,1)S(1)}, u32[]{:S(2)}) copy-start(bf16[32,1,1104]{0,2,1:T(8,128)(2,1)S(1)} %copy.50) | copy-start | bytes 211972
  23.0 12.5 %collective-permute-start.1 = (bf16[4,48,384]{2,1,0:T(8,128)(2,1)S(1)}, bf16[4,48,384]{2,1,0:T(8,128)(2,1)S(1)}, u32[]{:S(2)}, u32[]{:S(2)}) collective-permute-start(bf16[4,48,384]{2,1,0:T(8,128)(2,1)S(1)} %get-tuple-element.89), channel_id=1, source_target_pairs={{0,16},{1,17},{2,18},{3,19},{4,20},{5,21},{6,22},{7,23},{8,24},{9,... | collective-permute-start | bytes 442376 | tf_op jit(solution)/shard_map/ppermute | solution.py:32
  23.8 14.8 %collective-permute-start.5 = (bf16[4,48,384]{2,1,0:T(8,128)(2,1)}, bf16[4,48,384]{2,1,0:T(8,128)(2,1)S(1)}, u32[]{:S(2)}, u32[]{:S(2)}) collective-permute-start(bf16[4,48,384]{2,1,0:T(8,128)(2,1)} %get-tuple-element.88), channel_id=1, source_target_pairs={{0,16},{1,17},{2,18},{3,19},{4,20},{5,21},{6,22},{7,23},{8,24},{9,... | collective-permute-start | bytes 442376 | tf_op jit(solution)/shard_map/ppermute | solution.py:32
  26.8 18.8 %collective-permute-start.11 = (bf16[2,4,48,384]{3,2,1,0:T(8,128)(2,1)}, bf16[2,4,48,384]{3,2,1,0:T(8,128)(2,1)S(1)}, u32[]{:S(2)}, u32[]{:S(2)}) collective-permute-start(bf16[2,4,48,384]{3,2,1,0:T(8,128)(2,1)} %maximum_select_fusion.21), channel_id=1, source_target_pairs={{0,2},{1,3},{2,0},{3,1},{4,6},{5,7},{6,4},{7,5},{8,10},{9,11},{10,... | collective-permute-start | bytes 884744 | tf_op jit(solution)/shard_map/ppermute | solution.py:32
  36.3 11.4 %collective-permute-start.2 = (bf16[2,4,48,384]{3,2,1,0:T(8,128)(2,1)}, bf16[2,4,48,384]{3,2,1,0:T(8,128)(2,1)S(1)}, u32[]{:S(2)}, u32[]{:S(2)}) collective-permute-start(bf16[2,4,48,384]{3,2,1,0:T(8,128)(2,1)} %maximum_select_fusion.17), channel_id=1, source_target_pairs={{0,4},{1,5},{2,6},{3,7},{4,0},{5,1},{6,2},{7,3},{8,12},{9,13},{10,... | collective-permute-start | bytes 884744 | tf_op jit(solution)/shard_map/ppermute | solution.py:32
  39.4 9.9 %collective-permute-start.6 = (bf16[2,4,48,384]{3,2,1,0:T(8,128)(2,1)}, bf16[2,4,48,384]{3,2,1,0:T(8,128)(2,1)S(1)}, u32[]{:S(2)}, u32[]{:S(2)}) collective-permute-start(bf16[2,4,48,384]{3,2,1,0:T(8,128)(2,1)} %maximum_select_fusion.19), channel_id=1, source_target_pairs={{0,8},{1,9},{2,10},{3,11},{4,12},{5,13},{6,14},{7,15},{8,0},{9,1},... | collective-permute-start | bytes 884744 | tf_op jit(solution)/shard_map/ppermute | solution.py:32
  42.0 38.8 %all-to-all-start.1 = ((f32[32,1,4608]{2,1,0:T(1,128)}), f32[32,1,4608]{2,1,0:T(1,128)S(1)}, u32[]{:S(2)}, u32[]{:S(2)}) async-start(f32[32,1,4608]{2,1,0:T(1,128)} %all_to_all.49), calls=%async_computation.1 | async-start | bytes 1179648 | tf_op jit(solution)/shard_map/all_to_all | solution.py:556
  45.7 24.9 %collective-permute-start.12 = (bf16[2,2,4,48,384]{4,3,2,1,0:T(8,128)(2,1)S(1)}, bf16[2,2,4,48,384]{4,3,2,1,0:T(8,128)(2,1)S(1)}, u32[]{:S(2)}, u32[]{:S(2)}) collective-permute-start(bf16[2,2,4,48,384]{4,3,2,1,0:T(8,128)(2,1)S(1)} %maximum_select_fusion.14), channel_id=1, source_target_pairs={{0,8},{1,9},{2,10},{3,11},{4,12},{5,13},{6,14},{7,15},{8,0},{9,1},... | collective-permute-start | bytes 1769480 | tf_op jit(solution)/shard_map/ppermute | solution.py:32
  47.8 25.5 %collective-permute-start.3 = (bf16[2,2,4,48,384]{4,3,2,1,0:T(8,128)(2,1)S(1)}, bf16[2,2,4,48,384]{4,3,2,1,0:T(8,128)(2,1)S(1)}, u32[]{:S(2)}, u32[]{:S(2)}) collective-permute-start(bf16[2,2,4,48,384]{4,3,2,1,0:T(8,128)(2,1)S(1)} %maximum_select_fusion.10), channel_id=1, source_target_pairs={{0,2},{1,3},{2,0},{3,1},{4,6},{5,7},{6,4},{7,5},{8,10},{9,11},{10,... | collective-permute-start | bytes 1769480 | tf_op jit(solution)/shard_map/ppermute | solution.py:32
  49.4 25.7 %collective-permute-start.7 = (bf16[2,2,4,48,384]{4,3,2,1,0:T(8,128)(2,1)S(1)}, bf16[2,2,4,48,384]{4,3,2,1,0:T(8,128)(2,1)S(1)}, u32[]{:S(2)}, u32[]{:S(2)}) collective-permute-start(bf16[2,2,4,48,384]{4,3,2,1,0:T(8,128)(2,1)S(1)} %maximum_select_fusion.12), channel_id=1, source_target_pairs={{0,4},{1,5},{2,6},{3,7},{4,0},{5,1},{6,2},{7,3},{8,12},{9,13},{10,... | collective-permute-start | bytes 1769480 | tf_op jit(solution)/shard_map/ppermute | solution.py:32
  71.9 27.9 %collective-permute-start.13 = (bf16[2,2,2,4,48,384]{5,4,3,2,1,0:T(8,128)(2,1)}, bf16[2,2,2,4,48,384]{5,4,3,2,1,0:T(8,128)(2,1)}, u32[]{:S(2)}, u32[]{:S(2)}) collective-permute-start(bf16[2,2,2,4,48,384]{5,4,3,2,1,0:T(8,128)(2,1)} %maximum_select_fusion.6), channel_id=1, source_target_pairs={{0,4},{1,5},{2,6},{3,7},{4,0},{5,1},{6,2},{7,3},{8,12},{9,13},{10,... | collective-permute-start | bytes 3538952 | tf_op jit(solution)/shard_map/ppermute | solution.py:32
  74.5 27.5 %collective-permute-start.4 = (bf16[2,2,2,4,48,384]{5,4,3,2,1,0:T(8,128)(2,1)}, bf16[2,2,2,4,48,384]{5,4,3,2,1,0:T(8,128)(2,1)}, u32[]{:S(2)}, u32[]{:S(2)}) collective-permute-start(bf16[2,2,2,4,48,384]{5,4,3,2,1,0:T(8,128)(2,1)} %maximum_select_fusion.3), channel_id=1, source_target_pairs={{0,8},{1,9},{2,10},{3,11},{4,12},{5,13},{6,14},{7,15},{8,0},{9,1},... | collective-permute-start | bytes 3538952 | tf_op jit(solution)/shard_map/ppermute | solution.py:32
  76.3 27.2 %collective-permute-start.8 = (bf16[2,2,2,4,48,384]{5,4,3,2,1,0:T(8,128)(2,1)}, bf16[2,2,2,4,48,384]{5,4,3,2,1,0:T(8,128)(2,1)}, u32[]{:S(2)}, u32[]{:S(2)}) collective-permute-start(bf16[2,2,2,4,48,384]{5,4,3,2,1,0:T(8,128)(2,1)} %maximum_select_fusion.4), channel_id=1, source_target_pairs={{0,2},{1,3},{2,0},{3,1},{4,6},{5,7},{6,4},{7,5},{8,10},{9,11},{10,... | collective-permute-start | bytes 3538952 | tf_op jit(solution)/shard_map/ppermute | solution.py:32
  80.8 19.0 %copy-start.7 = (bf16[1,2,2,2,4,48,384]{6,5,4,3,2,1,0:T(8,128)(2,1)S(1)}, bf16[1,2,2,2,4,48,384]{6,5,4,3,2,1,0:T(8,128)(2,1)}, u32[]{:S(2)}) copy-start(bf16[1,2,2,2,4,48,384]{6,5,4,3,2,1,0:T(8,128)(2,1)} %maximum_select_fusion.7) | copy-start | bytes 3538948
  101.9 21.2 %collective-permute-start.14 = (bf16[16,4,48,384]{3,2,1,0:T(8,128)(2,1)S(1)}, bf16[16,4,48,384]{3,2,1,0:T(8,128)(2,1)}, u32[]{:S(2)}, u32[]{:S(2)}) collective-permute-start(bf16[16,4,48,384]{3,2,1,0:T(8,128)(2,1)S(1)} %bitcast.126), channel_id=1, source_target_pairs={{0,1},{1,0},{2,3},{3,2},{4,5},{5,4},{6,7},{7,6},{8,9},{9,8},{10,11... | collective-permute-start | bytes 7077896 | tf_op jit(solution)/shard_map/ppermute | solution.py:32
  106.9 9.3 %collective-permute-start.9 = (bf16[16,4,48,384]{3,2,1,0:T(8,128)(2,1)}, bf16[16,4,48,384]{3,2,1,0:T(8,128)(2,1)}, u32[]{:S(2)}, u32[]{:S(2)}) collective-permute-start(bf16[16,4,48,384]{3,2,1,0:T(8,128)(2,1)} %bitcast.26.mine_ref), channel_id=1, source_target_pairs={{0,1},{1,0},{2,3},{3,2},{4,5},{5,4},{6,7},{7,6},{8,9},{9,8},{10,11... | collective-permute-start | bytes 7077896 | tf_op jit(solution)/shard_map/ppermute | solution.py:32
  110.5 5.8 %copy-start.2 = (bf16[1,256,768]{2,1,0:T(8,128)(2,1)S(1)}, bf16[1,256,768]{2,1,0:T(8,128)(2,1)}, u32[]{:S(2)}) copy-start(bf16[1,256,768]{2,1,0:T(8,128)(2,1)} %param.8) | copy-start | bytes 1179652
  110.5 12.7 %collective-permute-start.15 = (bf16[16,4,48,384]{3,2,1,0:T(8,128)(2,1)}, bf16[16,4,48,384]{3,2,1,0:T(8,128)(2,1)}, u32[]{:S(2)}, u32[]{:S(2)}) collective-permute-start(bf16[16,4,48,384]{3,2,1,0:T(8,128)(2,1)} %bitcast.43.down_ref), channel_id=1, source_target_pairs={{0,1},{1,0},{2,3},{3,2},{4,5},{5,4},{6,7},{7,6},{8,9},{9,8},{10,11... | collective-permute-start | bytes 7077896 | tf_op jit(solution)/shard_map/ppermute | solution.py:32
  116.3 6.9 %copy-start.1 = (bf16[1,256,768]{2,1,0:T(8,128)(2,1)S(1)}, bf16[1,256,768]{2,1,0:T(8,128)(2,1)}, u32[]{:S(2)}) copy-start(bf16[1,256,768]{2,1,0:T(8,128)(2,1)} %param.10) | copy-start | bytes 1179652
  123.2 28.8 %collective-permute-start.22 = (bf16[3,256,768]{2,1,0:T(8,128)(2,1)}, bf16[3,256,768]{2,1,0:T(8,128)(2,1)}, u32[]{:S(2)}, u32[]{:S(2)}) collective-permute-start(bf16[3,256,768]{2,1,0:T(8,128)(2,1)} %get-tuple-element.44.lefts_ref.left_ref), channel_id=1, source_target_pairs={{0,1},{1,0},{2,3},{3,2},{4,5},{5,4},{6,7},{7,6},{8,9},{9,8},{10,11... | collective-permute-start | bytes 3538952 | tf_op jit(solution)/shard_map/ppermute | solution.py:32
  123.2 11.2 %copy-start.3 = (bf16[1,256,768]{2,1,0:T(8,128)(2,1)S(1)}, bf16[1,256,768]{2,1,0:T(8,128)(2,1)}, u32[]{:S(2)}) copy-start(bf16[1,256,768]{2,1,0:T(8,128)(2,1)} %param.8) | copy-start | bytes 1179652
  134.4 11.9 %copy-start = (bf16[5,256,384]{2,1,0:T(8,128)(2,1)}, bf16[5,256,384]{2,1,0:T(8,128)(2,1)S(1)}, u32[]{:S(2)}) copy-start(bf16[5,256,384]{2,1,0:T(8,128)(2,1)S(1)} %get-tuple-element.55.right_ref) | copy-start | bytes 2949124
  147.2 4.8 %collective-permute-start.23 = (bf16[4,256,384]{2,1,0:T(8,128)(2,1)S(1)}, bf16[4,256,384]{2,1,0:T(8,128)(2,1)}, u32[]{:S(2)}, u32[]{:S(2)}) collective-permute-start(bf16[4,256,384]{2,1,0:T(8,128)(2,1)S(1)} %get-tuple-element.64), channel_id=1, source_target_pairs={{0,1},{1,0},{2,3},{3,2},{4,5},{5,4},{6,7},{7,6},{8,9},{9,8},{10,11... | collective-permute-start | bytes 2359304 | tf_op jit(solution)/shard_map/ppermute | solution.py:32
  147.7 48.7 %collective-permute-start.16 = (bf16[4,256,768]{2,1,0:T(8,128)(2,1)}, bf16[4,256,768]{2,1,0:T(8,128)(2,1)S(1)}, u32[]{:S(2)}, u32[]{:S(2)}) collective-permute-start(bf16[4,256,768]{2,1,0:T(8,128)(2,1)} %get-tuple-element.54.left_ref), channel_id=1, source_target_pairs={{0,1},{1,0},{2,3},{3,2},{4,5},{5,4},{6,7},{7,6},{8,9},{9,8},{10,11... | collective-permute-start | bytes 4718600 | tf_op jit(solution)/shard_map/ppermute | solution.py:32
  147.7 17.5 %collective-permute-start.17 = (bf16[5,256,384]{2,1,0:T(8,128)(2,1)S(1)}, bf16[5,256,384]{2,1,0:T(8,128)(2,1)}, u32[]{:S(2)}, u32[]{:S(2)}) collective-permute-start(bf16[5,256,384]{2,1,0:T(8,128)(2,1)S(1)} %get-tuple-element.56), channel_id=1, source_target_pairs={{0,1},{1,0},{2,3},{3,2},{4,5},{5,4},{6,7},{7,6},{8,9},{9,8},{10,11... | collective-permute-start | bytes 2949128 | tf_op jit(solution)/shard_map/ppermute | solution.py:32
  157.6 52.5 %collective-permute-start.24 = (bf16[4,384,384]{2,1,0:T(8,128)(2,1)}, bf16[4,384,384]{2,1,0:T(8,128)(2,1)}, u32[]{:S(2)}, u32[]{:S(2)}) collective-permute-start(bf16[4,384,384]{2,1,0:T(8,128)(2,1)} %get-tuple-element.66), channel_id=1, source_target_pairs={{0,8},{1,9},{2,10},{3,11},{4,12},{5,13},{6,14},{7,15},{8,0},{9,1},... | collective-permute-start | bytes 3538952 | tf_op jit(solution)/shard_map/ppermute | solution.py:32
  161.1 32.1 %all-to-all-start.2 = ((bf16[32,2,2640]{2,1,0:T(2,128)(2,1)}), bf16[32,2,2640]{2,1,0:T(2,128)(2,1)}, u32[]{:S(2)}, u32[]{:S(2)}) async-start(bf16[32,2,2640]{2,1,0:T(2,128)(2,1)} %reshape.1009), calls=%async_computation.2 | async-start | bytes 688128 | tf_op jit(solution)/shard_map/all_to_all | solution.py:556
  170.7 43.0 %collective-permute-start.28 = (bf16[4,384,384]{2,1,0:T(8,128)(2,1)}, bf16[4,384,384]{2,1,0:T(8,128)(2,1)}, u32[]{:S(2)}, u32[]{:S(2)}) collective-permute-start(bf16[4,384,384]{2,1,0:T(8,128)(2,1)} %get-tuple-element.68), channel_id=1, source_target_pairs={{0,4},{1,5},{2,6},{3,7},{4,0},{5,1},{6,2},{7,3},{8,12},{9,13},{10,... | collective-permute-start | bytes 3538952 | tf_op jit(solution)/shard_map/ppermute | solution.py:32
  197.6 12.4 %copy-start.10 = (f32[4,384,384]{2,1,0:T(8,128)S(1)}, f32[4,384,384]{2,1,0:T(8,128)}, u32[]{:S(2)}) copy-start(f32[4,384,384]{2,1,0:T(8,128)} %get-tuple-element.65) | copy-start | bytes 7077892
  203.2 29.3 %collective-permute-start.18 = (bf16[4,384,384]{2,1,0:T(8,128)(2,1)}, bf16[4,384,384]{2,1,0:T(8,128)(2,1)}, u32[]{:S(2)}, u32[]{:S(2)}) collective-permute-start(bf16[4,384,384]{2,1,0:T(8,128)(2,1)} %get-tuple-element.58), channel_id=1, source_target_pairs={{0,2},{1,3},{2,0},{3,1},{4,6},{5,7},{6,4},{7,5},{8,10},{9,11},{10,... | collective-permute-start | bytes 3538952 | tf_op jit(solution)/shard_map/ppermute | solution.py:32
  206.5 63.9 %all-to-all-start.3 = ((f32[32,1,24]{2,1,0:T(1,128)}), f32[32,1,24]{2,1,0:T(1,128)S(1)}, u32[]{:S(2)}, u32[]{:S(2)}) async-start(f32[32,1,24]{2,1,0:T(1,128)} %bitcast.82), calls=%async_computation.3 | async-start | bytes 32768 | tf_op jit(solution)/shard_map/all_to_all | solution.py:556
  211.8 33.1 %collective-permute-start.25 = (bf16[4,2,2,48,384]{4,3,0,1,2:T(8,128)(2,1)S(1)}, bf16[4,2,2,48,384]{4,3,0,1,2:T(8,128)(2,1)S(1)}, u32[]{:S(2)}, u32[]{:S(2)}) collective-permute-start(bf16[4,2,2,48,384]{4,3,0,1,2:T(8,128)(2,1)S(1)} %fusion.1), channel_id=1, source_target_pairs={{0,2},{1,3},{2,0},{3,1},{4,6},{5,7},{6,4},{7,5},{8,10},{9,11},{10,... | collective-permute-start | bytes 1769480 | tf_op jit(solution)/shard_map/ppermute | solution.py:32
  213.7 18.8 %copy-start.12 = (f32[4,384,384]{2,1,0:T(8,128)S(1)}, f32[4,384,384]{2,1,0:T(8,128)}, u32[]{:S(2)}) copy-start(f32[4,384,384]{2,1,0:T(8,128)} %get-tuple-element.57) | copy-start | bytes 7077892
  215.5 30.0 %collective-permute-start.29 = (bf16[4,2,2,48,384]{4,3,0,1,2:T(8,128)(2,1)S(1)}, bf16[4,2,2,48,384]{4,3,0,1,2:T(8,128)(2,1)S(1)}, u32[]{:S(2)}, u32[]{:S(2)}) collective-permute-start(bf16[4,2,2,48,384]{4,3,0,1,2:T(8,128)(2,1)S(1)} %fusion.2), channel_id=1, source_target_pairs={{0,8},{1,9},{2,10},{3,11},{4,12},{5,13},{6,14},{7,15},{8,0},{9,1},... | collective-permute-start | bytes 1769480 | tf_op jit(solution)/shard_map/ppermute | solution.py:32
  234.1 21.6 %collective-permute-start.19 = (bf16[4,2,2,48,384]{4,3,0,1,2:T(8,128)(2,1)S(1)}, bf16[4,2,2,48,384]{4,3,0,1,2:T(8,128)(2,1)S(1)}, u32[]{:S(2)}, u32[]{:S(2)}) collective-permute-start(bf16[4,2,2,48,384]{4,3,0,1,2:T(8,128)(2,1)S(1)} %fusion), channel_id=1, source_target_pairs={{0,4},{1,5},{2,6},{3,7},{4,0},{5,1},{6,2},{7,3},{8,12},{9,13},{10,... | collective-permute-start | bytes 1769480 | tf_op jit(solution)/shard_map/ppermute | solution.py:32
  245.1 10.4 %collective-permute-start.26 = (bf16[4,2,48,384]{3,2,0,1:T(8,128)(2,1)S(1)}, bf16[4,2,48,384]{3,2,0,1:T(8,128)(2,1)S(1)}, u32[]{:S(2)}, u32[]{:S(2)}) collective-permute-start(bf16[4,2,48,384]{3,2,0,1:T(8,128)(2,1)S(1)} %fusion.4), channel_id=1, source_target_pairs={{0,4},{1,5},{2,6},{3,7},{4,0},{5,1},{6,2},{7,3},{8,12},{9,13},{10,... | collective-permute-start | bytes 884744 | tf_op jit(solution)/shard_map/ppermute | solution.py:32
  245.7 10.0 %collective-permute-start.30 = (bf16[4,2,48,384]{3,2,0,1:T(8,128)(2,1)S(1)}, bf16[4,2,48,384]{3,2,0,1:T(8,128)(2,1)S(1)}, u32[]{:S(2)}, u32[]{:S(2)}) collective-permute-start(bf16[4,2,48,384]{3,2,0,1:T(8,128)(2,1)S(1)} %fusion.5), channel_id=1, source_target_pairs={{0,2},{1,3},{2,0},{3,1},{4,6},{5,7},{6,4},{7,5},{8,10},{9,11},{10,... | collective-permute-start | bytes 884744 | tf_op jit(solution)/shard_map/ppermute | solution.py:32
  255.6 8.1 %collective-permute-start.27 = (bf16[4,48,384]{2,1,0:T(8,128)(2,1)S(1)}, bf16[4,48,384]{2,1,0:T(8,128)(2,1)S(1)}, u32[]{:S(2)}, u32[]{:S(2)}) collective-permute-start(bf16[4,48,384]{2,1,0:T(8,128)(2,1)S(1)} %fusion.14), channel_id=1, source_target_pairs={{0,16},{1,17},{2,18},{3,19},{4,20},{5,21},{6,22},{7,23},{8,24},{9,... | collective-permute-start | bytes 442376 | tf_op jit(solution)/shard_map/ppermute | solution.py:32
  255.9 14.2 %collective-permute-start.20 = (bf16[4,2,48,384]{3,2,0,1:T(8,128)(2,1)S(1)}, bf16[4,2,48,384]{3,2,0,1:T(8,128)(2,1)S(1)}, u32[]{:S(2)}, u32[]{:S(2)}) collective-permute-start(bf16[4,2,48,384]{3,2,0,1:T(8,128)(2,1)S(1)} %fusion.3), channel_id=1, source_target_pairs={{0,8},{1,9},{2,10},{3,11},{4,12},{5,13},{6,14},{7,15},{8,0},{9,1},... | collective-permute-start | bytes 884744 | tf_op jit(solution)/shard_map/ppermute | solution.py:32
  257.4 12.9 %collective-permute-start.31 = (bf16[4,48,384]{2,1,0:T(8,128)(2,1)S(1)}, bf16[4,48,384]{2,1,0:T(8,128)(2,1)S(1)}, u32[]{:S(2)}, u32[]{:S(2)}) collective-permute-start(bf16[4,48,384]{2,1,0:T(8,128)(2,1)S(1)} %fusion.15), channel_id=1, source_target_pairs={{0,16},{1,17},{2,18},{3,19},{4,20},{5,21},{6,22},{7,23},{8,24},{9,... | collective-permute-start | bytes 442376 | tf_op jit(solution)/shard_map/ppermute | solution.py:32
  270.2 7.6 %collective-permute-start.21 = (bf16[4,48,384]{2,1,0:T(8,128)(2,1)S(1)}, bf16[4,48,384]{2,1,0:T(8,128)(2,1)S(1)}, u32[]{:S(2)}, u32[]{:S(2)}) collective-permute-start(bf16[4,48,384]{2,1,0:T(8,128)(2,1)S(1)} %fusion.13), channel_id=1, source_target_pairs={{0,16},{1,17},{2,18},{3,19},{4,20},{5,21},{6,22},{7,23},{8,24},{9,... | collective-permute-start | bytes 442376 | tf_op jit(solution)/shard_map/ppermute | solution.py:32
  277.9 2.0 collective-permute-start.32
  325.2 31.8 %all-to-all-start.5 = ((bf16[32,24,768]{2,1,0:T(8,128)(2,1)}), bf16[32,24,768]{2,1,0:T(8,128)(2,1)S(1)}, u32[]{:S(2)}, u32[]{:S(2)}) async-start(bf16[32,24,768]{2,1,0:T(8,128)(2,1)} %bitcast.78), calls=%async_computation.5 | async-start | bytes 2359296 | tf_op jit(solution)/shard_map/all_to_all | solution.py:556
  328.0 29.0 %copy-start.5 = (f32[18,24,768]{2,1,0:T(8,128)S(1)}, f32[18,24,768]{2,1,0:T(8,128)}, u32[]{:S(2)}) copy-start(f32[18,24,768]{2,1,0:T(8,128)} %param.11) | copy-start | bytes 3981316
  (12 other events, 34.2 us)
where the time goes:
time: 363 us; the launch traced here: 358 us
  waiting for transfers between devices  156 us (43%)
  Pallas kernels  54.3 us (15%)
  starting transfers between devices  52.4 us (14%)
  other arithmetic  35 us (10%)
  blocking collectives  34.5 us (10%)
  local copies, waits for them, and re-layouts  20.5 us (6%)
    ppermute x33, waiting for transfers between devices, flip(): lax.ppermute(values, 'dp', [(i, i ^ 1 << bit) for i in range(devices)])  101 us
    all_to_all x5, waiting for transfers between devices, all_to_all(): return lax.all_to_all(values, 'dp', split_axis=0, concat_axis=0, tiled=True)  55.6 us
    ppermute x33, starting transfers between devices, flip(): lax.ppermute(values, 'dp', [(i, i ^ 1 << bit) for i in range(devices)])  34.5 us
    all_to_all x1, blocking collectives, all_to_all(): return lax.all_to_all(values, 'dp', split_axis=0, concat_axis=0, tiled=True)  34.5 us
    select_n x21, other arithmetic, joined(): jnp.where(taken == 1, jnp.stack([other, values], axis), jnp.stack([values...  19.3 us
    all_to_all x5, starting transfers between devices, all_to_all(): return lax.all_to_all(values, 'dp', split_axis=0, concat_axis=0, tiled=True)  17.9 us
    pallas_call x3, Pallas kernels, run_products(): pl.pallas_call(functools.partial(pair_products, chunk), name='pair_produc...  16.7 us
    pallas_call x1, Pallas kernels, run_attention_backward(): pl.pallas_call(functools.partial(attention_backward, order), name='attent...  11.9 us
  transfers between devices with their start and end apart: 38, of which 16 were waited for; matrix products, arithmetic and copies ran while one was open for 13% of the time, Pallas kernels for 13%

commit v1 on v0

--- a/solution.py
+++ b/solution.py
@@ -54,6 +54,31 @@
             bit = order[stage]
             groups[index] = joined(groups[index], others[index], bit_of(myself, bit), 0)
     return groups, carried
+
+
+def gather_step(values, order, bit, myself):
+    held = order[: order.index(bit)]
+    position = 1 + sum(1 for before in held if before > bit)
+    return joined(values, flip(values, bit), bit_of(myself, bit), position)
+
+
+def flip_by_core(values, first_bit, second_bit):
+    devices = lax.axis_size("dp")
+    return lax.ppermute(
+        values, "dp", [(i, i ^ (1 << (second_bit if i & 1 else first_bit))) for i in range(devices)]
+    )
+
+
+def corner_rows(near, far, order, myself):
+    high, low = bit_of(myself, order[-2]), bit_of(myself, order[-1])
+    core = bit_of(myself, 0)
+    first, second = jnp.where(core == 1, low, high), jnp.where(core == 1, high, low)
+    axis = len(order) - 1
+    pairs = [
+        joined(pair[0], pair[1], first, axis) for pair in (near, far)
+    ]
+    by_first = joined(pairs[0], pairs[1], second, axis)
+    return jnp.where(core == 1, by_first, jnp.swapaxes(by_first, axis, axis + 1))
 
 
 def split_bit(values, mine, position, sent_as):
@@ -523,8 +548,8 @@
     )(mine[None], lefts, lefts_other, rights, rights_other)
 
 
-def orthogonalize(block_ref, out_ref):
-    values = block_ref[...].astype(jnp.float32)
+def muon_steps(block):
+    values = block.astype(jnp.float32)
     scaled = (values / (jnp.sqrt(jnp.sum(values * values)) + 1e-07)).astype(jnp.bfloat16)
     for _ in range(NS_ITERS):
         gram = contract(scaled, scaled, 1, 1).astype(jnp.bfloat16)
@@ -533,23 +558,51 @@
         scaled = (
             COEF_FIRST * scaled.astype(jnp.float32) + contract(mixed, scaled, 1, 0)
         ).astype(jnp.bfloat16)
-    out_ref[...] = scaled
-
-
-def run_orthogonalize(block):
+    return scaled
+
+
+def orthogonalize_halves(place_ref, mine_ref, other_ref, out_ref):
+    core = place_ref[0]
+    mine, other = mine_ref[...], other_ref[...]
+    low, high = jnp.where(core == 1, other, mine), jnp.where(core == 1, mine, other)
+    scaled = muon_steps(jnp.concatenate([low, high], axis=1))
+    out_ref[...] = split_columns(scaled, core)[0]
+
+
+def orthogonalize_whole(block_ref, out_ref):
+    out_ref[0] = muon_steps(block_ref[0])
+
+
+def muon_cost(count, rows):
+    return pl.CostEstimate(
+        flops=6 * count * NS_ITERS * rows**3, bytes_accessed=4 * count * rows**2, transcendentals=0
+    )
+
+
+def run_orthogonalize_halves(place, mine, other):
     return pl.pallas_call(
-        orthogonalize,
-        name="orthogonalize",
-        out_shape=struct(block.shape, block.dtype),
-        in_specs=[VMEM],
+        orthogonalize_halves,
+        name="orthogonalize_halves",
+        out_shape=struct(mine.shape, mine.dtype),
+        in_specs=[SMEM, VMEM, VMEM],
         out_specs=VMEM,
         compiler_params=pltpu.CompilerParams(vmem_limit_bytes=24 << 20),
-        cost_estimate=pl.CostEstimate(
-            flops=6 * NS_ITERS * block.shape[0] ** 3,
-            bytes_accessed=4 * block.size,
-            transcendentals=0,
-        ),
-    )(block)
+        cost_estimate=muon_cost(1, mine.shape[0]),
+    )(place, mine, other)
+
+
+def run_orthogonalize_whole(blocks):
+    spec = pl.BlockSpec((1,) + blocks.shape[1:], lambda step: (step, 0, 0))
+    return pl.pallas_call(
+        orthogonalize_whole,
+        name="orthogonalize_whole",
+        grid=(blocks.shape[0],),
+        out_shape=struct(blocks.shape, blocks.dtype),
+        in_specs=[spec],
+        out_specs=spec,
+        compiler_params=pltpu.CompilerParams(vmem_limit_bytes=24 << 20),
+        cost_estimate=muon_cost(*blocks.shape[:2]),
+    )(blocks)
 
 
 def all_to_all(values):
@@ -598,21 +651,21 @@
     def modulations(small_all):
         silu_rows = lax.dynamic_slice_in_dim(small_all[:, :features], myself * share, share, 1)
         mod_parts = product("ld,kde->lke", silu_rows, ada_w).reshape(devices, ADA * features)
-        return small_all, silu_rows, all_to_all(mod_parts)
-
-    groups, (small_all, silu_rows, mod_sums) = gather_all(
+        offsets = (
+            small_all[:, features:]
+            .reshape(devices, bias_count, share)
+            .transpose(1, 0, 2)
+            .reshape(bias_count, features)
+            .astype(jnp.float32)
+        )
+        return small_all, silu_rows, offsets, all_to_all(mod_parts)
+
+    groups, (small_all, silu_rows, offsets, mod_sums) = gather_all(
         [chip_rows[low:high] for low, high in zip(bounds[:-1], bounds[1:])],
         [tuple(reversed(order)) for order in orders],
         myself,
         small_all,
         modulations,
-    )
-    offsets = (
-        small_all[:, features:]
-        .reshape(devices, bias_count, share)
-        .transpose(1, 0, 2)
-        .reshape(bias_count, features)
-        .astype(jnp.float32)
     )
     modulation = jnp.sum(mod_sums, axis=0).reshape(ADA, features) + offsets[:ADA]
     rows = 2 * share
@@ -631,10 +684,35 @@
     lefts, qkv, attn_out, middle = run_attention_forward(
         held_orders[0], place, latents[0], modulation, offsets, *attn_ws
     )
+    extra = max(0, block_count - devices // 2)
+    assert extra % 2 == 0 and extra <= ADA
+    main = block_count - extra
+    spare = ()
+    spare_bits = tuple(reversed(range(1, bits)))
+    if extra:
+        spare = momenta[:extra].astype(jnp.bfloat16).reshape(2, extra // 2, share, features)
+        spare_mine = lax.dynamic_index_in_dim(spare, core, 0, keepdims=False)
+        spare_other = flip(lax.dynamic_index_in_dim(spare, 1 - core, 0, keepdims=False), 0)
+        spare = joined(spare_mine, spare_other, core, 1).reshape(extra // 2, 2 * share, features)
+        lefts, spare = lax.optimization_barrier((lefts, spare))
+        spare = gather_step(spare, spare_bits, spare_bits[0], myself)
     lefts_other = flip(lefts, 0)
     output, hidden, mlp_keep, mlp_send, grad_middle, grad_attn, rows = run_mlp(
-        held_orders[1:], place, lefts, middle, attn_out, cotangent[0], modulation, offsets, up_ws, down_ws
-    )
+        held_orders[1:],
+        place,
+        lefts,
+        middle,
+        attn_out,
+        cotangent[0],
+        modulation,
+        offsets,
+        up_ws,
+        down_ws,
+    )
+    if extra:
+        grad_attn, spare = lax.optimization_barrier((grad_attn, spare))
+        for bit in spare_bits[1:-2]:
+            spare = gather_step(spare, spare_bits, bit, myself)
     hidden_other = flip(hidden, 0)
     mlp_other = flip(mlp_send, 0)
 
@@ -663,6 +741,13 @@
     input_grad, attn_keep, attn_send, grad_offsets = run_attention_backward(
         held_orders[0], place, latents[0], modulation, *attn_ws, qkv, grad_middle, grad_attn, rows
     )
+    if extra:
+        attn_send, spare = lax.optimization_barrier((attn_send, spare))
+        received = flip_by_core(spare, spare_bits[-2], spare_bits[-1])
+        near = jnp.stack([spare, received])
+        far = flip_by_core(near, spare_bits[-1], spare_bits[-2])
+        spare = corner_rows(near, far, spare_bits, myself)
+        spare = spare.reshape(extra // 2, features, features)
     attn_other = flip(attn_send, 0)
     attn_halves = products(
         lefts, lefts_other, attn_keep, attn_other, lambda b: b // 3, lambda b: b, 4, orders[2]
@@ -722,11 +807,37 @@
     new_bias_momenta = BETA_BIAS * bias_momenta + bias_grads
     new_biases = biases - RATE_BIAS * new_bias_momenta
 
-    outgoing = jnp.pad(
-        new_momenta.astype(jnp.bfloat16), ((0, devices - block_count), (0, 0), (0, 0))
-    )
-    ortho = run_orthogonalize(all_to_all(outgoing).reshape(features, features))
-    ortho_local = all_to_all(ortho.reshape(devices, share, features))[:block_count]
+    outgoing = (
+        new_momenta[extra:]
+        .astype(jnp.bfloat16)
+        .reshape(main, share, 2, half)
+        .transpose(0, 2, 1, 3)
+        .reshape(2 * main, share, half)
+    )
+    outgoing = jnp.pad(outgoing, ((0, devices - 2 * main), (0, 0), (0, 0)))
+    columns_mine = all_to_all(outgoing).reshape(features, half)
+    ortho_half = run_orthogonalize_halves(place, columns_mine, flip(columns_mine, 0))
+    ortho_local = (
+        all_to_all(ortho_half.reshape(devices, share, half))[: 2 * main]
+        .reshape(main, 2, share, half)
+        .transpose(0, 2, 1, 3)
+        .reshape(main, share, features)
+    )
+    if extra:
+        silu_all = small_all[:, :features]
+        mod_mine = lax.dynamic_slice_in_dim(mod_all, core * (extra // 2), extra // 2, 1)
+        spare_grads = product("ld,lke->kde", silu_all, mod_mine) * grad_scale
+        spare = (BETA_WEIGHT * spare.astype(jnp.float32) + spare_grads).astype(jnp.bfloat16)
+        spare_ortho = run_orthogonalize_whole(spare)
+        chip_ortho = lax.dynamic_slice_in_dim(
+            spare_ortho, (myself - core) * share, 2 * share, 1
+        ).reshape(extra // 2, 2, share, features)
+        ortho_mine = lax.dynamic_index_in_dim(chip_ortho, core, 1, keepdims=False)
+        ortho_other = flip(
+            lax.dynamic_index_in_dim(chip_ortho, 1 - core, 1, keepdims=False), 0
+        )
+        spare_local = joined(ortho_mine, ortho_other, core, 0).reshape(extra, share, features)
+        ortho_local = jnp.concatenate([spare_local, ortho_local])
     silu_back = jax.vjp(jax.nn.silu, condition)[1]
     cond_grad = silu_back(grad_silu.reshape(features))[0] * seqlen ** (-0.5)
     new_weights = weights - RATE_WEIGHT * ortho_local.astype(jnp.float32)

time: 363 us -> 344 us (0.948)
  blocking collectives: 34.5 us -> 0 us
  starting transfers between devices: 52.4 us -> 71.8 us
  waiting for transfers between devices: 156 us -> 144 us
  other arithmetic: 35 us -> 41.7 us
  local copies, waits for them, and re-layouts: 20.5 us -> 14.8 us
  Pallas kernels: 54.3 us -> 59.9 us
    all_to_all x1 -> x0, blocking collectives: 34.5 us -> none  [all_to_all(): return lax.all_to_all(values, 'dp', split_axis=0, concat_axis=0, tiled=True)]
    all_to_all x5 -> x6, waiting for transfers between devices: 55.6 us -> 43.7 us  [all_to_all(): return lax.all_to_all(values, 'dp', split_axis=0, concat_axis=0, tiled=True)]
    ppermute x33 -> x38, starting transfers between devices: 34.5 us -> 44.3 us  [flip(): lax.ppermute(values, 'dp', [(i, i ^ 1 << bit) for i in range(devices)])]
    pallas_call x1 -> x2, Pallas kernels: 7.69 us -> 14.7 us  [the longest x1 8.04 us: run_orthogonalize_halves(): pl.pallas_call(orthogonalize_halves, name='orthogonalize_halves', out_sha...]
    all_to_all x5 -> x6, starting transfers between devices: 17.9 us -> 24.6 us  [all_to_all(): return lax.all_to_all(values, 'dp', split_axis=0, concat_axis=0, tiled=True)]
    select_n x21 -> x26, other arithmetic: 19.3 us -> 21 us  [joined(): jnp.where(taken == 1, jnp.stack([other, values], axis), jnp.stack([values...]
    unnamed x50 -> x66, local copies, waits for them, and re-layouts: 7.88 us -> 6.2 us
    ppermute x33 -> x38, waiting for transfers between devices: 101 us -> 100 us  [flip(): lax.ppermute(values, 'dp', [(i, i ^ 1 << bit) for i in range(devices)])]
  transfers between devices with their start and end apart: 38 -> 46, of which waited for: 16 -> 22; matrix products, arithmetic and copies ran while one was open for 13% -> 15% of each run, Pallas kernels for 13% -> 15%
where the time goes in v1:
time: 344 us; the launch traced here: 340 us
  waiting for transfers between devices  144 us (42%)
  starting transfers between devices  71.8 us (21%)
  Pallas kernels  59.9 us (17%)
  other arithmetic  41.7 us (12%)
  local copies, waits for them, and re-layouts  14.8 us (4%)
  matrix products  4.31 us (1%)
    ppermute x38, waiting for transfers between devices, flip(): lax.ppermute(values, 'dp', [(i, i ^ 1 << bit) for i in range(devices)])  100 us
    ppermute x38, starting transfers between devices, flip(): lax.ppermute(values, 'dp', [(i, i ^ 1 << bit) for i in range(devices)])  44.3 us
    all_to_all x6, waiting for transfers between devices, all_to_all(): return lax.all_to_all(values, 'dp', split_axis=0, concat_axis=0, tiled=True)  43.7 us
    all_to_all x6, starting transfers between devices, all_to_all(): return lax.all_to_all(values, 'dp', split_axis=0, concat_axis=0, tiled=True)  24.6 us
    select_n x26, other arithmetic, joined(): jnp.where(taken == 1, jnp.stack([other, values], axis), jnp.stack([values...  21 us
    pallas_call x3, Pallas kernels, run_products(): pl.pallas_call(functools.partial(pair_products, chunk), name='pair_produc...  16.7 us
    pallas_call x1, Pallas kernels, run_mlp(): pl.pallas_call(functools.partial(mlp_both_ways, *mlp_orders), name='mlp_b...  11.2 us
    pallas_call x1, Pallas kernels, run_attention_backward(): pl.pallas_call(functools.partial(attention_backward, order), name='attent...  10.9 us
  transfers between devices with their start and end apart: 46, of which 22 were waited for; matrix products, arithmetic and copies ran while one was open for 15% of the time, Pallas kernels for 15%

profile of v1, /device:TPU:0, one launch (start us, length us, event | category | flops | bytes accessed | tf_op | source)
XLA Modules:
  0.0 339.6 jit_solution(711116207803184305)
XLA Ops:
  4.8 3.9 %collective-permute-start.1 = (bf16[4,48,384]{2,1,0:T(8,128)(2,1)S(1)}, bf16[4,48,384]{2,1,0:T(8,128)(2,1)S(1)}, u32[]{:S(2)}, u32[]{:S(2)}) collective-permute-start(bf16[4,48,384]{2,1,0:T(8,128)(2,1)S(1)} %get-tuple-element.107), channel_id=1, source_target_pairs={{0,16},{1,17},{2,18},{3,19},{4,20},{5,21},{6,22},{7,23},{8,24},{9,... | collective-permute-start | bytes 442376 | tf_op jit(solution)/shard_map/ppermute | solution.py:32
  11.2 3.8 %all-to-all-start = ((bf16[32,2,552]{2,1,0:T(2,128)(2,1)}), bf16[32,2,552]{2,1,0:T(2,128)(2,1)S(1)}, u32[]{:S(2)}, u32[]{:S(2)}) async-start(bf16[32,2,552]{2,1,0:T(2,128)(2,1)} %reshape.1617), calls=%async_computation | async-start | bytes 163840 | tf_op jit(solution)/shard_map/all_to_all | solution.py:609
  15.1 7.6 %all-to-all-done = bf16[32,2,552]{2,1,0:T(2,128)(2,1)S(1)} async-done(((bf16[32,2,552]{2,1,0:T(2,128)(2,1)}), bf16[32,2,552]{2,1,0:T(2,128)(2,1)S(1)}, u32[]{:S(2)}, u32[]{:S(2)}) %all-to-all-start) | async-done | bytes 70688 | tf_op jit(solution)/shard_map/all_to_all | solution.py:609
  23.8 2.2 collective-permute-start.11
  26.9 8.7 %collective-permute-done.5 = bf16[4,48,384]{2,1,0:T(8,128)(2,1)S(1)} collective-permute-done((bf16[4,48,384]{2,1,0:T(8,128)(2,1)S(1)}, bf16[4,48,384]{2,1,0:T(8,128)(2,1)S(1)}, u32[]{:S(2)}, u32[]{:S(2)}) %collective-permute-start.5) | collective-permute-done | bytes 147488 | tf_op jit(solution)/shard_map/ppermute | solution.py:32
  40.6 3.8 %all-to-all-start.1 = ((f32[32,1,4608]{2,1,0:T(1,128)}), f32[32,1,4608]{2,1,0:T(1,128)}, u32[]{:S(2)}, u32[]{:S(2)}) async-start(f32[32,1,4608]{2,1,0:T(1,128)} %all_to_all.49), calls=%async_computation.1 | async-start | bytes 1179648 | tf_op jit(solution)/shard_map/all_to_all | solution.py:609
  44.5 1.9 collective-permute-start.6
  48.8 14.1 %collective-permute-done.6 = bf16[2,4,48,384]{3,2,1,0:T(8,128)(2,1)S(1)} collective-permute-done((bf16[2,4,48,384]{3,2,1,0:T(8,128)(2,1)S(1)}, bf16[2,4,48,384]{3,2,1,0:T(8,128)(2,1)S(1)}, u32[]{:S(2)}, u32[]{:S(2)}) %collective-permute-start.6) | collective-permute-done | bytes 294944 | tf_op jit(solution)/shard_map/ppermute | solution.py:32
  65.5 6.8 %collective-permute-done.3 = bf16[2,2,4,48,384]{4,3,2,1,0:T(8,128)(2,1)S(1)} collective-permute-done((bf16[2,2,4,48,384]{4,3,2,1,0:T(8,128)(2,1)S(1)}, bf16[2,2,4,48,384]{4,3,2,1,0:T(8,128)(2,1)S(1)}, u32[]{:S(2)}, u32[]{:S(2)}) %collective-permute-start.3) | collective-permute-done | bytes 589856 | tf_op jit(solution)/shard_map/ppermute | solution.py:32
  75.1 2.7 collective-permute-done.7
  89.0 15.7 %collective-permute-done.4 = bf16[2,2,2,4,48,384]{5,4,3,2,1,0:T(8,128)(2,1)} collective-permute-done((bf16[2,2,2,4,48,384]{5,4,3,2,1,0:T(8,128)(2,1)}, bf16[2,2,2,4,48,384]{5,4,3,2,1,0:T(8,128)(2,1)}, u32[]{:S(2)}, u32[]{:S(2)}) %collective-permute-start.4) | collective-permute-done | bytes 1179680 | tf_op jit(solution)/shard_map/ppermute | solution.py:32
  105.9 2.2 maximum_select_fusion
  108.6 3.6 %maximum_select_fusion.1 = bf16[2,2,2,2,4,48,384]{6,5,4,3,2,1,0:T(8,128)(2,1)} fusion(bf16[1,2,2,2,4,48,384]{6,5,4,3,2,1,0:T(8,128)(2,1)S(1)} %copy-done.7, bf16[1,2,2,2,4,48,384]{6,5,4,3,2,1,0:T(8,128)(2,1)} %bitcast.39, pred[]{:T(512)S(6)} %eq.21), kind=kLoop, calls=%fused_computation.1 | loop fusion | flops 3538944 | bytes 4718593 | tf_op jit(solution)/shard_map/jit(_where)/select_n | solution.py:40
  112.4 3.6 %maximum_select_fusion.2 = bf16[2,2,2,2,4,48,384]{6,5,4,3,2,1,0:T(8,128)(2,1)} fusion(bf16[1,2,2,2,4,48,384]{6,5,4,3,2,1,0:T(8,128)(2,1)S(1)} %copy-done.6, bf16[1,2,2,2,4,48,384]{6,5,4,3,2,1,0:T(8,128)(2,1)} %bitcast.43, pred[]{:T(512)S(6)} %eq.24), kind=kLoop, calls=%fused_computation.2 | loop fusion | flops 3538944 | bytes 4718593 | tf_op jit(solution)/shard_map/jit(_where)/select_n | solution.py:40
  118.8 2.0 collective-permute-done.10
  121.8 6.4 %attention_forward.1 = (bf16[3,256,768]{2,1,0:T(8,128)(2,1)}, bf16[3,256,768]{2,1,0:T(8,128)(2,1)S(1)}, f32[256,768]{1,0:T(8,128)S(1)}, f32[256,768]{1,0:T(8,128)S(1)}) custom-call(s32[2]{0:T(128)S(1)} %pad_add_fusion.place_ref, bf16[256,768]{1,0:T(8,128)(2,1)S(1)} %bitcast.177, f32[6,768]{1,0:T(8,128)S(1)} %slice_add_fusion.mod_ref, ...), custom_call_target="tpu_custom_call" | custom-call | flops 2013265920 | bytes 8650752 | tf_op jit(solution)/shard_map/attention_forward/pallas_call | solution.py:410
  128.6 11.2 %mlp_both_ways.1 = (bf16[256,768]{1,0:T(8,128)(2,1)}, bf16[4,256,768]{2,1,0:T(8,128)(2,1)}, bf16[5,256,384]{2,1,0:T(8,128)(2,1)S(1)}, bf16[5,256,384]{2,1,0:T(8,...) custom-call(s32[2]{0:T(128)S(1)} %pad_add_fusion.place_ref, ...), custom_call_target="tpu_custom_call" | custom-call | flops 4831838208 | bytes 17301504 | tf_op jit(solution)/shard_map/mlp_both_ways/pallas_call | solution.py:435
  140.1 2.5 collective-permute-start.17
  142.6 4.5 %collective-permute-done.17 = bf16[1,48,768]{2,1,0:T(8,128)(2,1)S(1)} collective-permute-done((bf16[1,48,768]{2,1,0:T(8,128)(2,1)S(1)}, bf16[1,48,768]{2,1,0:T(8,128)(2,1)S(1)}, u32[]{:S(2)}, u32[]{:S(2)}) %collective-permute-start.17) | collective-permute-done | bytes 73760 | tf_op jit(solution)/shard_map/ppermute | solution.py:32
  147.4 10.9 %attention_backward.1 = (f32[256,768]{1,0:T(8,128)}, bf16[4,256,384]{2,1,0:T(8,128)(2,1)S(1)}, bf16[4,256,384]{2,1,0:T(8,128)(2,1)}, f32[14,768]{1,0:T(8,128)S(1)}) custom-call(s32[2]{0:T(128)S(1)} %pad_add_fusion.place_ref, bf16[256,768]{1,0:T(8,128)(2,1)S(1)} %bitcast.178, f32[6,768]{1,0:T(8,128)S(1)} %slice_add_fusion.mod_ref, ...), custom_call_target="tpu_custom_call" | custom-call | flops 3221225472 | bytes 9437184 | tf_op jit(solution)/shard_map/attention_backward/pallas_call | solution.py:486
  159.8 5.5 %pair_products.5 = (f32[4,384,384]{2,1,0:T(8,128)}, bf16[4,384,384]{2,1,0:T(8,128)(2,1)}) custom-call(s32[1]{0:T(128)} %bitcast.75.mine_ref, bf16[3,256,768]{2,1,0:T(8,128)(2,1)} %get-tuple-element.52.lefts_ref.left_ref, bf16[3,256,768]{2,1,0:T(8,128)(2,1)} %collective-permute-done.24.left_other_ref, bf16[5,256,384]{2,1,0:T(8,128)(2,1)} %copy-done, ...), custom_call_target="tpu_custom_call" | custom-call | flops 1207959552 | bytes 7077888 | tf_op jit(solution)/shard_map/pair_products/pallas_call | solution.py:537
  165.3 1.7 collective-permute-start.31
  169.1 4.5 %all-to-all-start.2 = ((bf16[32,2,2640]{2,1,0:T(2,128)(2,1)}), bf16[32,2,2640]{2,1,0:T(2,128)(2,1)S(1)}, u32[]{:S(2)}, u32[]{:S(2)}) async-start(bf16[32,2,2640]{2,1,0:T(2,128)(2,1)} %reshape.1619), calls=%async_computation.2 | async-start | bytes 688128 | tf_op jit(solution)/shard_map/all_to_all | solution.py:609
  174.5 5.6 %pair_products.4 = (f32[4,384,384]{2,1,0:T(8,128)}, bf16[4,384,384]{2,1,0:T(8,128)(2,1)}) custom-call(s32[1]{0:T(128)} %bitcast.65.mine_ref, bf16[3,256,768]{2,1,0:T(8,128)(2,1)} %get-tuple-element.52.lefts_ref.left_ref, bf16[3,256,768]{2,1,0:T(8,128)(2,1)} %collective-permute-done.24.left_other_ref, bf16[4,256,384]{2,1,0:T(8,128)(2,1)} %copy-done.4, ...), custom_call_target="tpu_custom_call" | custom-call | flops 1207959552 | bytes 7077888 | tf_op jit(solution)/shard_map/pair_products/pallas_call | solution.py:537
  180.1 1.8 collective-permute-start.27
  183.3 14.2 %all-to-all-done.2 = bf16[32,2,2640]{2,1,0:T(2,128)(2,1)S(1)} async-done(((bf16[32,2,2640]{2,1,0:T(2,128)(2,1)}), bf16[32,2,2640]{2,1,0:T(2,128)(2,1)S(1)}, u32[]{:S(2)}, u32[]{:S(2)}) %all-to-all-start.2) | async-done | bytes 337952 | tf_op jit(solution)/shard_map/all_to_all | solution.py:609
  199.2 5.6 %pair_products.3 = (f32[4,384,384]{2,1,0:T(8,128)}, bf16[4,384,384]{2,1,0:T(8,128)(2,1)}) custom-call(s32[1]{0:T(128)} %bitcast.51.mine_ref, bf16[4,256,768]{2,1,0:T(8,128)(2,1)} %get-tuple-element.64.left_ref, bf16[4,256,768]{2,1,0:T(8,128)(2,1)} %collective-permute-done.18.left_other_ref, bf16[5,256,384]{2,1,0:T(8,128)(2,1)} %copy-done, ...), custom_call_target="tpu_custom_call" | custom-call | flops 1207959552 | bytes 7077888 | tf_op jit(solution)/shard_map/pair_products/pallas_call | solution.py:537
  206.2 1.7 fusion.8
  207.9 5.2 %all-to-all-start.3 = ((f32[32,1,24]{2,1,0:T(1,128)}), f32[32,1,24]{2,1,0:T(1,128)S(1)}, u32[]{:S(2)}, u32[]{:S(2)}) async-start(f32[32,1,24]{2,1,0:T(1,128)} %bitcast.109), calls=%async_computation.3 | async-start | bytes 32768 | tf_op jit(solution)/shard_map/all_to_all | solution.py:609
  213.1 1.7 convert_add_fusion
  214.9 1.9 collective-permute-start.32
  216.9 1.7 convert_add_fusion.1
  220.2 13.9 %collective-permute-done.20 = bf16[4,384,384]{2,1,0:T(8,128)(2,1)} collective-permute-done((bf16[4,384,384]{2,1,0:T(8,128)(2,1)}, bf16[4,384,384]{2,1,0:T(8,128)(2,1)}, u32[]{:S(2)}, u32[]{:S(2)}) %collective-permute-start.20) | collective-permute-done | bytes 1179680 | tf_op jit(solution)/shard_map/ppermute | solution.py:32
  239.0 7.7 %collective-permute-done.28 = bf16[4,2,2,48,384]{4,3,0,1,2:T(8,128)(2,1)S(1)} collective-permute-done((bf16[4,2,2,48,384]{4,3,0,1,2:T(8,128)(2,1)S(1)}, bf16[4,2,2,48,384]{4,3,0,1,2:T(8,128)(2,1)S(1)}, u32[]{:S(2)}, u32[]{:S(2)}) %collective-permute-start.28) | collective-permute-done | bytes 589856 | tf_op jit(solution)/shard_map/ppermute | solution.py:32
  248.6 3.6 %collective-permute-done.33 = bf16[4,2,48,384]{3,2,0,1:T(8,128)(2,1)S(1)} collective-permute-done((bf16[4,2,48,384]{3,2,0,1:T(8,128)(2,1)S(1)}, bf16[4,2,48,384]{3,2,0,1:T(8,128)(2,1)S(1)}, u32[]{:S(2)}, u32[]{:S(2)}) %collective-permute-start.33) | collective-permute-done | bytes 294944 | tf_op jit(solution)/shard_map/ppermute | solution.py:32
  252.3 3.4 %collective-permute-start.34 = (bf16[4,48,384]{2,1,0:T(8,128)(2,1)S(1)}, bf16[4,48,384]{2,1,0:T(8,128)(2,1)S(1)}, u32[]{:S(2)}, u32[]{:S(2)}) collective-permute-start(bf16[4,48,384]{2,1,0:T(8,128)(2,1)S(1)} %fusion.18), channel_id=1, source_target_pairs={{0,16},{1,17},{2,18},{3,19},{4,20},{5,21},{6,22},{7,23},{8,24},{9,... | collective-permute-start | bytes 442376 | tf_op jit(solution)/shard_map/ppermute | solution.py:32
  258.1 1.9 collective-permute-start.30
  260.0 2.9 collective-permute-done.34
  262.9 6.7 %collective-permute-done.22 = bf16[4,2,48,384]{3,2,0,1:T(8,128)(2,1)S(1)} collective-permute-done((bf16[4,2,48,384]{3,2,0,1:T(8,128)(2,1)S(1)}, bf16[4,2,48,384]{3,2,0,1:T(8,128)(2,1)S(1)}, u32[]{:S(2)}, u32[]{:S(2)}) %collective-permute-start.22) | collective-permute-done | bytes 294944 | tf_op jit(solution)/shard_map/ppermute | solution.py:32
  270.2 7.5 %collective-permute-done.23 = bf16[4,48,384]{2,1,0:T(8,128)(2,1)S(1)} collective-permute-done((bf16[4,48,384]{2,1,0:T(8,128)(2,1)S(1)}, bf16[4,48,384]{2,1,0:T(8,128)(2,1)S(1)}, u32[]{:S(2)}, u32[]{:S(2)}) %collective-permute-start.23) | collective-permute-done | bytes 147488 | tf_op jit(solution)/shard_map/ppermute | solution.py:32
  282.6 1.8 fusion.31
  285.3 3.7 %all-to-all-start.4 = ((bf16[32,24,384]{2,1,0:T(8,128)(2,1)}), bf16[32,24,384]{2,1,0:T(8,128)(2,1)S(1)}, u32[]{:S(2)}, u32[]{:S(2)}) async-start(bf16[32,24,384]{2,1,0:T(8,128)(2,1)} %bitcast.99), calls=%async_computation.4 | async-start | bytes 1179648 | tf_op jit(solution)/shard_map/all_to_all | solution.py:609
  292.2 13.6 %all-to-all-done.4 = bf16[32,24,384]{2,1,0:T(8,128)(2,1)S(1)} async-done(((bf16[32,24,384]{2,1,0:T(8,128)(2,1)}), bf16[32,24,384]{2,1,0:T(8,128)(2,1)S(1)}, u32[]{:S(2)}, u32[]{:S(2)}) %all-to-all-start.4) | async-done | bytes 589856 | tf_op jit(solution)/shard_map/all_to_all | solution.py:609
  306.3 2.1 fusion.block_ref
  308.4 8.0 %orthogonalize_halves.1 = bf16[768,384]{1,0:T(8,128)(2,1)} custom-call(s32[2]{0:T(128)S(1)} %pad_add_fusion.place_ref, bf16[768,384]{1,0:T(8,128)(2,1)S(1)} %bitcast.175, bf16[768,384]{1,0:T(8,128)(2,1)S(1)} %collective-permute-done.39.other_ref), custom_call_target="tpu_custom_call" | custom-call | flops 5435817984 | bytes 2359296 | tf_op jit(solution)/shard_map/orthogonalize_halves/pallas_call | solution.py:583
  316.5 3.6 %all-to-all-start.5 = ((bf16[32,24,384]{2,1,0:T(8,128)(2,1)}), bf16[32,24,384]{2,1,0:T(8,128)(2,1)S(1)}, u32[]{:S(2)}, u32[]{:S(2)}) async-start(bf16[32,24,384]{2,1,0:T(8,128)(2,1)} %bitcast.101), calls=%async_computation.5 | async-start | bytes 1179648 | tf_op jit(solution)/shard_map/all_to_all | solution.py:609
  320.1 6.7 %orthogonalize_whole.1 = bf16[1,768,768]{2,1,0:T(8,128)(2,1)S(1)} custom-call(bf16[1,768,768]{2,1,0:T(8,128)(2,1)S(1)} %fusion.block_ref), custom_call_target="tpu_custom_call" | custom-call | flops 5435817984 | bytes 2359296 | tf_op jit(solution)/shard_map/orthogonalize_whole/pallas_call | solution.py:596
  328.5 8.4 %all-to-all-done.5 = bf16[32,24,384]{2,1,0:T(8,128)(2,1)S(1)} async-done(((bf16[32,24,384]{2,1,0:T(8,128)(2,1)}), bf16[32,24,384]{2,1,0:T(8,128)(2,1)S(1)}, u32[]{:S(2)}, u32[]{:S(2)}) %all-to-all-start.5) | async-done | bytes 589856 | tf_op jit(solution)/shard_map/all_to_all | solution.py:609
  (237 shorter events, 71.5 us)
Async XLA Ops:
  2.0 36.5 %copy-start.9 = (bf16[18,24,768]{2,1,0:T(8,128)(2,1)}, bf16[18,24,768]{2,1,0:T(8,128)(2,1)S(1)}, u32[]{:S(2)}) copy-start(bf16[18,24,768]{2,1,0:T(8,128)(2,1)S(1)} %convert_element_type.152) | copy-start | bytes 1990660
  2.2 1.7 collective-permute-start
  4.8 21.2 %collective-permute-start.1 = (bf16[4,48,384]{2,1,0:T(8,128)(2,1)S(1)}, bf16[4,48,384]{2,1,0:T(8,128)(2,1)S(1)}, u32[]{:S(2)}, u32[]{:S(2)}) collective-permute-start(bf16[4,48,384]{2,1,0:T(8,128)(2,1)S(1)} %get-tuple-element.107), channel_id=1, source_target_pairs={{0,16},{1,17},{2,18},{3,19},{4,20},{5,21},{6,22},{7,23},{8,24},{9,... | collective-permute-start | bytes 442376 | tf_op jit(solution)/shard_map/ppermute | solution.py:32
  11.2 11.4 %all-to-all-start = ((bf16[32,2,552]{2,1,0:T(2,128)(2,1)}), bf16[32,2,552]{2,1,0:T(2,128)(2,1)S(1)}, u32[]{:S(2)}, u32[]{:S(2)}) async-start(bf16[32,2,552]{2,1,0:T(2,128)(2,1)} %reshape.1617), calls=%async_computation | async-start | bytes 163840 | tf_op jit(solution)/shard_map/all_to_all | solution.py:609
  23.0 60.4 %copy-start.15 = (bf16[32,1,1104]{0,2,1:T(8,128)(2,1)}, bf16[32,1,1104]{0,2,1:T(8,128)(2,1)S(1)}, u32[]{:S(2)}) copy-start(bf16[32,1,1104]{0,2,1:T(8,128)(2,1)S(1)} %copy.82) | copy-start | bytes 211972
  23.1 12.5 %collective-permute-start.5 = (bf16[4,48,384]{2,1,0:T(8,128)(2,1)S(1)}, bf16[4,48,384]{2,1,0:T(8,128)(2,1)S(1)}, u32[]{:S(2)}, u32[]{:S(2)}) collective-permute-start(bf16[4,48,384]{2,1,0:T(8,128)(2,1)S(1)} %get-tuple-element.106), channel_id=1, source_target_pairs={{0,16},{1,17},{2,18},{3,19},{4,20},{5,21},{6,22},{7,23},{8,24},{9,... | collective-permute-start | bytes 442376 | tf_op jit(solution)/shard_map/ppermute | solution.py:32
  23.8 22.6 %collective-permute-start.11 = (bf16[4,48,384]{2,1,0:T(8,128)(2,1)}, bf16[4,48,384]{2,1,0:T(8,128)(2,1)S(1)}, u32[]{:S(2)}, u32[]{:S(2)}) collective-permute-start(bf16[4,48,384]{2,1,0:T(8,128)(2,1)} %get-tuple-element.105), channel_id=1, source_target_pairs={{0,16},{1,17},{2,18},{3,19},{4,20},{5,21},{6,22},{7,23},{8,24},{9,... | collective-permute-start | bytes 442376 | tf_op jit(solution)/shard_map/ppermute | solution.py:32
  37.1 10.9 %collective-permute-start.2 = (bf16[2,4,48,384]{3,2,1,0:T(8,128)(2,1)}, bf16[2,4,48,384]{3,2,1,0:T(8,128)(2,1)S(1)}, u32[]{:S(2)}, u32[]{:S(2)}) collective-permute-start(bf16[2,4,48,384]{3,2,1,0:T(8,128)(2,1)} %maximum_select_fusion.20), channel_id=1, source_target_pairs={{0,4},{1,5},{2,6},{3,7},{4,0},{5,1},{6,2},{7,3},{8,12},{9,13},{10,... | collective-permute-start | bytes 884744 | tf_op jit(solution)/shard_map/ppermute | solution.py:32
  40.6 47.2 %all-to-all-start.1 = ((f32[32,1,4608]{2,1,0:T(1,128)}), f32[32,1,4608]{2,1,0:T(1,128)}, u32[]{:S(2)}, u32[]{:S(2)}) async-start(f32[32,1,4608]{2,1,0:T(1,128)} %all_to_all.49), calls=%async_computation.1 | async-start | bytes 1179648 | tf_op jit(solution)/shard_map/all_to_all | solution.py:609
  44.5 18.4 %collective-permute-start.6 = (bf16[2,4,48,384]{3,2,1,0:T(8,128)(2,1)S(1)}, bf16[2,4,48,384]{3,2,1,0:T(8,128)(2,1)S(1)}, u32[]{:S(2)}, u32[]{:S(2)}) collective-permute-start(bf16[2,4,48,384]{3,2,1,0:T(8,128)(2,1)S(1)} %maximum_select_fusion.22), channel_id=1, source_target_pairs={{0,8},{1,9},{2,10},{3,11},{4,12},{5,13},{6,14},{7,15},{8,0},{9,1},... | collective-permute-start | bytes 884744 | tf_op jit(solution)/shard_map/ppermute | solution.py:32
  46.4 18.2 %collective-permute-start.12 = (bf16[2,4,48,384]{3,2,1,0:T(8,128)(2,1)S(1)}, bf16[2,4,48,384]{3,2,1,0:T(8,128)(2,1)S(1)}, u32[]{:S(2)}, u32[]{:S(2)}) collective-permute-start(bf16[2,4,48,384]{3,2,1,0:T(8,128)(2,1)S(1)} %maximum_select_fusion.24), channel_id=1, source_target_pairs={{0,2},{1,3},{2,0},{3,1},{4,6},{5,7},{6,4},{7,5},{8,10},{9,11},{10,... | collective-permute-start | bytes 884744 | tf_op jit(solution)/shard_map/ppermute | solution.py:32
  48.2 24.1 %collective-permute-start.3 = (bf16[2,2,4,48,384]{4,3,2,1,0:T(8,128)(2,1)S(1)}, bf16[2,2,4,48,384]{4,3,2,1,0:T(8,128)(2,1)S(1)}, u32[]{:S(2)}, u32[]{:S(2)}) collective-permute-start(bf16[2,2,4,48,384]{4,3,2,1,0:T(8,128)(2,1)S(1)} %maximum_select_fusion.11), channel_id=1, source_target_pairs={{0,2},{1,3},{2,0},{3,1},{4,6},{5,7},{6,4},{7,5},{8,10},{9,11},{10,... | collective-permute-start | bytes 1769480 | tf_op jit(solution)/shard_map/ppermute | solution.py:32
  63.0 14.8 %collective-permute-start.7 = (bf16[2,2,4,48,384]{4,3,2,1,0:T(8,128)(2,1)S(1)}, bf16[2,2,4,48,384]{4,3,2,1,0:T(8,128)(2,1)S(1)}, u32[]{:S(2)}, u32[]{:S(2)}) collective-permute-start(bf16[2,2,4,48,384]{4,3,2,1,0:T(8,128)(2,1)S(1)} %maximum_select_fusion.13), channel_id=1, source_target_pairs={{0,4},{1,5},{2,6},{3,7},{4,0},{5,1},{6,2},{7,3},{8,12},{9,13},{10,... | collective-permute-start | bytes 1769480 | tf_op jit(solution)/shard_map/ppermute | solution.py:32
  64.7 16.3 %collective-permute-start.13 = (bf16[2,2,4,48,384]{4,3,2,1,0:T(8,128)(2,1)S(1)}, bf16[2,2,4,48,384]{4,3,2,1,0:T(8,128)(2,1)S(1)}, u32[]{:S(2)}, u32[]{:S(2)}) collective-permute-start(bf16[2,2,4,48,384]{4,3,2,1,0:T(8,128)(2,1)S(1)} %maximum_select_fusion.15), channel_id=1, source_target_pairs={{0,8},{1,9},{2,10},{3,11},{4,12},{5,13},{6,14},{7,15},{8,0},{9,1},... | collective-permute-start | bytes 1769480 | tf_op jit(solution)/shard_map/ppermute | solution.py:32
  73.5 31.1 %collective-permute-start.4 = (bf16[2,2,2,4,48,384]{5,4,3,2,1,0:T(8,128)(2,1)}, bf16[2,2,2,4,48,384]{5,4,3,2,1,0:T(8,128)(2,1)}, u32[]{:S(2)}, u32[]{:S(2)}) collective-permute-start(bf16[2,2,2,4,48,384]{5,4,3,2,1,0:T(8,128)(2,1)} %maximum_select_fusion.3), channel_id=1, source_target_pairs={{0,8},{1,9},{2,10},{3,11},{4,12},{5,13},{6,14},{7,15},{8,0},{9,1},... | collective-permute-start | bytes 3538952 | tf_op jit(solution)/shard_map/ppermute | solution.py:32
  79.0 26.9 %collective-permute-start.8 = (bf16[2,2,2,4,48,384]{5,4,3,2,1,0:T(8,128)(2,1)}, bf16[2,2,2,4,48,384]{5,4,3,2,1,0:T(8,128)(2,1)}, u32[]{:S(2)}, u32[]{:S(2)}) collective-permute-start(bf16[2,2,2,4,48,384]{5,4,3,2,1,0:T(8,128)(2,1)} %maximum_select_fusion.4), channel_id=1, source_target_pairs={{0,2},{1,3},{2,0},{3,1},{4,6},{5,7},{6,4},{7,5},{8,10},{9,11},{10,... | collective-permute-start | bytes 3538952 | tf_op jit(solution)/shard_map/ppermute | solution.py:32
  82.3 26.3 %collective-permute-start.14 = (bf16[2,2,2,4,48,384]{5,4,3,2,1,0:T(8,128)(2,1)}, bf16[2,2,2,4,48,384]{5,4,3,2,1,0:T(8,128)(2,1)}, u32[]{:S(2)}, u32[]{:S(2)}) collective-permute-start(bf16[2,2,2,4,48,384]{5,4,3,2,1,0:T(8,128)(2,1)} %maximum_select_fusion.6), channel_id=1, source_target_pairs={{0,4},{1,5},{2,6},{3,7},{4,0},{5,1},{6,2},{7,3},{8,12},{9,13},{10,... | collective-permute-start | bytes 3538952 | tf_op jit(solution)/shard_map/ppermute | solution.py:32
  108.1 13.7 %collective-permute-start.9 = (bf16[16,4,48,384]{3,2,1,0:T(8,128)(2,1)S(1)}, bf16[16,4,48,384]{3,2,1,0:T(8,128)(2,1)}, u32[]{:S(2)}, u32[]{:S(2)}) collective-permute-start(bf16[16,4,48,384]{3,2,1,0:T(8,128)(2,1)S(1)} %bitcast.171), channel_id=1, source_target_pairs={{0,1},{1,0},{2,3},{3,2},{4,5},{5,4},{6,7},{7,6},{8,9},{9,8},{10,11... | collective-permute-start | bytes 7077896 | tf_op jit(solution)/shard_map/ppermute | solution.py:32
  112.2 16.4 %collective-permute-start.15 = (bf16[16,4,48,384]{3,2,1,0:T(8,128)(2,1)}, bf16[16,4,48,384]{3,2,1,0:T(8,128)(2,1)}, u32[]{:S(2)}, u32[]{:S(2)}) collective-permute-start(bf16[16,4,48,384]{3,2,1,0:T(8,128)(2,1)} %bitcast.42.up_ref), channel_id=1, source_target_pairs={{0,1},{1,0},{2,3},{3,2},{4,5},{5,4},{6,7},{7,6},{8,9},{9,8},{10,11... | collective-permute-start | bytes 7077896 | tf_op jit(solution)/shard_map/ppermute | solution.py:32
  115.9 12.7 %collective-permute-start.16 = (bf16[16,4,48,384]{3,2,1,0:T(8,128)(2,1)}, bf16[16,4,48,384]{3,2,1,0:T(8,128)(2,1)}, u32[]{:S(2)}, u32[]{:S(2)}) collective-permute-start(bf16[16,4,48,384]{3,2,1,0:T(8,128)(2,1)} %bitcast.46.down_ref), channel_id=1, source_target_pairs={{0,1},{1,0},{2,3},{3,2},{4,5},{5,4},{6,7},{7,6},{8,9},{9,8},{10,11... | collective-permute-start | bytes 7077896 | tf_op jit(solution)/shard_map/ppermute | solution.py:32
  117.3 3.6 %collective-permute-start.10 = (bf16[1,24,768]{2,1,0:T(8,128)(2,1)S(1)}, bf16[1,24,768]{2,1,0:T(8,128)(2,1)}, u32[]{:S(2)}, u32[]{:S(2)}) collective-permute-start(bf16[1,24,768]{2,1,0:T(8,128)(2,1)S(1)} %get-tuple-element.112), channel_id=1, source_target_pairs={{0,1},{1,0},{2,3},{3,2},{4,5},{5,4},{6,7},{7,6},{8,9},{9,8},{10,11... | collective-permute-start | bytes 110600 | tf_op jit(solution)/shard_map/ppermute | solution.py:32
  128.2 31.6 %collective-permute-start.24 = (bf16[3,256,768]{2,1,0:T(8,128)(2,1)}, bf16[3,256,768]{2,1,0:T(8,128)(2,1)}, u32[]{:S(2)}, u32[]{:S(2)}) collective-permute-start(bf16[3,256,768]{2,1,0:T(8,128)(2,1)} %get-tuple-element.52.lefts_ref.left_ref), channel_id=1, source_target_pairs={{0,1},{1,0},{2,3},{3,2},{4,5},{5,4},{6,7},{7,6},{8,9},{9,8},{10,11... | collective-permute-start | bytes 3538952 | tf_op jit(solution)/shard_map/ppermute | solution.py:32
  139.9 19.9 %collective-permute-start.19 = (bf16[5,256,384]{2,1,0:T(8,128)(2,1)S(1)}, bf16[5,256,384]{2,1,0:T(8,128)(2,1)}, u32[]{:S(2)}, u32[]{:S(2)}) collective-permute-start(bf16[5,256,384]{2,1,0:T(8,128)(2,1)S(1)} %get-tuple-element.66), channel_id=1, source_target_pairs={{0,1},{1,0},{2,3},{3,2},{4,5},{5,4},{6,7},{7,6},{8,9},{9,8},{10,11... | collective-permute-start | bytes 2949128 | tf_op jit(solution)/shard_map/ppermute | solution.py:32
  140.1 7.0 %collective-permute-start.17 = (bf16[1,48,768]{2,1,0:T(8,128)(2,1)S(1)}, bf16[1,48,768]{2,1,0:T(8,128)(2,1)S(1)}, u32[]{:S(2)}, u32[]{:S(2)}) collective-permute-start(bf16[1,48,768]{2,1,0:T(8,128)(2,1)S(1)} %bitcast.226), channel_id=1, source_target_pairs={{0,16},{1,17},{2,18},{3,19},{4,20},{5,21},{6,22},{7,23},{8,24},{9,... | collective-permute-start | bytes 221192 | tf_op jit(solution)/shard_map/ppermute | solution.py:32
  142.6 56.7 %collective-permute-start.18 = (bf16[4,256,768]{2,1,0:T(8,128)(2,1)}, bf16[4,256,768]{2,1,0:T(8,128)(2,1)}, u32[]{:S(2)}, u32[]{:S(2)}) collective-permute-start(bf16[4,256,768]{2,1,0:T(8,128)(2,1)} %get-tuple-element.64.left_ref), channel_id=1, source_target_pairs={{0,1},{1,0},{2,3},{3,2},{4,5},{5,4},{6,7},{7,6},{8,9},{9,8},{10,11... | collective-permute-start | bytes 4718600 | tf_op jit(solution)/shard_map/ppermute | solution.py:32
  147.1 12.1 %collective-permute-start.25 = (bf16[1,2,48,768]{3,2,1,0:T(8,128)(2,1)S(1)}, bf16[1,2,48,768]{3,2,1,0:T(8,128)(2,1)S(1)}, u32[]{:S(2)}, u32[]{:S(2)}) collective-permute-start(bf16[1,2,48,768]{3,2,1,0:T(8,128)(2,1)S(1)} %maximum_select_fusion.27), channel_id=1, source_target_pairs={{0,8},{1,9},{2,10},{3,11},{4,12},{5,13},{6,14},{7,15},{8,0},{9,1},... | collective-permute-start | bytes 442376 | tf_op jit(solution)/shard_map/ppermute | solution.py:32
  159.2 14.4 %collective-permute-start.26 = (bf16[4,256,384]{2,1,0:T(8,128)(2,1)}, bf16[4,256,384]{2,1,0:T(8,128)(2,1)S(1)}, u32[]{:S(2)}, u32[]{:S(2)}) collective-permute-start(bf16[4,256,384]{2,1,0:T(8,128)(2,1)} %get-tuple-element.76), channel_id=1, source_target_pairs={{0,1},{1,0},{2,3},{3,2},{4,5},{5,4},{6,7},{7,6},{8,9},{9,8},{10,11... | collective-permute-start | bytes 2359304 | tf_op jit(solution)/shard_map/ppermute | solution.py:32
  165.3 47.8 %collective-permute-start.31 = (bf16[4,384,384]{2,1,0:T(8,128)(2,1)}, bf16[4,384,384]{2,1,0:T(8,128)(2,1)}, u32[]{:S(2)}, u32[]{:S(2)}) collective-permute-start(bf16[4,384,384]{2,1,0:T(8,128)(2,1)} %get-tuple-element.80), channel_id=1, source_target_pairs={{0,4},{1,5},{2,6},{3,7},{4,0},{5,1},{6,2},{7,3},{8,12},{9,13},{10,... | collective-permute-start | bytes 3538952 | tf_op jit(solution)/shard_map/ppermute | solution.py:32
  169.1 28.4 %all-to-all-start.2 = ((bf16[32,2,2640]{2,1,0:T(2,128)(2,1)}), bf16[32,2,2640]{2,1,0:T(2,128)(2,1)S(1)}, u32[]{:S(2)}, u32[]{:S(2)}) async-start(bf16[32,2,2640]{2,1,0:T(2,128)(2,1)} %reshape.1619), calls=%async_computation.2 | async-start | bytes 688128 | tf_op jit(solution)/shard_map/all_to_all | solution.py:609
  180.1 36.8 %collective-permute-start.27 = (bf16[4,384,384]{2,1,0:T(8,128)(2,1)}, bf16[4,384,384]{2,1,0:T(8,128)(2,1)}, u32[]{:S(2)}, u32[]{:S(2)}) collective-permute-start(bf16[4,384,384]{2,1,0:T(8,128)(2,1)} %get-tuple-element.78), channel_id=1, source_target_pairs={{0,8},{1,9},{2,10},{3,11},{4,12},{5,13},{6,14},{7,15},{8,0},{9,1},... | collective-permute-start | bytes 3538952 | tf_op jit(solution)/shard_map/ppermute | solution.py:32
  181.9 96.7 %collective-permute-start.36 = (bf16[1,2,2,48,768]{4,3,2,1,0:T(8,128)(2,1)S(1)}, bf16[1,2,2,48,768]{4,3,2,1,0:T(8,128)(2,1)}, u32[]{:S(2)}, u32[]{:S(2)}) collective-permute-start(bf16[1,2,2,48,768]{4,3,2,1,0:T(8,128)(2,1)S(1)} %maximum_select_fusion.26), channel_id=1, source_target_pairs={{0,4},{1,3},{2,6},{3,1},{4,0},{5,7},{6,2},{7,5},{8,12},{9,11},{10,... | collective-permute-start | bytes 884744 | tf_op jit(solution)/shard_map/ppermute | solution.py:67
  204.9 29.3 %collective-permute-start.20 = (bf16[4,384,384]{2,1,0:T(8,128)(2,1)}, bf16[4,384,384]{2,1,0:T(8,128)(2,1)}, u32[]{:S(2)}, u32[]{:S(2)}) collective-permute-start(bf16[4,384,384]{2,1,0:T(8,128)(2,1)} %get-tuple-element.68), channel_id=1, source_target_pairs={{0,2},{1,3},{2,0},{3,1},{4,6},{5,7},{6,4},{7,5},{8,10},{9,11},{10,... | collective-permute-start | bytes 3538952 | tf_op jit(solution)/shard_map/ppermute | solution.py:32
  207.9 62.2 %all-to-all-start.3 = ((f32[32,1,24]{2,1,0:T(1,128)}), f32[32,1,24]{2,1,0:T(1,128)S(1)}, u32[]{:S(2)}, u32[]{:S(2)}) async-start(f32[32,1,24]{2,1,0:T(1,128)} %bitcast.109), calls=%async_computation.3 | async-start | bytes 32768 | tf_op jit(solution)/shard_map/all_to_all | solution.py:609
  214.9 22.6 %collective-permute-start.32 = (bf16[4,2,2,48,384]{4,3,0,1,2:T(8,128)(2,1)S(1)}, bf16[4,2,2,48,384]{4,3,0,1,2:T(8,128)(2,1)S(1)}, u32[]{:S(2)}, u32[]{:S(2)}) collective-permute-start(bf16[4,2,2,48,384]{4,3,0,1,2:T(8,128)(2,1)S(1)} %fusion.3), channel_id=1, source_target_pairs={{0,8},{1,9},{2,10},{3,11},{4,12},{5,13},{6,14},{7,15},{8,0},{9,1},... | collective-permute-start | bytes 1769480 | tf_op jit(solution)/shard_map/ppermute | solution.py:32
  218.7 28.1 %collective-permute-start.28 = (bf16[4,2,2,48,384]{4,3,0,1,2:T(8,128)(2,1)S(1)}, bf16[4,2,2,48,384]{4,3,0,1,2:T(8,128)(2,1)S(1)}, u32[]{:S(2)}, u32[]{:S(2)}) collective-permute-start(bf16[4,2,2,48,384]{4,3,0,1,2:T(8,128)(2,1)S(1)} %fusion.2), channel_id=1, source_target_pairs={{0,2},{1,3},{2,0},{3,1},{4,6},{5,7},{6,4},{7,5},{8,10},{9,11},{10,... | collective-permute-start | bytes 1769480 | tf_op jit(solution)/shard_map/ppermute | solution.py:32
  235.8 20.4 %collective-permute-start.21 = (bf16[4,2,2,48,384]{4,3,0,1,2:T(8,128)(2,1)S(1)}, bf16[4,2,2,48,384]{4,3,0,1,2:T(8,128)(2,1)S(1)}, u32[]{:S(2)}, u32[]{:S(2)}) collective-permute-start(bf16[4,2,2,48,384]{4,3,0,1,2:T(8,128)(2,1)S(1)} %fusion.1), channel_id=1, source_target_pairs={{0,4},{1,5},{2,6},{3,7},{4,0},{5,1},{6,2},{7,3},{8,12},{9,13},{10,... | collective-permute-start | bytes 1769480 | tf_op jit(solution)/shard_map/ppermute | solution.py:32
  237.7 14.5 %collective-permute-start.33 = (bf16[4,2,48,384]{3,2,0,1:T(8,128)(2,1)S(1)}, bf16[4,2,48,384]{3,2,0,1:T(8,128)(2,1)S(1)}, u32[]{:S(2)}, u32[]{:S(2)}) collective-permute-start(bf16[4,2,48,384]{3,2,0,1:T(8,128)(2,1)S(1)} %fusion.7), channel_id=1, source_target_pairs={{0,2},{1,3},{2,0},{3,1},{4,6},{5,7},{6,4},{7,5},{8,10},{9,11},{10,... | collective-permute-start | bytes 884744 | tf_op jit(solution)/shard_map/ppermute | solution.py:32
  246.9 9.3 %collective-permute-start.29 = (bf16[4,2,48,384]{3,2,0,1:T(8,128)(2,1)S(1)}, bf16[4,2,48,384]{3,2,0,1:T(8,128)(2,1)S(1)}, u32[]{:S(2)}, u32[]{:S(2)}) collective-permute-start(bf16[4,2,48,384]{3,2,0,1:T(8,128)(2,1)S(1)} %fusion.6), channel_id=1, source_target_pairs={{0,4},{1,5},{2,6},{3,7},{4,0},{5,1},{6,2},{7,3},{8,12},{9,13},{10,... | collective-permute-start | bytes 884744 | tf_op jit(solution)/shard_map/ppermute | solution.py:32
  252.3 10.6 %collective-permute-start.34 = (bf16[4,48,384]{2,1,0:T(8,128)(2,1)S(1)}, bf16[4,48,384]{2,1,0:T(8,128)(2,1)S(1)}, u32[]{:S(2)}, u32[]{:S(2)}) collective-permute-start(bf16[4,48,384]{2,1,0:T(8,128)(2,1)S(1)} %fusion.18), channel_id=1, source_target_pairs={{0,16},{1,17},{2,18},{3,19},{4,20},{5,21},{6,22},{7,23},{8,24},{9,... | collective-permute-start | bytes 442376 | tf_op jit(solution)/shard_map/ppermute | solution.py:32
  256.4 13.2 %collective-permute-start.22 = (bf16[4,2,48,384]{3,2,0,1:T(8,128)(2,1)S(1)}, bf16[4,2,48,384]{3,2,0,1:T(8,128)(2,1)S(1)}, u32[]{:S(2)}, u32[]{:S(2)}) collective-permute-start(bf16[4,2,48,384]{3,2,0,1:T(8,128)(2,1)S(1)} %fusion.5), channel_id=1, source_target_pairs={{0,8},{1,9},{2,10},{3,11},{4,12},{5,13},{6,14},{7,15},{8,0},{9,1},... | collective-permute-start | bytes 884744 | tf_op jit(solution)/shard_map/ppermute | solution.py:32
  258.1 12.0 %collective-permute-start.30 = (bf16[4,48,384]{2,1,0:T(8,128)(2,1)S(1)}, bf16[4,48,384]{2,1,0:T(8,128)(2,1)S(1)}, u32[]{:S(2)}, u32[]{:S(2)}) collective-permute-start(bf16[4,48,384]{2,1,0:T(8,128)(2,1)S(1)} %fusion.17), channel_id=1, source_target_pairs={{0,16},{1,17},{2,18},{3,19},{4,20},{5,21},{6,22},{7,23},{8,24},{9,... | collective-permute-start | bytes 442376 | tf_op jit(solution)/shard_map/ppermute | solution.py:32
  269.7 7.9 %collective-permute-start.23 = (bf16[4,48,384]{2,1,0:T(8,128)(2,1)S(1)}, bf16[4,48,384]{2,1,0:T(8,128)(2,1)S(1)}, u32[]{:S(2)}, u32[]{:S(2)}) collective-permute-start(bf16[4,48,384]{2,1,0:T(8,128)(2,1)S(1)} %fusion.16), channel_id=1, source_target_pairs={{0,16},{1,17},{2,18},{3,19},{4,20},{5,21},{6,22},{7,23},{8,24},{9,... | collective-permute-start | bytes 442376 | tf_op jit(solution)/shard_map/ppermute | solution.py:32
  277.8 3.4 %collective-permute-start.35 = (f32[12,24,384]{2,1,0:T(8,128)S(1)}, f32[12,24,384]{2,1,0:T(8,128)}, u32[]{:S(2)}, u32[]{:S(2)}) collective-permute-start(f32[12,24,384]{2,1,0:T(8,128)S(1)} %get-tuple-element.93), channel_id=1, source_target_pairs={{0,1},{1,0},{2,3},{3,2},{4,5},{5,4},{6,7},{7,6},{8,9},{9,8},{10,11... | collective-permute-start | bytes 1327112 | tf_op jit(solution)/shard_map/ppermute | solution.py:32
  279.6 10.5 %collective-permute-start.37 = (bf16[2,1,2,2,48,768]{5,4,3,2,1,0:T(8,128)(2,1)S(1)}, bf16[2,1,2,2,48,768]{5,4,3,2,1,0:T(8,128)(2,1)S(1)}, u32[]{:S(2)}, u32[]{:S(2)}) collective-permute-start(bf16[2,1,2,2,48,768]{5,4,3,2,1,0:T(8,128)(2,1)S(1)} %pad_maximum_fusion.1), channel_id=1, source_target_pairs={{0,2},{1,5},{2,0},{3,7},{4,6},{5,1},{6,4},{7,3},{8,10},{9,13},{10,... | collective-permute-start | bytes 1769480 | tf_op jit(solution)/shard_map/ppermute | solution.py:67
  285.3 20.5 %all-to-all-start.4 = ((bf16[32,24,384]{2,1,0:T(8,128)(2,1)}), bf16[32,24,384]{2,1,0:T(8,128)(2,1)S(1)}, u32[]{:S(2)}, u32[]{:S(2)}) async-start(bf16[32,24,384]{2,1,0:T(8,128)(2,1)} %bitcast.99), calls=%async_computation.4 | async-start | bytes 1179648 | tf_op jit(solution)/shard_map/all_to_all | solution.py:609
  305.7 2.7 collective-permute-start.39
  316.5 20.4 %all-to-all-start.5 = ((bf16[32,24,384]{2,1,0:T(8,128)(2,1)}), bf16[32,24,384]{2,1,0:T(8,128)(2,1)S(1)}, u32[]{:S(2)}, u32[]{:S(2)}) async-start(bf16[32,24,384]{2,1,0:T(8,128)(2,1)} %bitcast.101), calls=%async_computation.5 | async-start | bytes 1179648 | tf_op jit(solution)/shard_map/all_to_all | solution.py:609
  326.8 1.6 collective-permute-start.38
  (28 other events, 199.3 us)

commit v2 on v1

--- a/solution.py
+++ b/solution.py
@@ -681,9 +681,6 @@
     attn_ws, up_ws, down_ws = pairs
 
     place = jnp.stack([core, live_here.astype(jnp.int32)]).astype(jnp.int32)
-    lefts, qkv, attn_out, middle = run_attention_forward(
-        held_orders[0], place, latents[0], modulation, offsets, *attn_ws
-    )
     extra = max(0, block_count - devices // 2)
     assert extra % 2 == 0 and extra <= ADA
     main = block_count - extra
@@ -694,8 +691,18 @@
         spare_mine = lax.dynamic_index_in_dim(spare, core, 0, keepdims=False)
         spare_other = flip(lax.dynamic_index_in_dim(spare, 1 - core, 0, keepdims=False), 0)
         spare = joined(spare_mine, spare_other, core, 1).reshape(extra // 2, 2 * share, features)
-        lefts, spare = lax.optimization_barrier((lefts, spare))
+        modulation, spare = lax.optimization_barrier((modulation, spare))
         spare = gather_step(spare, spare_bits, spare_bits[0], myself)
+        for bit in spare_bits[1:-2]:
+            spare = gather_step(spare, spare_bits, bit, myself)
+        received = flip_by_core(spare, spare_bits[-2], spare_bits[-1])
+        near = jnp.stack([spare, received])
+        far = flip_by_core(near, spare_bits[-1], spare_bits[-2])
+        spare = corner_rows(near, far, spare_bits, myself)
+        spare = spare.reshape(extra // 2, features, features)
+    lefts, qkv, attn_out, middle = run_attention_forward(
+        held_orders[0], place, latents[0], modulation, offsets, *attn_ws
+    )
     lefts_other = flip(lefts, 0)
     output, hidden, mlp_keep, mlp_send, grad_middle, grad_attn, rows = run_mlp(
         held_orders[1:],
@@ -709,10 +716,6 @@
         up_ws,
         down_ws,
     )
-    if extra:
-        grad_attn, spare = lax.optimization_barrier((grad_attn, spare))
-        for bit in spare_bits[1:-2]:
-            spare = gather_step(spare, spare_bits, bit, myself)
     hidden_other = flip(hidden, 0)
     mlp_other = flip(mlp_send, 0)
 
@@ -741,13 +744,6 @@
     input_grad, attn_keep, attn_send, grad_offsets = run_attention_backward(
         held_orders[0], place, latents[0], modulation, *attn_ws, qkv, grad_middle, grad_attn, rows
     )
-    if extra:
-        attn_send, spare = lax.optimization_barrier((attn_send, spare))
-        received = flip_by_core(spare, spare_bits[-2], spare_bits[-1])
-        near = jnp.stack([spare, received])
-        far = flip_by_core(near, spare_bits[-1], spare_bits[-2])
-        spare = corner_rows(near, far, spare_bits, myself)
-        spare = spare.reshape(extra // 2, features, features)
     attn_other = flip(attn_send, 0)
     attn_halves = products(
         lefts, lefts_other, attn_keep, attn_other, lambda b: b // 3, lambda b: b, 4, orders[2]

time: 344 us -> 355 us (1.032)
  waiting for transfers between devices: 144 us -> 163 us
  starting transfers between devices: 71.8 us -> 61.2 us
    ppermute x38, waiting for transfers between devices: 100 us -> 133 us  [flip(): lax.ppermute(values, 'dp', [(i, i ^ 1 << bit) for i in range(devices)])]
    all_to_all x6, waiting for transfers between devices: 43.7 us -> 29.2 us  [all_to_all(): return lax.all_to_all(values, 'dp', split_axis=0, concat_axis=0, tiled=True)]
    ppermute x38, starting transfers between devices: 44.3 us -> 36.8 us  [flip(): lax.ppermute(values, 'dp', [(i, i ^ 1 << bit) for i in range(devices)])]
    unnamed x66 -> x68, local copies, waits for them, and re-layouts: 6.2 us -> 8.28 us
    select_n x26 -> x27, other arithmetic: 21 us -> 21.8 us  [joined(): jnp.where(taken == 1, jnp.stack([other, values], axis), jnp.stack([values...]
  transfers between devices with their start and end apart: 46 -> 46, of which waited for: 22 -> 23; matrix products, arithmetic and copies ran while one was open for 15% -> 15% of each run, Pallas kernels for 15% -> 15%
where the time goes in v2:
time: 355 us; the launch traced here: 350 us
  waiting for transfers between devices  163 us (46%)
  starting transfers between devices  61.2 us (17%)
  Pallas kernels  59.9 us (17%)
  other arithmetic  40.9 us (12%)
  local copies, waits for them, and re-layouts  17.7 us (5%)
  matrix products  4.4 us (1%)
    ppermute x38, waiting for transfers between devices, flip(): lax.ppermute(values, 'dp', [(i, i ^ 1 << bit) for i in range(devices)])  133 us
    ppermute x38, starting transfers between devices, flip(): lax.ppermute(values, 'dp', [(i, i ^ 1 << bit) for i in range(devices)])  36.8 us
    all_to_all x6, waiting for transfers between devices, all_to_all(): return lax.all_to_all(values, 'dp', split_axis=0, concat_axis=0, tiled=True)  29.2 us
    all_to_all x6, starting transfers between devices, all_to_all(): return lax.all_to_all(values, 'dp', split_axis=0, concat_axis=0, tiled=True)  22.9 us
    select_n x27, other arithmetic, joined(): jnp.where(taken == 1, jnp.stack([other, values], axis), jnp.stack([values...  21.8 us
    pallas_call x3, Pallas kernels, run_products(): pl.pallas_call(functools.partial(pair_products, chunk), name='pair_produc...  16.7 us
    pallas_call x1, Pallas kernels, run_mlp(): pl.pallas_call(functools.partial(mlp_both_ways, *mlp_orders), name='mlp_b...  11.2 us
    pallas_call x1, Pallas kernels, run_attention_backward(): pl.pallas_call(functools.partial(attention_backward, order), name='attent...  10.9 us
  transfers between devices with their start and end apart: 46, of which 23 were waited for; matrix products, arithmetic and copies ran while one was open for 15% of the time, Pallas kernels for 15%

profile of v2, /device:TPU:0, one launch (start us, length us, event | category | flops | bytes accessed | tf_op | source)
XLA Modules:
  0.0 350.3 jit_solution(14941862911058572543)
XLA Ops:
  4.8 3.9 %collective-permute-start.1 = (bf16[4,48,384]{2,1,0:T(8,128)(2,1)S(1)}, bf16[4,48,384]{2,1,0:T(8,128)(2,1)S(1)}, u32[]{:S(2)}, u32[]{:S(2)}) collective-permute-start(bf16[4,48,384]{2,1,0:T(8,128)(2,1)S(1)} %get-tuple-element.99), channel_id=1, source_target_pairs={{0,16},{1,17},{2,18},{3,19},{4,20},{5,21},{6,22},{7,23},{8,24},{9,... | collective-permute-start | bytes 442376 | tf_op jit(solution)/shard_map/ppermute | solution.py:32
  11.2 3.8 %all-to-all-start = ((bf16[32,2,552]{2,1,0:T(2,128)(2,1)}), bf16[32,2,552]{2,1,0:T(2,128)(2,1)S(1)}, u32[]{:S(2)}, u32[]{:S(2)}) async-start(bf16[32,2,552]{2,1,0:T(2,128)(2,1)} %reshape.2058), calls=%async_computation | async-start | bytes 163840 | tf_op jit(solution)/shard_map/all_to_all | solution.py:609
  15.1 7.6 %all-to-all-done = bf16[32,2,552]{2,1,0:T(2,128)(2,1)S(1)} async-done(((bf16[32,2,552]{2,1,0:T(2,128)(2,1)}), bf16[32,2,552]{2,1,0:T(2,128)(2,1)S(1)}, u32[]{:S(2)}, u32[]{:S(2)}) %all-to-all-start) | async-done | bytes 70688 | tf_op jit(solution)/shard_map/all_to_all | solution.py:609
  23.8 2.2 collective-permute-start.11
  26.9 8.7 %collective-permute-done.6 = bf16[4,48,384]{2,1,0:T(8,128)(2,1)S(1)} collective-permute-done((bf16[4,48,384]{2,1,0:T(8,128)(2,1)S(1)}, bf16[4,48,384]{2,1,0:T(8,128)(2,1)S(1)}, u32[]{:S(2)}, u32[]{:S(2)}) %collective-permute-start.6) | collective-permute-done | bytes 147488 | tf_op jit(solution)/shard_map/ppermute | solution.py:32
  40.6 3.8 %all-to-all-start.1 = ((f32[32,1,4608]{2,1,0:T(1,128)}), f32[32,1,4608]{2,1,0:T(1,128)}, u32[]{:S(2)}, u32[]{:S(2)}) async-start(f32[32,1,4608]{2,1,0:T(1,128)} %all_to_all.49), calls=%async_computation.1 | async-start | bytes 1179648 | tf_op jit(solution)/shard_map/all_to_all | solution.py:609
  44.5 1.9 collective-permute-start.7
  46.4 1.5 collective-permute-start.12
  48.8 14.1 %collective-permute-done.7 = bf16[2,4,48,384]{3,2,1,0:T(8,128)(2,1)S(1)} collective-permute-done((bf16[2,4,48,384]{3,2,1,0:T(8,128)(2,1)S(1)}, bf16[2,4,48,384]{3,2,1,0:T(8,128)(2,1)S(1)}, u32[]{:S(2)}, u32[]{:S(2)}) %collective-permute-start.7) | collective-permute-done | bytes 294944 | tf_op jit(solution)/shard_map/ppermute | solution.py:32
  63.0 1.6 collective-permute-start.8
  65.5 6.8 %collective-permute-done.3 = bf16[2,2,4,48,384]{4,3,2,1,0:T(8,128)(2,1)S(1)} collective-permute-done((bf16[2,2,4,48,384]{4,3,2,1,0:T(8,128)(2,1)S(1)}, bf16[2,2,4,48,384]{4,3,2,1,0:T(8,128)(2,1)S(1)}, u32[]{:S(2)}, u32[]{:S(2)}) %collective-permute-start.3) | collective-permute-done | bytes 589856 | tf_op jit(solution)/shard_map/ppermute | solution.py:32
  75.1 2.7 collective-permute-done.8
  89.0 15.7 %collective-permute-done.4 = bf16[2,2,2,4,48,384]{5,4,3,2,1,0:T(8,128)(2,1)} collective-permute-done((bf16[2,2,2,4,48,384]{5,4,3,2,1,0:T(8,128)(2,1)}, bf16[2,2,2,4,48,384]{5,4,3,2,1,0:T(8,128)(2,1)}, u32[]{:S(2)}, u32[]{:S(2)}) %collective-permute-start.4) | collective-permute-done | bytes 1179680 | tf_op jit(solution)/shard_map/ppermute | solution.py:32
  105.9 2.2 maximum_select_fusion
  108.6 3.7 %maximum_select_fusion.1 = bf16[2,2,2,2,4,48,384]{6,5,4,3,2,1,0:T(8,128)(2,1)} fusion(bf16[1,2,2,2,4,48,384]{6,5,4,3,2,1,0:T(8,128)(2,1)S(1)} %copy-done.7, bf16[1,2,2,2,4,48,384]{6,5,4,3,2,1,0:T(8,128)(2,1)} %bitcast.39, pred[]{:T(512)S(6)} %eq.21), kind=kLoop, calls=%fused_computation.1 | loop fusion | flops 3538944 | bytes 4718593 | tf_op jit(solution)/shard_map/jit(_where)/select_n | solution.py:40
  112.4 3.6 %maximum_select_fusion.2 = bf16[2,2,2,2,4,48,384]{6,5,4,3,2,1,0:T(8,128)(2,1)} fusion(bf16[1,2,2,2,4,48,384]{6,5,4,3,2,1,0:T(8,128)(2,1)S(1)} %copy-done.6, bf16[1,2,2,2,4,48,384]{6,5,4,3,2,1,0:T(8,128)(2,1)} %bitcast.43, pred[]{:T(512)S(6)} %eq.24), kind=kLoop, calls=%fused_computation.2 | loop fusion | flops 3538944 | bytes 4718593 | tf_op jit(solution)/shard_map/jit(_where)/select_n | solution.py:40
  121.9 6.4 %attention_forward.1 = (bf16[3,256,768]{2,1,0:T(8,128)(2,1)}, bf16[3,256,768]{2,1,0:T(8,128)(2,1)S(1)}, f32[256,768]{1,0:T(8,128)S(1)}, f32[256,768]{1,0:T(8,128)S(1)}) custom-call(s32[2]{0:T(128)S(1)} %pad_add_fusion.place_ref, bf16[256,768]{1,0:T(8,128)(2,1)S(1)} %bitcast.206, f32[6,768]{1,0:T(8,128)S(1)} %slice_add_fusion.mod_ref, ...), custom_call_target="tpu_custom_call" | custom-call | flops 2013265920 | bytes 8650752 | tf_op jit(solution)/shard_map/attention_forward/pallas_call | solution.py:410
  128.7 11.2 %mlp_both_ways.1 = (bf16[256,768]{1,0:T(8,128)(2,1)}, bf16[4,256,768]{2,1,0:T(8,128)(2,1)}, bf16[5,256,384]{2,1,0:T(8,128)(2,1)S(1)}, bf16[5,256,384]{2,1,0:T(8,...) custom-call(s32[2]{0:T(128)S(1)} %pad_add_fusion.place_ref, ...), custom_call_target="tpu_custom_call" | custom-call | flops 4831838208 | bytes 17301504 | tf_op jit(solution)/shard_map/mlp_both_ways/pallas_call | solution.py:435
  140.5 10.9 %attention_backward.1 = (f32[256,768]{1,0:T(8,128)}, bf16[4,256,384]{2,1,0:T(8,128)(2,1)S(1)}, bf16[4,256,384]{2,1,0:T(8,128)(2,1)}, f32[14,768]{1,0:T(8,128)S(1)}) custom-call(s32[2]{0:T(128)S(1)} %pad_add_fusion.place_ref, bf16[256,768]{1,0:T(8,128)(2,1)S(1)} %bitcast.207, f32[6,768]{1,0:T(8,128)S(1)} %slice_add_fusion.mod_ref, ...), custom_call_target="tpu_custom_call" | custom-call | flops 3221225472 | bytes 9437184 | tf_op jit(solution)/shard_map/attention_backward/pallas_call | solution.py:486
  153.0 5.5 %pair_products.5 = (f32[4,384,384]{2,1,0:T(8,128)}, bf16[4,384,384]{2,1,0:T(8,128)(2,1)}) custom-call(s32[1]{0:T(128)} %bitcast.71.mine_ref, bf16[3,256,768]{2,1,0:T(8,128)(2,1)} %get-tuple-element.48.lefts_ref.left_ref, bf16[3,256,768]{2,1,0:T(8,128)(2,1)} %collective-permute-done.23.left_other_ref, bf16[5,256,384]{2,1,0:T(8,128)(2,1)} %copy-done, ...), custom_call_target="tpu_custom_call" | custom-call | flops 1207959552 | bytes 7077888 | tf_op jit(solution)/shard_map/pair_products/pallas_call | solution.py:537
  162.0 4.6 %all-to-all-start.2 = ((bf16[32,2,2640]{2,1,0:T(2,128)(2,1)}), bf16[32,2,2640]{2,1,0:T(2,128)(2,1)S(1)}, u32[]{:S(2)}, u32[]{:S(2)}) async-start(bf16[32,2,2640]{2,1,0:T(2,128)(2,1)} %reshape.2060), calls=%async_computation.2 | async-start | bytes 688128 | tf_op jit(solution)/shard_map/all_to_all | solution.py:609
  166.6 2.7 collective-permute-start.34
  170.2 5.6 %pair_products.4 = (f32[4,384,384]{2,1,0:T(8,128)}, bf16[4,384,384]{2,1,0:T(8,128)(2,1)}) custom-call(s32[1]{0:T(128)} %bitcast.63.mine_ref, bf16[3,256,768]{2,1,0:T(8,128)(2,1)} %get-tuple-element.48.lefts_ref.left_ref, bf16[3,256,768]{2,1,0:T(8,128)(2,1)} %collective-permute-done.23.left_other_ref, bf16[4,256,384]{2,1,0:T(8,128)(2,1)} %copy-done.4, ...), custom_call_target="tpu_custom_call" | custom-call | flops 1207959552 | bytes 7077888 | tf_op jit(solution)/shard_map/pair_products/pallas_call | solution.py:537
  177.3 3.5 %collective-permute-done.34 = bf16[1,48,768]{2,1,0:T(8,128)(2,1)S(1)} collective-permute-done((bf16[1,48,768]{2,1,0:T(8,128)(2,1)S(1)}, bf16[1,48,768]{2,1,0:T(8,128)(2,1)S(1)}, u32[]{:S(2)}, u32[]{:S(2)}) %collective-permute-start.34) | collective-permute-done | bytes 73760 | tf_op jit(solution)/shard_map/ppermute | solution.py:32
  182.4 26.6 %collective-permute-done.35 = bf16[1,2,48,768]{3,2,1,0:T(8,128)(2,1)S(1)} collective-permute-done((bf16[1,2,48,768]{3,2,1,0:T(8,128)(2,1)S(1)}, bf16[1,2,48,768]{3,2,1,0:T(8,128)(2,1)S(1)}, u32[]{:S(2)}, u32[]{:S(2)}) %collective-permute-start.35) | collective-permute-done | bytes 147488 | tf_op jit(solution)/shard_map/ppermute | solution.py:32
  212.5 5.6 %pair_products.3 = (f32[4,384,384]{2,1,0:T(8,128)}, bf16[4,384,384]{2,1,0:T(8,128)(2,1)}) custom-call(s32[1]{0:T(128)} %bitcast.49.mine_ref, bf16[4,256,768]{2,1,0:T(8,128)(2,1)} %get-tuple-element.58.left_ref, bf16[4,256,768]{2,1,0:T(8,128)(2,1)} %collective-permute-done.17.left_other_ref, bf16[5,256,384]{2,1,0:T(8,128)(2,1)} %copy-done, ...), custom_call_target="tpu_custom_call" | custom-call | flops 1207959552 | bytes 7077888 | tf_op jit(solution)/shard_map/pair_products/pallas_call | solution.py:537
  219.6 1.8 fusion.8
  221.4 2.8 all-to-all-start.3
  224.2 1.7 convert_add_fusion
  226.0 1.9 collective-permute-start.30
  227.9 1.7 convert_add_fusion.1
  231.2 16.2 %collective-permute-done.19 = bf16[4,384,384]{2,1,0:T(8,128)(2,1)} collective-permute-done((bf16[4,384,384]{2,1,0:T(8,128)(2,1)}, bf16[4,384,384]{2,1,0:T(8,128)(2,1)}, u32[]{:S(2)}, u32[]{:S(2)}) %collective-permute-start.19) | collective-permute-done | bytes 1179680 | tf_op jit(solution)/shard_map/ppermute | solution.py:32
  247.4 1.6 convert_add_fusion.2
  251.3 8.6 %collective-permute-done.26 = bf16[4,2,2,48,384]{4,3,0,1,2:T(8,128)(2,1)S(1)} collective-permute-done((bf16[4,2,2,48,384]{4,3,0,1,2:T(8,128)(2,1)S(1)}, bf16[4,2,2,48,384]{4,3,0,1,2:T(8,128)(2,1)S(1)}, u32[]{:S(2)}, u32[]{:S(2)}) %collective-permute-start.26) | collective-permute-done | bytes 589856 | tf_op jit(solution)/shard_map/ppermute | solution.py:32
  260.9 3.9 %collective-permute-done.31 = bf16[4,2,48,384]{3,2,0,1:T(8,128)(2,1)S(1)} collective-permute-done((bf16[4,2,48,384]{3,2,0,1:T(8,128)(2,1)S(1)}, bf16[4,2,48,384]{3,2,0,1:T(8,128)(2,1)S(1)}, u32[]{:S(2)}, u32[]{:S(2)}) %collective-permute-start.31) | collective-permute-done | bytes 294944 | tf_op jit(solution)/shard_map/ppermute | solution.py:32
  265.0 3.4 collective-permute-done.27
  270.3 3.4 collective-permute-done.32
  273.7 7.3 %collective-permute-done.21 = bf16[4,2,48,384]{3,2,0,1:T(8,128)(2,1)S(1)} collective-permute-done((bf16[4,2,48,384]{3,2,0,1:T(8,128)(2,1)S(1)}, bf16[4,2,48,384]{3,2,0,1:T(8,128)(2,1)S(1)}, u32[]{:S(2)}, u32[]{:S(2)}) %collective-permute-start.21) | collective-permute-done | bytes 294944 | tf_op jit(solution)/shard_map/ppermute | solution.py:32
  281.2 7.9 %collective-permute-done.22 = bf16[4,48,384]{2,1,0:T(8,128)(2,1)S(1)} collective-permute-done((bf16[4,48,384]{2,1,0:T(8,128)(2,1)S(1)}, bf16[4,48,384]{2,1,0:T(8,128)(2,1)S(1)}, u32[]{:S(2)}, u32[]{:S(2)}) %collective-permute-start.22) | collective-permute-done | bytes 147488 | tf_op jit(solution)/shard_map/ppermute | solution.py:32
  292.5 1.8 fusion.36
  295.2 4.4 %all-to-all-start.4 = ((bf16[32,24,384]{2,1,0:T(8,128)(2,1)}), bf16[32,24,384]{2,1,0:T(8,128)(2,1)S(1)}, u32[]{:S(2)}, u32[]{:S(2)}) async-start(bf16[32,24,384]{2,1,0:T(8,128)(2,1)} %bitcast.104), calls=%async_computation.4 | async-start | bytes 1179648 | tf_op jit(solution)/shard_map/all_to_all | solution.py:609
  301.4 1.7 convert_multiply_fusion
  303.2 13.2 %all-to-all-done.4 = bf16[32,24,384]{2,1,0:T(8,128)(2,1)S(1)} async-done(((bf16[32,24,384]{2,1,0:T(8,128)(2,1)}), bf16[32,24,384]{2,1,0:T(8,128)(2,1)S(1)}, u32[]{:S(2)}, u32[]{:S(2)}) %all-to-all-start.4) | async-done | bytes 589856 | tf_op jit(solution)/shard_map/all_to_all | solution.py:609
  317.0 2.1 fusion.block_ref
  319.1 8.1 %orthogonalize_halves.1 = bf16[768,384]{1,0:T(8,128)(2,1)} custom-call(s32[2]{0:T(128)S(1)} %pad_add_fusion.place_ref, bf16[768,384]{1,0:T(8,128)(2,1)S(1)} %bitcast.204, bf16[768,384]{1,0:T(8,128)(2,1)S(1)} %collective-permute-done.39.other_ref), custom_call_target="tpu_custom_call" | custom-call | flops 5435817984 | bytes 2359296 | tf_op jit(solution)/shard_map/orthogonalize_halves/pallas_call | solution.py:583
  327.2 3.6 %all-to-all-start.5 = ((bf16[32,24,384]{2,1,0:T(8,128)(2,1)}), bf16[32,24,384]{2,1,0:T(8,128)(2,1)S(1)}, u32[]{:S(2)}, u32[]{:S(2)}) async-start(bf16[32,24,384]{2,1,0:T(8,128)(2,1)} %bitcast.106), calls=%async_computation.5 | async-start | bytes 1179648 | tf_op jit(solution)/shard_map/all_to_all | solution.py:609
  330.8 6.7 %orthogonalize_whole.1 = bf16[1,768,768]{2,1,0:T(8,128)(2,1)S(1)} custom-call(bf16[1,768,768]{2,1,0:T(8,128)(2,1)S(1)} %fusion.block_ref), custom_call_target="tpu_custom_call" | custom-call | flops 5435817984 | bytes 2359296 | tf_op jit(solution)/shard_map/orthogonalize_whole/pallas_call | solution.py:596
  339.2 8.4 %all-to-all-done.5 = bf16[32,24,384]{2,1,0:T(8,128)(2,1)S(1)} async-done(((bf16[32,24,384]{2,1,0:T(8,128)(2,1)}), bf16[32,24,384]{2,1,0:T(8,128)(2,1)S(1)}, u32[]{:S(2)}, u32[]{:S(2)}) %all-to-all-start.5) | async-done | bytes 589856 | tf_op jit(solution)/shard_map/all_to_all | solution.py:609
  (243 shorter events, 68.6 us)
Async XLA Ops:
  2.0 36.5 %copy-start.9 = (bf16[18,24,768]{2,1,0:T(8,128)(2,1)}, bf16[18,24,768]{2,1,0:T(8,128)(2,1)S(1)}, u32[]{:S(2)}) copy-start(bf16[18,24,768]{2,1,0:T(8,128)(2,1)S(1)} %convert_element_type.152) | copy-start | bytes 1990660
  2.2 1.7 collective-permute-start
  4.8 21.2 %collective-permute-start.1 = (bf16[4,48,384]{2,1,0:T(8,128)(2,1)S(1)}, bf16[4,48,384]{2,1,0:T(8,128)(2,1)S(1)}, u32[]{:S(2)}, u32[]{:S(2)}) collective-permute-start(bf16[4,48,384]{2,1,0:T(8,128)(2,1)S(1)} %get-tuple-element.99), channel_id=1, source_target_pairs={{0,16},{1,17},{2,18},{3,19},{4,20},{5,21},{6,22},{7,23},{8,24},{9,... | collective-permute-start | bytes 442376 | tf_op jit(solution)/shard_map/ppermute | solution.py:32
  11.2 11.4 %all-to-all-start = ((bf16[32,2,552]{2,1,0:T(2,128)(2,1)}), bf16[32,2,552]{2,1,0:T(2,128)(2,1)S(1)}, u32[]{:S(2)}, u32[]{:S(2)}) async-start(bf16[32,2,552]{2,1,0:T(2,128)(2,1)} %reshape.2058), calls=%async_computation | async-start | bytes 163840 | tf_op jit(solution)/shard_map/all_to_all | solution.py:609
  23.0 60.4 %copy-start.15 = (bf16[32,1,1104]{0,2,1:T(8,128)(2,1)}, bf16[32,1,1104]{0,2,1:T(8,128)(2,1)S(1)}, u32[]{:S(2)}) copy-start(bf16[32,1,1104]{0,2,1:T(8,128)(2,1)S(1)} %copy.94) | copy-start | bytes 211972
  23.1 12.5 %collective-permute-start.6 = (bf16[4,48,384]{2,1,0:T(8,128)(2,1)S(1)}, bf16[4,48,384]{2,1,0:T(8,128)(2,1)S(1)}, u32[]{:S(2)}, u32[]{:S(2)}) collective-permute-start(bf16[4,48,384]{2,1,0:T(8,128)(2,1)S(1)} %get-tuple-element.98), channel_id=1, source_target_pairs={{0,16},{1,17},{2,18},{3,19},{4,20},{5,21},{6,22},{7,23},{8,24},{9,... | collective-permute-start | bytes 442376 | tf_op jit(solution)/shard_map/ppermute | solution.py:32
  23.8 22.6 %collective-permute-start.11 = (bf16[4,48,384]{2,1,0:T(8,128)(2,1)}, bf16[4,48,384]{2,1,0:T(8,128)(2,1)S(1)}, u32[]{:S(2)}, u32[]{:S(2)}) collective-permute-start(bf16[4,48,384]{2,1,0:T(8,128)(2,1)} %get-tuple-element.97), channel_id=1, source_target_pairs={{0,16},{1,17},{2,18},{3,19},{4,20},{5,21},{6,22},{7,23},{8,24},{9,... | collective-permute-start | bytes 442376 | tf_op jit(solution)/shard_map/ppermute | solution.py:32
  37.1 10.9 %collective-permute-start.2 = (bf16[2,4,48,384]{3,2,1,0:T(8,128)(2,1)}, bf16[2,4,48,384]{3,2,1,0:T(8,128)(2,1)S(1)}, u32[]{:S(2)}, u32[]{:S(2)}) collective-permute-start(bf16[2,4,48,384]{3,2,1,0:T(8,128)(2,1)} %maximum_select_fusion.20), channel_id=1, source_target_pairs={{0,4},{1,5},{2,6},{3,7},{4,0},{5,1},{6,2},{7,3},{8,12},{9,13},{10,... | collective-permute-start | bytes 884744 | tf_op jit(solution)/shard_map/ppermute | solution.py:32
  40.6 47.2 %all-to-all-start.1 = ((f32[32,1,4608]{2,1,0:T(1,128)}), f32[32,1,4608]{2,1,0:T(1,128)}, u32[]{:S(2)}, u32[]{:S(2)}) async-start(f32[32,1,4608]{2,1,0:T(1,128)} %all_to_all.49), calls=%async_computation.1 | async-start | bytes 1179648 | tf_op jit(solution)/shard_map/all_to_all | solution.py:609
  44.5 18.4 %collective-permute-start.7 = (bf16[2,4,48,384]{3,2,1,0:T(8,128)(2,1)S(1)}, bf16[2,4,48,384]{3,2,1,0:T(8,128)(2,1)S(1)}, u32[]{:S(2)}, u32[]{:S(2)}) collective-permute-start(bf16[2,4,48,384]{3,2,1,0:T(8,128)(2,1)S(1)} %maximum_select_fusion.22), channel_id=1, source_target_pairs={{0,8},{1,9},{2,10},{3,11},{4,12},{5,13},{6,14},{7,15},{8,0},{9,1},... | collective-permute-start | bytes 884744 | tf_op jit(solution)/shard_map/ppermute | solution.py:32
  46.4 18.2 %collective-permute-start.12 = (bf16[2,4,48,384]{3,2,1,0:T(8,128)(2,1)S(1)}, bf16[2,4,48,384]{3,2,1,0:T(8,128)(2,1)S(1)}, u32[]{:S(2)}, u32[]{:S(2)}) collective-permute-start(bf16[2,4,48,384]{3,2,1,0:T(8,128)(2,1)S(1)} %maximum_select_fusion.24), channel_id=1, source_target_pairs={{0,2},{1,3},{2,0},{3,1},{4,6},{5,7},{6,4},{7,5},{8,10},{9,11},{10,... | collective-permute-start | bytes 884744 | tf_op jit(solution)/shard_map/ppermute | solution.py:32
  48.2 24.1 %collective-permute-start.3 = (bf16[2,2,4,48,384]{4,3,2,1,0:T(8,128)(2,1)S(1)}, bf16[2,2,4,48,384]{4,3,2,1,0:T(8,128)(2,1)S(1)}, u32[]{:S(2)}, u32[]{:S(2)}) collective-permute-start(bf16[2,2,4,48,384]{4,3,2,1,0:T(8,128)(2,1)S(1)} %maximum_select_fusion.11), channel_id=1, source_target_pairs={{0,2},{1,3},{2,0},{3,1},{4,6},{5,7},{6,4},{7,5},{8,10},{9,11},{10,... | collective-permute-start | bytes 1769480 | tf_op jit(solution)/shard_map/ppermute | solution.py:32
  63.0 14.8 %collective-permute-start.8 = (bf16[2,2,4,48,384]{4,3,2,1,0:T(8,128)(2,1)S(1)}, bf16[2,2,4,48,384]{4,3,2,1,0:T(8,128)(2,1)S(1)}, u32[]{:S(2)}, u32[]{:S(2)}) collective-permute-start(bf16[2,2,4,48,384]{4,3,2,1,0:T(8,128)(2,1)S(1)} %maximum_select_fusion.13), channel_id=1, source_target_pairs={{0,4},{1,5},{2,6},{3,7},{4,0},{5,1},{6,2},{7,3},{8,12},{9,13},{10,... | collective-permute-start | bytes 1769480 | tf_op jit(solution)/shard_map/ppermute | solution.py:32
  64.7 16.3 %collective-permute-start.13 = (bf16[2,2,4,48,384]{4,3,2,1,0:T(8,128)(2,1)S(1)}, bf16[2,2,4,48,384]{4,3,2,1,0:T(8,128)(2,1)S(1)}, u32[]{:S(2)}, u32[]{:S(2)}) collective-permute-start(bf16[2,2,4,48,384]{4,3,2,1,0:T(8,128)(2,1)S(1)} %maximum_select_fusion.15), channel_id=1, source_target_pairs={{0,8},{1,9},{2,10},{3,11},{4,12},{5,13},{6,14},{7,15},{8,0},{9,1},... | collective-permute-start | bytes 1769480 | tf_op jit(solution)/shard_map/ppermute | solution.py:32
  73.6 31.1 %collective-permute-start.4 = (bf16[2,2,2,4,48,384]{5,4,3,2,1,0:T(8,128)(2,1)}, bf16[2,2,2,4,48,384]{5,4,3,2,1,0:T(8,128)(2,1)}, u32[]{:S(2)}, u32[]{:S(2)}) collective-permute-start(bf16[2,2,2,4,48,384]{5,4,3,2,1,0:T(8,128)(2,1)} %maximum_select_fusion.3), channel_id=1, source_target_pairs={{0,8},{1,9},{2,10},{3,11},{4,12},{5,13},{6,14},{7,15},{8,0},{9,1},... | collective-permute-start | bytes 3538952 | tf_op jit(solution)/shard_map/ppermute | solution.py:32
  79.0 26.9 %collective-permute-start.9 = (bf16[2,2,2,4,48,384]{5,4,3,2,1,0:T(8,128)(2,1)}, bf16[2,2,2,4,48,384]{5,4,3,2,1,0:T(8,128)(2,1)}, u32[]{:S(2)}, u32[]{:S(2)}) collective-permute-start(bf16[2,2,2,4,48,384]{5,4,3,2,1,0:T(8,128)(2,1)} %maximum_select_fusion.4), channel_id=1, source_target_pairs={{0,2},{1,3},{2,0},{3,1},{4,6},{5,7},{6,4},{7,5},{8,10},{9,11},{10,... | collective-permute-start | bytes 3538952 | tf_op jit(solution)/shard_map/ppermute | solution.py:32
  82.3 26.3 %collective-permute-start.14 = (bf16[2,2,2,4,48,384]{5,4,3,2,1,0:T(8,128)(2,1)}, bf16[2,2,2,4,48,384]{5,4,3,2,1,0:T(8,128)(2,1)}, u32[]{:S(2)}, u32[]{:S(2)}) collective-permute-start(bf16[2,2,2,4,48,384]{5,4,3,2,1,0:T(8,128)(2,1)} %maximum_select_fusion.6), channel_id=1, source_target_pairs={{0,4},{1,5},{2,6},{3,7},{4,0},{5,1},{6,2},{7,3},{8,12},{9,13},{10,... | collective-permute-start | bytes 3538952 | tf_op jit(solution)/shard_map/ppermute | solution.py:32
  108.1 13.7 %collective-permute-start.10 = (bf16[16,4,48,384]{3,2,1,0:T(8,128)(2,1)S(1)}, bf16[16,4,48,384]{3,2,1,0:T(8,128)(2,1)}, u32[]{:S(2)}, u32[]{:S(2)}) collective-permute-start(bf16[16,4,48,384]{3,2,1,0:T(8,128)(2,1)S(1)} %bitcast.200), channel_id=1, source_target_pairs={{0,1},{1,0},{2,3},{3,2},{4,5},{5,4},{6,7},{7,6},{8,9},{9,8},{10,11... | collective-permute-start | bytes 7077896 | tf_op jit(solution)/shard_map/ppermute | solution.py:32
  112.2 16.4 %collective-permute-start.15 = (bf16[16,4,48,384]{3,2,1,0:T(8,128)(2,1)}, bf16[16,4,48,384]{3,2,1,0:T(8,128)(2,1)}, u32[]{:S(2)}, u32[]{:S(2)}) collective-permute-start(bf16[16,4,48,384]{3,2,1,0:T(8,128)(2,1)} %bitcast.42.up_ref), channel_id=1, source_target_pairs={{0,1},{1,0},{2,3},{3,2},{4,5},{5,4},{6,7},{7,6},{8,9},{9,8},{10,11... | collective-permute-start | bytes 7077896 | tf_op jit(solution)/shard_map/ppermute | solution.py:32
  116.0 12.7 %collective-permute-start.16 = (bf16[16,4,48,384]{3,2,1,0:T(8,128)(2,1)}, bf16[16,4,48,384]{3,2,1,0:T(8,128)(2,1)}, u32[]{:S(2)}, u32[]{:S(2)}) collective-permute-start(bf16[16,4,48,384]{3,2,1,0:T(8,128)(2,1)} %bitcast.46.down_ref), channel_id=1, source_target_pairs={{0,1},{1,0},{2,3},{3,2},{4,5},{5,4},{6,7},{7,6},{8,9},{9,8},{10,11... | collective-permute-start | bytes 7077896 | tf_op jit(solution)/shard_map/ppermute | solution.py:32
  117.9 3.0 collective-permute-start.5
  128.3 24.7 %collective-permute-start.23 = (bf16[3,256,768]{2,1,0:T(8,128)(2,1)}, bf16[3,256,768]{2,1,0:T(8,128)(2,1)}, u32[]{:S(2)}, u32[]{:S(2)}) collective-permute-start(bf16[3,256,768]{2,1,0:T(8,128)(2,1)} %get-tuple-element.48.lefts_ref.left_ref), channel_id=1, source_target_pairs={{0,1},{1,0},{2,3},{3,2},{4,5},{5,4},{6,7},{7,6},{8,9},{9,8},{10,11... | collective-permute-start | bytes 3538952 | tf_op jit(solution)/shard_map/ppermute | solution.py:32
  139.9 13.0 %collective-permute-start.18 = (bf16[5,256,384]{2,1,0:T(8,128)(2,1)S(1)}, bf16[5,256,384]{2,1,0:T(8,128)(2,1)}, u32[]{:S(2)}, u32[]{:S(2)}) collective-permute-start(bf16[5,256,384]{2,1,0:T(8,128)(2,1)S(1)} %get-tuple-element.60), channel_id=1, source_target_pairs={{0,1},{1,0},{2,3},{3,2},{4,5},{5,4},{6,7},{7,6},{8,9},{9,8},{10,11... | collective-permute-start | bytes 2949128 | tf_op jit(solution)/shard_map/ppermute | solution.py:32
  140.1 72.0 %collective-permute-start.17 = (bf16[4,256,768]{2,1,0:T(8,128)(2,1)}, bf16[4,256,768]{2,1,0:T(8,128)(2,1)}, u32[]{:S(2)}, u32[]{:S(2)}) collective-permute-start(bf16[4,256,768]{2,1,0:T(8,128)(2,1)} %get-tuple-element.58.left_ref), channel_id=1, source_target_pairs={{0,1},{1,0},{2,3},{3,2},{4,5},{5,4},{6,7},{7,6},{8,9},{9,8},{10,11... | collective-permute-start | bytes 4718600 | tf_op jit(solution)/shard_map/ppermute | solution.py:32
  152.3 17.0 %collective-permute-start.24 = (bf16[4,256,384]{2,1,0:T(8,128)(2,1)}, bf16[4,256,384]{2,1,0:T(8,128)(2,1)S(1)}, u32[]{:S(2)}, u32[]{:S(2)}) collective-permute-start(bf16[4,256,384]{2,1,0:T(8,128)(2,1)} %get-tuple-element.68), channel_id=1, source_target_pairs={{0,1},{1,0},{2,3},{3,2},{4,5},{5,4},{6,7},{7,6},{8,9},{9,8},{10,11... | collective-permute-start | bytes 2359304 | tf_op jit(solution)/shard_map/ppermute | solution.py:32
  158.4 65.8 %collective-permute-start.29 = (bf16[4,384,384]{2,1,0:T(8,128)(2,1)}, bf16[4,384,384]{2,1,0:T(8,128)(2,1)}, u32[]{:S(2)}, u32[]{:S(2)}) collective-permute-start(bf16[4,384,384]{2,1,0:T(8,128)(2,1)} %get-tuple-element.72), channel_id=1, source_target_pairs={{0,4},{1,5},{2,6},{3,7},{4,0},{5,1},{6,2},{7,3},{8,12},{9,13},{10,... | collective-permute-start | bytes 3538952 | tf_op jit(solution)/shard_map/ppermute | solution.py:32
  162.0 49.1 %all-to-all-start.2 = ((bf16[32,2,2640]{2,1,0:T(2,128)(2,1)}), bf16[32,2,2640]{2,1,0:T(2,128)(2,1)S(1)}, u32[]{:S(2)}, u32[]{:S(2)}) async-start(bf16[32,2,2640]{2,1,0:T(2,128)(2,1)} %reshape.2060), calls=%async_computation.2 | async-start | bytes 688128 | tf_op jit(solution)/shard_map/all_to_all | solution.py:609
  166.6 14.3 %collective-permute-start.34 = (bf16[1,48,768]{2,1,0:T(8,128)(2,1)S(1)}, bf16[1,48,768]{2,1,0:T(8,128)(2,1)S(1)}, u32[]{:S(2)}, u32[]{:S(2)}) collective-permute-start(bf16[1,48,768]{2,1,0:T(8,128)(2,1)S(1)} %bitcast.254), channel_id=1, source_target_pairs={{0,16},{1,17},{2,18},{3,19},{4,20},{5,21},{6,22},{7,23},{8,24},{9,... | collective-permute-start | bytes 221192 | tf_op jit(solution)/shard_map/ppermute | solution.py:32
  175.8 52.1 %collective-permute-start.25 = (bf16[4,384,384]{2,1,0:T(8,128)(2,1)}, bf16[4,384,384]{2,1,0:T(8,128)(2,1)}, u32[]{:S(2)}, u32[]{:S(2)}) collective-permute-start(bf16[4,384,384]{2,1,0:T(8,128)(2,1)} %get-tuple-element.70), channel_id=1, source_target_pairs={{0,8},{1,9},{2,10},{3,11},{4,12},{5,13},{6,14},{7,15},{8,0},{9,1},... | collective-permute-start | bytes 3538952 | tf_op jit(solution)/shard_map/ppermute | solution.py:32
  180.9 28.2 %collective-permute-start.35 = (bf16[1,2,48,768]{3,2,1,0:T(8,128)(2,1)S(1)}, bf16[1,2,48,768]{3,2,1,0:T(8,128)(2,1)S(1)}, u32[]{:S(2)}, u32[]{:S(2)}) collective-permute-start(bf16[1,2,48,768]{3,2,1,0:T(8,128)(2,1)S(1)} %maximum_select_fusion.29), channel_id=1, source_target_pairs={{0,8},{1,9},{2,10},{3,11},{4,12},{5,13},{6,14},{7,15},{8,0},{9,1},... | collective-permute-start | bytes 442376 | tf_op jit(solution)/shard_map/ppermute | solution.py:32
  209.8 80.4 %collective-permute-start.36 = (bf16[1,2,2,48,768]{4,3,1,2,0:T(8,128)(2,1)}, bf16[1,2,2,48,768]{4,3,1,2,0:T(8,128)(2,1)}, u32[]{:S(2)}, u32[]{:S(2)}) collective-permute-start(bf16[1,2,2,48,768]{4,3,1,2,0:T(8,128)(2,1)} %maximum_select_fusion.27), channel_id=1, source_target_pairs={{0,4},{1,3},{2,6},{3,1},{4,0},{5,7},{6,2},{7,5},{8,12},{9,11},{10,... | collective-permute-start | bytes 884744 | tf_op jit(solution)/shard_map/ppermute | solution.py:67
  218.1 29.3 %collective-permute-start.19 = (bf16[4,384,384]{2,1,0:T(8,128)(2,1)}, bf16[4,384,384]{2,1,0:T(8,128)(2,1)}, u32[]{:S(2)}, u32[]{:S(2)}) collective-permute-start(bf16[4,384,384]{2,1,0:T(8,128)(2,1)} %get-tuple-element.62), channel_id=1, source_target_pairs={{0,2},{1,3},{2,0},{3,1},{4,6},{5,7},{6,4},{7,5},{8,10},{9,11},{10,... | collective-permute-start | bytes 3538952 | tf_op jit(solution)/shard_map/ppermute | solution.py:32
  221.4 59.8 %all-to-all-start.3 = ((f32[32,1,24]{2,1,0:T(1,128)}), f32[32,1,24]{2,1,0:T(1,128)S(1)}, u32[]{:S(2)}, u32[]{:S(2)}) async-start(f32[32,1,24]{2,1,0:T(1,128)} %bitcast.114), calls=%async_computation.3 | async-start | bytes 32768 | tf_op jit(solution)/shard_map/all_to_all | solution.py:609
  226.0 23.7 %collective-permute-start.30 = (bf16[4,2,2,48,384]{4,3,0,1,2:T(8,128)(2,1)S(1)}, bf16[4,2,2,48,384]{4,3,0,1,2:T(8,128)(2,1)S(1)}, u32[]{:S(2)}, u32[]{:S(2)}) collective-permute-start(bf16[4,2,2,48,384]{4,3,0,1,2:T(8,128)(2,1)S(1)} %fusion.3), channel_id=1, source_target_pairs={{0,8},{1,9},{2,10},{3,11},{4,12},{5,13},{6,14},{7,15},{8,0},{9,1},... | collective-permute-start | bytes 1769480 | tf_op jit(solution)/shard_map/ppermute | solution.py:32
  229.7 30.3 %collective-permute-start.26 = (bf16[4,2,2,48,384]{4,3,0,1,2:T(8,128)(2,1)S(1)}, bf16[4,2,2,48,384]{4,3,0,1,2:T(8,128)(2,1)S(1)}, u32[]{:S(2)}, u32[]{:S(2)}) collective-permute-start(bf16[4,2,2,48,384]{4,3,0,1,2:T(8,128)(2,1)S(1)} %fusion.2), channel_id=1, source_target_pairs={{0,2},{1,3},{2,0},{3,1},{4,6},{5,7},{6,4},{7,5},{8,10},{9,11},{10,... | collective-permute-start | bytes 1769480 | tf_op jit(solution)/shard_map/ppermute | solution.py:32
  249.0 19.4 %collective-permute-start.20 = (bf16[4,2,2,48,384]{4,3,0,1,2:T(8,128)(2,1)S(1)}, bf16[4,2,2,48,384]{4,3,0,1,2:T(8,128)(2,1)S(1)}, u32[]{:S(2)}, u32[]{:S(2)}) collective-permute-start(bf16[4,2,2,48,384]{4,3,0,1,2:T(8,128)(2,1)S(1)} %fusion.1), channel_id=1, source_target_pairs={{0,4},{1,5},{2,6},{3,7},{4,0},{5,1},{6,2},{7,3},{8,12},{9,13},{10,... | collective-permute-start | bytes 1769480 | tf_op jit(solution)/shard_map/ppermute | solution.py:32
  249.9 14.9 %collective-permute-start.31 = (bf16[4,2,48,384]{3,2,0,1:T(8,128)(2,1)S(1)}, bf16[4,2,48,384]{3,2,0,1:T(8,128)(2,1)S(1)}, u32[]{:S(2)}, u32[]{:S(2)}) collective-permute-start(bf16[4,2,48,384]{3,2,0,1:T(8,128)(2,1)S(1)} %fusion.7), channel_id=1, source_target_pairs={{0,2},{1,3},{2,0},{3,1},{4,6},{5,7},{6,4},{7,5},{8,10},{9,11},{10,... | collective-permute-start | bytes 884744 | tf_op jit(solution)/shard_map/ppermute | solution.py:32
  260.1 8.2 %collective-permute-start.27 = (bf16[4,2,48,384]{3,2,0,1:T(8,128)(2,1)S(1)}, bf16[4,2,48,384]{3,2,0,1:T(8,128)(2,1)S(1)}, u32[]{:S(2)}, u32[]{:S(2)}) collective-permute-start(bf16[4,2,48,384]{3,2,0,1:T(8,128)(2,1)S(1)} %fusion.6), channel_id=1, source_target_pairs={{0,4},{1,5},{2,6},{3,7},{4,0},{5,1},{6,2},{7,3},{8,12},{9,13},{10,... | collective-permute-start | bytes 884744 | tf_op jit(solution)/shard_map/ppermute | solution.py:32
  264.9 8.8 %collective-permute-start.32 = (bf16[4,48,384]{2,1,0:T(8,128)(2,1)S(1)}, bf16[4,48,384]{2,1,0:T(8,128)(2,1)S(1)}, u32[]{:S(2)}, u32[]{:S(2)}) collective-permute-start(bf16[4,48,384]{2,1,0:T(8,128)(2,1)S(1)} %fusion.19), channel_id=1, source_target_pairs={{0,16},{1,17},{2,18},{3,19},{4,20},{5,21},{6,22},{7,23},{8,24},{9,... | collective-permute-start | bytes 442376 | tf_op jit(solution)/shard_map/ppermute | solution.py:32
  268.7 12.3 %collective-permute-start.21 = (bf16[4,2,48,384]{3,2,0,1:T(8,128)(2,1)S(1)}, bf16[4,2,48,384]{3,2,0,1:T(8,128)(2,1)S(1)}, u32[]{:S(2)}, u32[]{:S(2)}) collective-permute-start(bf16[4,2,48,384]{3,2,0,1:T(8,128)(2,1)S(1)} %fusion.5), channel_id=1, source_target_pairs={{0,8},{1,9},{2,10},{3,11},{4,12},{5,13},{6,14},{7,15},{8,0},{9,1},... | collective-permute-start | bytes 884744 | tf_op jit(solution)/shard_map/ppermute | solution.py:32
  268.8 12.4 %collective-permute-start.28 = (bf16[4,48,384]{2,1,0:T(8,128)(2,1)S(1)}, bf16[4,48,384]{2,1,0:T(8,128)(2,1)S(1)}, u32[]{:S(2)}, u32[]{:S(2)}) collective-permute-start(bf16[4,48,384]{2,1,0:T(8,128)(2,1)S(1)} %fusion.18), channel_id=1, source_target_pairs={{0,16},{1,17},{2,18},{3,19},{4,20},{5,21},{6,22},{7,23},{8,24},{9,... | collective-permute-start | bytes 442376 | tf_op jit(solution)/shard_map/ppermute | solution.py:32
  281.1 8.0 %collective-permute-start.22 = (bf16[4,48,384]{2,1,0:T(8,128)(2,1)S(1)}, bf16[4,48,384]{2,1,0:T(8,128)(2,1)S(1)}, u32[]{:S(2)}, u32[]{:S(2)}) collective-permute-start(bf16[4,48,384]{2,1,0:T(8,128)(2,1)S(1)} %fusion.17), channel_id=1, source_target_pairs={{0,16},{1,17},{2,18},{3,19},{4,20},{5,21},{6,22},{7,23},{8,24},{9,... | collective-permute-start | bytes 442376 | tf_op jit(solution)/shard_map/ppermute | solution.py:32
  289.3 2.2 collective-permute-start.33
  291.2 9.9 %collective-permute-start.37 = (bf16[2,1,2,2,48,768]{5,4,2,3,1,0:T(8,128)(2,1)S(1)}, bf16[2,1,2,2,48,768]{5,4,2,3,1,0:T(8,128)(2,1)S(1)}, u32[]{:S(2)}, u32[]{:S(2)}) collective-permute-start(bf16[2,1,2,2,48,768]{5,4,2,3,1,0:T(8,128)(2,1)S(1)} %pad_maximum_fusion.1), channel_id=1, source_target_pairs={{0,2},{1,5},{2,0},{3,7},{4,6},{5,1},{6,4},{7,3},{8,10},{9,13},{10,... | collective-permute-start | bytes 1769480 | tf_op jit(solution)/shard_map/ppermute | solution.py:67
  295.2 21.2 %all-to-all-start.4 = ((bf16[32,24,384]{2,1,0:T(8,128)(2,1)}), bf16[32,24,384]{2,1,0:T(8,128)(2,1)S(1)}, u32[]{:S(2)}, u32[]{:S(2)}) async-start(bf16[32,24,384]{2,1,0:T(8,128)(2,1)} %bitcast.104), calls=%async_computation.4 | async-start | bytes 1179648 | tf_op jit(solution)/shard_map/all_to_all | solution.py:609
  316.4 2.7 collective-permute-start.39
  327.2 20.4 %all-to-all-start.5 = ((bf16[32,24,384]{2,1,0:T(8,128)(2,1)}), bf16[32,24,384]{2,1,0:T(8,128)(2,1)S(1)}, u32[]{:S(2)}, u32[]{:S(2)}) async-start(bf16[32,24,384]{2,1,0:T(8,128)(2,1)} %bitcast.106), calls=%async_computation.5 | async-start | bytes 1179648 | tf_op jit(solution)/shard_map/all_to_all | solution.py:609
  337.5 1.7 collective-permute-start.38
  (29 other events, 180.6 us)

commit v3 on v2

--- a/solution.py
+++ b/solution.py
@@ -190,16 +190,18 @@
     normed, _ = layer_norm(stream)
     attn_input = (normed * (1.0 + mod_ref[1:2]) + mod_ref[0:1]).astype(jnp.bfloat16)
     lefts_ref[0] = attn_input
-    qkv_ref[0] = (contract(attn_input, whole_weight(mine_ref, other_ref, 0, core, order), 1, 0) + offsets_ref[6:7]).astype(
-        jnp.bfloat16
-    )
-    qkv_ref[1] = contract(attn_input, whole_weight(mine_ref, other_ref, 1, core, order), 1, 0).astype(jnp.bfloat16)
-    qkv_ref[2] = (contract(attn_input, whole_weight(mine_ref, other_ref, 2, core, order), 1, 0) + offsets_ref[7:8]).astype(
-        jnp.bfloat16
-    )
+
+    @pl.loop(0, 3)
+    def _(index):
+        row = jnp.where(index == 0, offsets_ref[6:7], offsets_ref[7:8])
+        values = contract(attn_input, whole_weight(mine_ref, other_ref, index, core, order), 1, 0)
+        qkv_ref[index] = (values + jnp.where(index == 1, 0.0, row)).astype(jnp.bfloat16)
+
     first = lax.broadcasted_iota(jnp.int32, (seqlen, 2 * width), 1) < width
-    for pair in range(HEADS // 2):
-        columns = slice(2 * width * pair, 2 * width * (pair + 1))
+
+    @pl.loop(0, HEADS // 2)
+    def _(pair):
+        columns = pl.ds(pl.multiple_of(2 * width * pair, 2 * width), 2 * width)
         query, keys, values = qkv_ref[0, :, columns], qkv_ref[1, :, columns], qkv_ref[2, :, columns]
         halves = []
         for mask in (first, jnp.logical_not(first)):
@@ -208,6 +210,7 @@
             probs = jnp.exp(scores - log_total).astype(jnp.bfloat16)
             halves.append(contract(probs, values, 1, 0))
         lefts_ref[1, :, columns] = jnp.where(first, *halves).astype(jnp.bfloat16)
+
     attn_out = contract(lefts_ref[1], whole_weight(mine_ref, other_ref, 3, core, order), 1, 0) + offsets_ref[8:9]
     attn_ref[...] = attn_out
     middle = stream + mod_ref[2:3] * attn_out
@@ -329,8 +332,10 @@
         grad_attn, whole_weight(mine_ref, other_ref, 3, core, order), 1, 1
     ).astype(jnp.bfloat16)
     first = lax.broadcasted_iota(jnp.int32, (seqlen, 2 * width), 1) < width
-    for pair in range(HEADS // 2):
-        columns = slice(2 * width * pair, 2 * width * (pair + 1))
+
+    @pl.loop(0, HEADS // 2)
+    def _(pair):
+        columns = pl.ds(pl.multiple_of(2 * width * pair, 2 * width), 2 * width)
         query, keys, values = qkv_ref[0, :, columns], qkv_ref[1, :, columns], qkv_ref[2, :, columns]
         upstream = context_ref[:, columns]
         parts = []
@@ -357,11 +362,18 @@
             if index != 1:
                 row = 6 if index == 0 else 7
                 rows_ref[row : row + 1, columns] = column_sum(merged)
-    grad_in = jnp.zeros((seqlen, features), jnp.float32)
-    for index in range(3):
+
+    grad_source_ref[...] = jnp.zeros_like(grad_source_ref)
+
+    @pl.loop(0, 3)
+    def _(index):
         grads = grads_ref[index]
         keep_ref[index], send_ref[index] = split_columns(grads, core)
-        grad_in += contract(grads, whole_weight(mine_ref, other_ref, index, core, order), 1, 1)
+        grad_source_ref[...] += contract(
+            grads, whole_weight(mine_ref, other_ref, index, core, order), 1, 1
+        )
+
+    grad_in = grad_source_ref[...]
     normed, inverse = layer_norm(source_ref[...].astype(jnp.float32))
     rows_ref[0:1] = column_sum(grad_in)
     rows_ref[1:2] = column_sum(grad_in * normed)
@@ -375,15 +387,25 @@
 def pair_products(
     chunk, mine_ref, left_ref, left_other_ref, right_ref, right_other_ref, keep_ref, send_ref
 ):
-    total = contract(left_ref[0], right_ref[0], 0, 0) + contract(
-        left_other_ref[0], right_other_ref[0], 0, 0
-    )
-    for start in range(0, total.shape[0] // 2, chunk):
-        low = total[2 * start : 2 * start + chunk]
-        high = total[2 * start + chunk : 2 * start + 2 * chunk]
-        mine = mine_ref[0] == 1
-        keep_ref[0, start : start + chunk] = jnp.where(mine, high, low)
-        send_ref[0, start : start + chunk] = jnp.where(mine, low, high).astype(jnp.bfloat16)
+    features = left_ref.shape[-1]
+    part = features // 2
+    if part % (2 * chunk) or part % 128:
+        part = features
+    mine = mine_ref[0] == 1
+
+    @pl.loop(0, features // part)
+    def _(index):
+        columns = pl.ds(pl.multiple_of(index * part, 128), part)
+        total = contract(left_ref[0, :, columns], right_ref[0], 0, 0) + contract(
+            left_other_ref[0, :, columns], right_other_ref[0], 0, 0
+        )
+        base = pl.multiple_of(index * (part // 2), 16)
+        for start in range(0, part // 2, chunk):
+            low = total[2 * start : 2 * start + chunk]
+            high = total[2 * start + chunk : 2 * start + 2 * chunk]
+            rows = pl.ds(base + start, chunk)
+            keep_ref[0, rows] = jnp.where(mine, high, low)
+            send_ref[0, rows] = jnp.where(mine, low, high).astype(jnp.bfloat16)
 
 
 def plain_products(left_ref, left_other_ref, right_ref, right_other_ref, out_ref):
@@ -548,29 +570,31 @@
     )(mine[None], lefts, lefts_other, rights, rights_other)
 
 
-def muon_steps(block):
+def muon_steps(block, scaled_ref):
     values = block.astype(jnp.float32)
-    scaled = (values / (jnp.sqrt(jnp.sum(values * values)) + 1e-07)).astype(jnp.bfloat16)
-    for _ in range(NS_ITERS):
+    scaled_ref[...] = (values / (jnp.sqrt(jnp.sum(values * values)) + 1e-07)).astype(jnp.bfloat16)
+
+    @pl.loop(0, NS_ITERS)
+    def _(iteration):
+        scaled = scaled_ref[...]
         gram = contract(scaled, scaled, 1, 1).astype(jnp.bfloat16)
         square = contract(gram, gram, 1, 0)
         mixed = (COEF_SECOND * gram.astype(jnp.float32) + COEF_THIRD * square).astype(jnp.bfloat16)
-        scaled = (
+        scaled_ref[...] = (
             COEF_FIRST * scaled.astype(jnp.float32) + contract(mixed, scaled, 1, 0)
         ).astype(jnp.bfloat16)
-    return scaled
-
-
-def orthogonalize_halves(place_ref, mine_ref, other_ref, out_ref):
+
+
+def orthogonalize_halves(place_ref, mine_ref, other_ref, out_ref, scaled_ref):
     core = place_ref[0]
     mine, other = mine_ref[...], other_ref[...]
     low, high = jnp.where(core == 1, other, mine), jnp.where(core == 1, mine, other)
-    scaled = muon_steps(jnp.concatenate([low, high], axis=1))
-    out_ref[...] = split_columns(scaled, core)[0]
+    muon_steps(jnp.concatenate([low, high], axis=1), scaled_ref)
+    out_ref[...] = split_columns(scaled_ref[...], core)[0]
 
 
 def orthogonalize_whole(block_ref, out_ref):
-    out_ref[0] = muon_steps(block_ref[0])
+    muon_steps(block_ref[0], out_ref.at[0])
 
 
 def muon_cost(count, rows):
@@ -586,6 +610,7 @@
         out_shape=struct(mine.shape, mine.dtype),
         in_specs=[SMEM, VMEM, VMEM],
         out_specs=VMEM,
+        scratch_shapes=[pltpu.VMEM((mine.shape[0], 2 * mine.shape[1]), mine.dtype)],
         compiler_params=pltpu.CompilerParams(vmem_limit_bytes=24 << 20),
         cost_estimate=muon_cost(1, mine.shape[0]),
     )(place, mine, other)
@@ -689,7 +714,8 @@
     if extra:
         spare = momenta[:extra].astype(jnp.bfloat16).reshape(2, extra // 2, share, features)
         spare_mine = lax.dynamic_index_in_dim(spare, core, 0, keepdims=False)
-        spare_other = flip(lax.dynamic_index_in_dim(spare, 1 - core, 0, keepdims=False), 0)
+        spare_other = lax.dynamic_index_in_dim(spare, 1 - core, 0, keepdims=False)
+        spare_other = flip(spare_other, 0)
         spare = joined(spare_mine, spare_other, core, 1).reshape(extra // 2, 2 * share, features)
         modulation, spare = lax.optimization_barrier((modulation, spare))
         spare = gather_step(spare, spare_bits, spare_bits[0], myself)

time: 355 us -> 361 us (1.017)
  Pallas kernels: 59.9 us -> 69 us
  transfers between devices with their start and end apart: 46 -> 46, of which waited for: 23 -> 23; matrix products, arithmetic and copies ran while one was open for 15% -> 15% of each run, Pallas kernels for 15% -> 17%
where the time goes in v3:
time: 361 us; the launch traced here: 359 us
  waiting for transfers between devices  164 us (45%)
  Pallas kernels  69 us (19%)
  starting transfers between devices  60.5 us (17%)
  other arithmetic  40.9 us (11%)
  local copies, waits for them, and re-layouts  17.7 us (5%)
  matrix products  4.39 us (1%)
    ppermute x38, waiting for transfers between devices, flip(): lax.ppermute(values, 'dp', [(i, i ^ 1 << bit) for i in range(devices)])  135 us
    ppermute x38, starting transfers between devices, flip(): lax.ppermute(values, 'dp', [(i, i ^ 1 << bit) for i in range(devices)])  36.9 us
    all_to_all x6, waiting for transfers between devices, all_to_all(): return lax.all_to_all(values, 'dp', split_axis=0, concat_axis=0, tiled=True)  28.6 us
    all_to_all x6, starting transfers between devices, all_to_all(): return lax.all_to_all(values, 'dp', split_axis=0, concat_axis=0, tiled=True)  22.2 us
    select_n x27, other arithmetic, joined(): jnp.where(taken == 1, jnp.stack([other, values], axis), jnp.stack([values...  21.8 us
    pallas_call x3, Pallas kernels, run_products(): pl.pallas_call(functools.partial(pair_products, chunk), name='pair_produc...  18.6 us
    pallas_call x1, Pallas kernels, run_attention_backward(): pl.pallas_call(functools.partial(attention_backward, order), name='attent...  13.8 us
    pallas_call x1, Pallas kernels, run_mlp(): pl.pallas_call(functools.partial(mlp_both_ways, *mlp_orders), name='mlp_b...  11.1 us
  transfers between devices with their start and end apart: 46, of which 23 were waited for; matrix products, arithmetic and copies ran while one was open for 15% of the time, Pallas kernels for 17%

profile of v3, /device:TPU:0, one launch (start us, length us, event | category | flops | bytes accessed | tf_op | source)
XLA Modules:
  0.0 359.2 jit_solution(3811128458787512188)
XLA Ops:
  4.8 3.9 %collective-permute-start.1 = (bf16[4,48,384]{2,1,0:T(8,128)(2,1)S(1)}, bf16[4,48,384]{2,1,0:T(8,128)(2,1)S(1)}, u32[]{:S(2)}, u32[]{:S(2)}) collective-permute-start(bf16[4,48,384]{2,1,0:T(8,128)(2,1)S(1)} %get-tuple-element.99), channel_id=1, source_target_pairs={{0,16},{1,17},{2,18},{3,19},{4,20},{5,21},{6,22},{7,23},{8,24},{9,... | collective-permute-start | bytes 442376 | tf_op jit(solution)/shard_map/ppermute | solution.py:32
  11.2 3.8 %all-to-all-start = ((bf16[32,2,552]{2,1,0:T(2,128)(2,1)}), bf16[32,2,552]{2,1,0:T(2,128)(2,1)S(1)}, u32[]{:S(2)}, u32[]{:S(2)}) async-start(bf16[32,2,552]{2,1,0:T(2,128)(2,1)} %reshape.2058), calls=%async_computation | async-start | bytes 163840 | tf_op jit(solution)/shard_map/all_to_all | solution.py:634
  15.1 7.6 %all-to-all-done = bf16[32,2,552]{2,1,0:T(2,128)(2,1)S(1)} async-done(((bf16[32,2,552]{2,1,0:T(2,128)(2,1)}), bf16[32,2,552]{2,1,0:T(2,128)(2,1)S(1)}, u32[]{:S(2)}, u32[]{:S(2)}) %all-to-all-start) | async-done | bytes 70688 | tf_op jit(solution)/shard_map/all_to_all | solution.py:634
  23.8 2.2 collective-permute-start.11
  26.9 8.7 %collective-permute-done.6 = bf16[4,48,384]{2,1,0:T(8,128)(2,1)S(1)} collective-permute-done((bf16[4,48,384]{2,1,0:T(8,128)(2,1)S(1)}, bf16[4,48,384]{2,1,0:T(8,128)(2,1)S(1)}, u32[]{:S(2)}, u32[]{:S(2)}) %collective-permute-start.6) | collective-permute-done | bytes 147488 | tf_op jit(solution)/shard_map/ppermute | solution.py:32
  40.6 3.5 all-to-all-start.1
  48.1 14.3 %collective-permute-done.7 = bf16[2,4,48,384]{3,2,1,0:T(8,128)(2,1)S(1)} collective-permute-done((bf16[2,4,48,384]{3,2,1,0:T(8,128)(2,1)S(1)}, bf16[2,4,48,384]{3,2,1,0:T(8,128)(2,1)S(1)}, u32[]{:S(2)}, u32[]{:S(2)}) %collective-permute-start.7) | collective-permute-done | bytes 294944 | tf_op jit(solution)/shard_map/ppermute | solution.py:32
  62.5 1.6 collective-permute-start.8
  65.0 6.8 %collective-permute-done.3 = bf16[2,2,4,48,384]{4,3,2,1,0:T(8,128)(2,1)S(1)} collective-permute-done((bf16[2,2,4,48,384]{4,3,2,1,0:T(8,128)(2,1)S(1)}, bf16[2,2,4,48,384]{4,3,2,1,0:T(8,128)(2,1)S(1)}, u32[]{:S(2)}, u32[]{:S(2)}) %collective-permute-start.3) | collective-permute-done | bytes 589856 | tf_op jit(solution)/shard_map/ppermute | solution.py:32
  74.6 2.7 collective-permute-done.8
  88.5 15.7 %collective-permute-done.4 = bf16[2,2,2,4,48,384]{5,4,3,2,1,0:T(8,128)(2,1)} collective-permute-done((bf16[2,2,2,4,48,384]{5,4,3,2,1,0:T(8,128)(2,1)}, bf16[2,2,2,4,48,384]{5,4,3,2,1,0:T(8,128)(2,1)}, u32[]{:S(2)}, u32[]{:S(2)}) %collective-permute-start.4) | collective-permute-done | bytes 1179680 | tf_op jit(solution)/shard_map/ppermute | solution.py:32
  105.4 2.2 maximum_select_fusion
  108.0 3.7 %maximum_select_fusion.1 = bf16[2,2,2,2,4,48,384]{6,5,4,3,2,1,0:T(8,128)(2,1)} fusion(bf16[1,2,2,2,4,48,384]{6,5,4,3,2,1,0:T(8,128)(2,1)S(1)} %copy-done.7, bf16[1,2,2,2,4,48,384]{6,5,4,3,2,1,0:T(8,128)(2,1)} %bitcast.39, pred[]{:T(512)S(6)} %eq.21), kind=kLoop, calls=%fused_computation.1 | loop fusion | flops 3538944 | bytes 4718593 | tf_op jit(solution)/shard_map/jit(_where)/select_n | solution.py:40
  111.9 3.6 %maximum_select_fusion.2 = bf16[2,2,2,2,4,48,384]{6,5,4,3,2,1,0:T(8,128)(2,1)} fusion(bf16[1,2,2,2,4,48,384]{6,5,4,3,2,1,0:T(8,128)(2,1)S(1)} %copy-done.6, bf16[1,2,2,2,4,48,384]{6,5,4,3,2,1,0:T(8,128)(2,1)} %bitcast.43, pred[]{:T(512)S(6)} %eq.24), kind=kLoop, calls=%fused_computation.2 | loop fusion | flops 3538944 | bytes 4718593 | tf_op jit(solution)/shard_map/jit(_where)/select_n | solution.py:40
  121.4 9.6 %attention_forward.1 = (bf16[3,256,768]{2,1,0:T(8,128)(2,1)}, bf16[3,256,768]{2,1,0:T(8,128)(2,1)S(1)}, f32[256,768]{1,0:T(8,128)S(1)}, f32[256,768]{1,0:T(8,128)S(1)}) custom-call(s32[2]{0:T(128)S(1)} %pad_add_fusion.place_ref, bf16[256,768]{1,0:T(8,128)(2,1)S(1)} %bitcast.206, f32[6,768]{1,0:T(8,128)S(1)} %slice_add_fusion.mod_ref, ...), custom_call_target="tpu_custom_call" | custom-call | flops 2013265920 | bytes 8650752 | tf_op jit(solution)/shard_map/attention_forward/pallas_call | solution.py:432
  131.4 11.1 %mlp_both_ways.1 = (bf16[256,768]{1,0:T(8,128)(2,1)}, bf16[4,256,768]{2,1,0:T(8,128)(2,1)}, bf16[5,256,384]{2,1,0:T(8,128)(2,1)S(1)}, bf16[5,256,384]{2,1,0:T(8,...) custom-call(s32[2]{0:T(128)S(1)} %pad_add_fusion.place_ref, ...), custom_call_target="tpu_custom_call" | custom-call | flops 4831838208 | bytes 17301504 | tf_op jit(solution)/shard_map/mlp_both_ways/pallas_call | solution.py:457
  143.0 13.8 %attention_backward.1 = (f32[256,768]{1,0:T(8,128)}, bf16[4,256,384]{2,1,0:T(8,128)(2,1)S(1)}, bf16[4,256,384]{2,1,0:T(8,128)(2,1)}, f32[14,768]{1,0:T(8,128)S(1)}) custom-call(s32[2]{0:T(128)S(1)} %pad_add_fusion.place_ref, bf16[256,768]{1,0:T(8,128)(2,1)S(1)} %bitcast.207, f32[6,768]{1,0:T(8,128)S(1)} %slice_add_fusion.mod_ref, ...), custom_call_target="tpu_custom_call" | custom-call | flops 3221225472 | bytes 9437184 | tf_op jit(solution)/shard_map/attention_backward/pallas_call | solution.py:508
  158.4 6.1 %pair_products.5 = (f32[4,384,384]{2,1,0:T(8,128)}, bf16[4,384,384]{2,1,0:T(8,128)(2,1)}) custom-call(s32[1]{0:T(128)} %bitcast.71.mine_ref, bf16[3,256,768]{2,1,0:T(8,128)(2,1)} %get-tuple-element.48.lefts_ref.left_ref, bf16[3,256,768]{2,1,0:T(8,128)(2,1)} %collective-permute-done.23.left_other_ref, bf16[5,256,384]{2,1,0:T(8,128)(2,1)} %copy-done, ...), custom_call_target="tpu_custom_call" | custom-call | flops 1207959552 | bytes 7077888 | tf_op jit(solution)/shard_map/pair_products/pallas_call | solution.py:559
  168.1 4.5 %all-to-all-start.2 = ((bf16[32,2,2640]{2,1,0:T(2,128)(2,1)}), bf16[32,2,2640]{2,1,0:T(2,128)(2,1)S(1)}, u32[]{:S(2)}, u32[]{:S(2)}) async-start(bf16[32,2,2640]{2,1,0:T(2,128)(2,1)} %reshape.2060), calls=%async_computation.2 | async-start | bytes 688128 | tf_op jit(solution)/shard_map/all_to_all | solution.py:634
  172.6 2.7 collective-permute-start.34
  176.2 6.2 %pair_products.4 = (f32[4,384,384]{2,1,0:T(8,128)}, bf16[4,384,384]{2,1,0:T(8,128)(2,1)}) custom-call(s32[1]{0:T(128)} %bitcast.63.mine_ref, bf16[3,256,768]{2,1,0:T(8,128)(2,1)} %get-tuple-element.48.lefts_ref.left_ref, bf16[3,256,768]{2,1,0:T(8,128)(2,1)} %collective-permute-done.23.left_other_ref, bf16[4,256,384]{2,1,0:T(8,128)(2,1)} %copy-done.4, ...), custom_call_target="tpu_custom_call" | custom-call | flops 1207959552 | bytes 7077888 | tf_op jit(solution)/shard_map/pair_products/pallas_call | solution.py:559
  184.0 3.0 collective-permute-done.34
  188.5 26.7 %collective-permute-done.35 = bf16[1,2,48,768]{3,2,1,0:T(8,128)(2,1)S(1)} collective-permute-done((bf16[1,2,48,768]{3,2,1,0:T(8,128)(2,1)S(1)}, bf16[1,2,48,768]{3,2,1,0:T(8,128)(2,1)S(1)}, u32[]{:S(2)}, u32[]{:S(2)}) %collective-permute-start.35) | collective-permute-done | bytes 147488 | tf_op jit(solution)/shard_map/ppermute | solution.py:32
  218.6 6.3 %pair_products.3 = (f32[4,384,384]{2,1,0:T(8,128)}, bf16[4,384,384]{2,1,0:T(8,128)(2,1)}) custom-call(s32[1]{0:T(128)} %bitcast.49.mine_ref, bf16[4,256,768]{2,1,0:T(8,128)(2,1)} %get-tuple-element.58.left_ref, bf16[4,256,768]{2,1,0:T(8,128)(2,1)} %collective-permute-done.17.left_other_ref, bf16[5,256,384]{2,1,0:T(8,128)(2,1)} %copy-done, ...), custom_call_target="tpu_custom_call" | custom-call | flops 1207959552 | bytes 7077888 | tf_op jit(solution)/shard_map/pair_products/pallas_call | solution.py:559
  224.9 1.6 collective-permute-start.19
  226.4 1.8 fusion.8
  228.3 2.6 all-to-all-start.3
  230.9 1.7 convert_add_fusion
  232.7 1.8 collective-permute-start.30
  234.4 1.7 convert_add_fusion.1
  237.8 16.4 %collective-permute-done.19 = bf16[4,384,384]{2,1,0:T(8,128)(2,1)} collective-permute-done((bf16[4,384,384]{2,1,0:T(8,128)(2,1)}, bf16[4,384,384]{2,1,0:T(8,128)(2,1)}, u32[]{:S(2)}, u32[]{:S(2)}) %collective-permute-start.19) | collective-permute-done | bytes 1179680 | tf_op jit(solution)/shard_map/ppermute | solution.py:32
  256.7 1.6 collective-permute-start.31
  258.2 8.5 %collective-permute-done.26 = bf16[4,2,2,48,384]{4,3,0,1,2:T(8,128)(2,1)S(1)} collective-permute-done((bf16[4,2,2,48,384]{4,3,0,1,2:T(8,128)(2,1)S(1)}, bf16[4,2,2,48,384]{4,3,0,1,2:T(8,128)(2,1)S(1)}, u32[]{:S(2)}, u32[]{:S(2)}) %collective-permute-start.26) | collective-permute-done | bytes 589856 | tf_op jit(solution)/shard_map/ppermute | solution.py:32
  267.6 4.3 %collective-permute-done.31 = bf16[4,2,48,384]{3,2,0,1:T(8,128)(2,1)S(1)} collective-permute-done((bf16[4,2,48,384]{3,2,0,1:T(8,128)(2,1)S(1)}, bf16[4,2,48,384]{3,2,0,1:T(8,128)(2,1)S(1)}, u32[]{:S(2)}, u32[]{:S(2)}) %collective-permute-start.31) | collective-permute-done | bytes 294944 | tf_op jit(solution)/shard_map/ppermute | solution.py:32
  272.1 3.7 %collective-permute-done.27 = bf16[4,2,48,384]{3,2,0,1:T(8,128)(2,1)S(1)} collective-permute-done((bf16[4,2,48,384]{3,2,0,1:T(8,128)(2,1)S(1)}, bf16[4,2,48,384]{3,2,0,1:T(8,128)(2,1)S(1)}, u32[]{:S(2)}, u32[]{:S(2)}) %collective-permute-start.27) | collective-permute-done | bytes 294944 | tf_op jit(solution)/shard_map/ppermute | solution.py:32
  276.1 2.0 collective-permute-start.28
  278.1 2.3 collective-permute-done.32
  280.5 8.7 %collective-permute-done.21 = bf16[4,2,48,384]{3,2,0,1:T(8,128)(2,1)S(1)} collective-permute-done((bf16[4,2,48,384]{3,2,0,1:T(8,128)(2,1)S(1)}, bf16[4,2,48,384]{3,2,0,1:T(8,128)(2,1)S(1)}, u32[]{:S(2)}, u32[]{:S(2)}) %collective-permute-start.21) | collective-permute-done | bytes 294944 | tf_op jit(solution)/shard_map/ppermute | solution.py:32
  289.4 8.7 %collective-permute-done.22 = bf16[4,48,384]{2,1,0:T(8,128)(2,1)S(1)} collective-permute-done((bf16[4,48,384]{2,1,0:T(8,128)(2,1)S(1)}, bf16[4,48,384]{2,1,0:T(8,128)(2,1)S(1)}, u32[]{:S(2)}, u32[]{:S(2)}) %collective-permute-start.22) | collective-permute-done | bytes 147488 | tf_op jit(solution)/shard_map/ppermute | solution.py:32
  301.5 1.8 fusion.36
  304.2 4.5 %all-to-all-start.4 = ((bf16[32,24,384]{2,1,0:T(8,128)(2,1)}), bf16[32,24,384]{2,1,0:T(8,128)(2,1)S(1)}, u32[]{:S(2)}, u32[]{:S(2)}) async-start(bf16[32,24,384]{2,1,0:T(8,128)(2,1)} %bitcast.104), calls=%async_computation.4 | async-start | bytes 1179648 | tf_op jit(solution)/shard_map/all_to_all | solution.py:634
  310.4 1.7 convert_multiply_fusion
  312.1 13.1 %all-to-all-done.4 = bf16[32,24,384]{2,1,0:T(8,128)(2,1)S(1)} async-done(((bf16[32,24,384]{2,1,0:T(8,128)(2,1)}), bf16[32,24,384]{2,1,0:T(8,128)(2,1)S(1)}, u32[]{:S(2)}, u32[]{:S(2)}) %all-to-all-start.4) | async-done | bytes 589856 | tf_op jit(solution)/shard_map/all_to_all | solution.py:634
  325.8 2.1 fusion.block_ref
  327.9 8.6 %orthogonalize_halves.1 = bf16[768,384]{1,0:T(8,128)(2,1)} custom-call(s32[2]{0:T(128)S(1)} %pad_add_fusion.place_ref, bf16[768,384]{1,0:T(8,128)(2,1)S(1)} %bitcast.204, bf16[768,384]{1,0:T(8,128)(2,1)S(1)} %collective-permute-done.39.other_ref), custom_call_target="tpu_custom_call" | custom-call | flops 5435817984 | bytes 2359296 | tf_op jit(solution)/shard_map/orthogonalize_halves/pallas_call | solution.py:607
  336.6 3.3 all-to-all-start.5
  339.9 7.2 %orthogonalize_whole.1 = bf16[1,768,768]{2,1,0:T(8,128)(2,1)S(1)} custom-call(bf16[1,768,768]{2,1,0:T(8,128)(2,1)S(1)} %fusion.block_ref), custom_call_target="tpu_custom_call" | custom-call | flops 5435817984 | bytes 2359296 | tf_op jit(solution)/shard_map/orthogonalize_whole/pallas_call | solution.py:621
  348.7 8.0 %all-to-all-done.5 = bf16[32,24,384]{2,1,0:T(8,128)(2,1)S(1)} async-done(((bf16[32,24,384]{2,1,0:T(8,128)(2,1)}), bf16[32,24,384]{2,1,0:T(8,128)(2,1)S(1)}, u32[]{:S(2)}, u32[]{:S(2)}) %all-to-all-start.5) | async-done | bytes 589856 | tf_op jit(solution)/shard_map/all_to_all | solution.py:634
  (243 shorter events, 68.5 us)
Async XLA Ops:
  2.0 36.5 %copy-start.9 = (bf16[18,24,768]{2,1,0:T(8,128)(2,1)}, bf16[18,24,768]{2,1,0:T(8,128)(2,1)S(1)}, u32[]{:S(2)}) copy-start(bf16[18,24,768]{2,1,0:T(8,128)(2,1)S(1)} %convert_element_type.152) | copy-start | bytes 1990660
  2.2 1.7 collective-permute-start
  4.8 21.2 %collective-permute-start.1 = (bf16[4,48,384]{2,1,0:T(8,128)(2,1)S(1)}, bf16[4,48,384]{2,1,0:T(8,128)(2,1)S(1)}, u32[]{:S(2)}, u32[]{:S(2)}) collective-permute-start(bf16[4,48,384]{2,1,0:T(8,128)(2,1)S(1)} %get-tuple-element.99), channel_id=1, source_target_pairs={{0,16},{1,17},{2,18},{3,19},{4,20},{5,21},{6,22},{7,23},{8,24},{9,... | collective-permute-start | bytes 442376 | tf_op jit(solution)/shard_map/ppermute | solution.py:32
  11.2 11.4 %all-to-all-start = ((bf16[32,2,552]{2,1,0:T(2,128)(2,1)}), bf16[32,2,552]{2,1,0:T(2,128)(2,1)S(1)}, u32[]{:S(2)}, u32[]{:S(2)}) async-start(bf16[32,2,552]{2,1,0:T(2,128)(2,1)} %reshape.2058), calls=%async_computation | async-start | bytes 163840 | tf_op jit(solution)/shard_map/all_to_all | solution.py:634
  23.0 59.9 %copy-start.15 = (bf16[32,1,1104]{0,2,1:T(8,128)(2,1)}, bf16[32,1,1104]{0,2,1:T(8,128)(2,1)S(1)}, u32[]{:S(2)}) copy-start(bf16[32,1,1104]{0,2,1:T(8,128)(2,1)S(1)} %copy.94) | copy-start | bytes 211972
  23.1 12.5 %collective-permute-start.6 = (bf16[4,48,384]{2,1,0:T(8,128)(2,1)S(1)}, bf16[4,48,384]{2,1,0:T(8,128)(2,1)S(1)}, u32[]{:S(2)}, u32[]{:S(2)}) collective-permute-start(bf16[4,48,384]{2,1,0:T(8,128)(2,1)S(1)} %get-tuple-element.98), channel_id=1, source_target_pairs={{0,16},{1,17},{2,18},{3,19},{4,20},{5,21},{6,22},{7,23},{8,24},{9,... | collective-permute-start | bytes 442376 | tf_op jit(solution)/shard_map/ppermute | solution.py:32
  23.8 21.9 %collective-permute-start.11 = (bf16[4,48,384]{2,1,0:T(8,128)(2,1)}, bf16[4,48,384]{2,1,0:T(8,128)(2,1)S(1)}, u32[]{:S(2)}, u32[]{:S(2)}) collective-permute-start(bf16[4,48,384]{2,1,0:T(8,128)(2,1)} %get-tuple-element.97), channel_id=1, source_target_pairs={{0,16},{1,17},{2,18},{3,19},{4,20},{5,21},{6,22},{7,23},{8,24},{9,... | collective-permute-start | bytes 442376 | tf_op jit(solution)/shard_map/ppermute | solution.py:32
  37.1 10.2 %collective-permute-start.2 = (bf16[2,4,48,384]{3,2,1,0:T(8,128)(2,1)}, bf16[2,4,48,384]{3,2,1,0:T(8,128)(2,1)S(1)}, u32[]{:S(2)}, u32[]{:S(2)}) collective-permute-start(bf16[2,4,48,384]{3,2,1,0:T(8,128)(2,1)} %maximum_select_fusion.20), channel_id=1, source_target_pairs={{0,4},{1,5},{2,6},{3,7},{4,0},{5,1},{6,2},{7,3},{8,12},{9,13},{10,... | collective-permute-start | bytes 884744 | tf_op jit(solution)/shard_map/ppermute | solution.py:32
  40.6 46.7 %all-to-all-start.1 = ((f32[32,1,4608]{2,1,0:T(1,128)}), f32[32,1,4608]{2,1,0:T(1,128)}, u32[]{:S(2)}, u32[]{:S(2)}) async-start(f32[32,1,4608]{2,1,0:T(1,128)} %all_to_all.49), calls=%async_computation.1 | async-start | bytes 1179648 | tf_op jit(solution)/shard_map/all_to_all | solution.py:634
  44.2 18.2 %collective-permute-start.7 = (bf16[2,4,48,384]{3,2,1,0:T(8,128)(2,1)S(1)}, bf16[2,4,48,384]{3,2,1,0:T(8,128)(2,1)S(1)}, u32[]{:S(2)}, u32[]{:S(2)}) collective-permute-start(bf16[2,4,48,384]{3,2,1,0:T(8,128)(2,1)S(1)} %maximum_select_fusion.22), channel_id=1, source_target_pairs={{0,8},{1,9},{2,10},{3,11},{4,12},{5,13},{6,14},{7,15},{8,0},{9,1},... | collective-permute-start | bytes 884744 | tf_op jit(solution)/shard_map/ppermute | solution.py:32
  45.7 18.3 %collective-permute-start.12 = (bf16[2,4,48,384]{3,2,1,0:T(8,128)(2,1)S(1)}, bf16[2,4,48,384]{3,2,1,0:T(8,128)(2,1)S(1)}, u32[]{:S(2)}, u32[]{:S(2)}) collective-permute-start(bf16[2,4,48,384]{3,2,1,0:T(8,128)(2,1)S(1)} %maximum_select_fusion.24), channel_id=1, source_target_pairs={{0,2},{1,3},{2,0},{3,1},{4,6},{5,7},{6,4},{7,5},{8,10},{9,11},{10,... | collective-permute-start | bytes 884744 | tf_op jit(solution)/shard_map/ppermute | solution.py:32
  47.5 24.3 %collective-permute-start.3 = (bf16[2,2,4,48,384]{4,3,2,1,0:T(8,128)(2,1)S(1)}, bf16[2,2,4,48,384]{4,3,2,1,0:T(8,128)(2,1)S(1)}, u32[]{:S(2)}, u32[]{:S(2)}) collective-permute-start(bf16[2,2,4,48,384]{4,3,2,1,0:T(8,128)(2,1)S(1)} %maximum_select_fusion.11), channel_id=1, source_target_pairs={{0,2},{1,3},{2,0},{3,1},{4,6},{5,7},{6,4},{7,5},{8,10},{9,11},{10,... | collective-permute-start | bytes 1769480 | tf_op jit(solution)/shard_map/ppermute | solution.py:32
  62.5 14.8 %collective-permute-start.8 = (bf16[2,2,4,48,384]{4,3,2,1,0:T(8,128)(2,1)S(1)}, bf16[2,2,4,48,384]{4,3,2,1,0:T(8,128)(2,1)S(1)}, u32[]{:S(2)}, u32[]{:S(2)}) collective-permute-start(bf16[2,2,4,48,384]{4,3,2,1,0:T(8,128)(2,1)S(1)} %maximum_select_fusion.13), channel_id=1, source_target_pairs={{0,4},{1,5},{2,6},{3,7},{4,0},{5,1},{6,2},{7,3},{8,12},{9,13},{10,... | collective-permute-start | bytes 1769480 | tf_op jit(solution)/shard_map/ppermute | solution.py:32
  64.2 16.3 %collective-permute-start.13 = (bf16[2,2,4,48,384]{4,3,2,1,0:T(8,128)(2,1)S(1)}, bf16[2,2,4,48,384]{4,3,2,1,0:T(8,128)(2,1)S(1)}, u32[]{:S(2)}, u32[]{:S(2)}) collective-permute-start(bf16[2,2,4,48,384]{4,3,2,1,0:T(8,128)(2,1)S(1)} %maximum_select_fusion.15), channel_id=1, source_target_pairs={{0,8},{1,9},{2,10},{3,11},{4,12},{5,13},{6,14},{7,15},{8,0},{9,1},... | collective-permute-start | bytes 1769480 | tf_op jit(solution)/shard_map/ppermute | solution.py:32
  73.0 31.1 %collective-permute-start.4 = (bf16[2,2,2,4,48,384]{5,4,3,2,1,0:T(8,128)(2,1)}, bf16[2,2,2,4,48,384]{5,4,3,2,1,0:T(8,128)(2,1)}, u32[]{:S(2)}, u32[]{:S(2)}) collective-permute-start(bf16[2,2,2,4,48,384]{5,4,3,2,1,0:T(8,128)(2,1)} %maximum_select_fusion.3), channel_id=1, source_target_pairs={{0,8},{1,9},{2,10},{3,11},{4,12},{5,13},{6,14},{7,15},{8,0},{9,1},... | collective-permute-start | bytes 3538952 | tf_op jit(solution)/shard_map/ppermute | solution.py:32
  78.5 26.9 %collective-permute-start.9 = (bf16[2,2,2,4,48,384]{5,4,3,2,1,0:T(8,128)(2,1)}, bf16[2,2,2,4,48,384]{5,4,3,2,1,0:T(8,128)(2,1)}, u32[]{:S(2)}, u32[]{:S(2)}) collective-permute-start(bf16[2,2,2,4,48,384]{5,4,3,2,1,0:T(8,128)(2,1)} %maximum_select_fusion.4), channel_id=1, source_target_pairs={{0,2},{1,3},{2,0},{3,1},{4,6},{5,7},{6,4},{7,5},{8,10},{9,11},{10,... | collective-permute-start | bytes 3538952 | tf_op jit(solution)/shard_map/ppermute | solution.py:32
  81.7 26.3 %collective-permute-start.14 = (bf16[2,2,2,4,48,384]{5,4,3,2,1,0:T(8,128)(2,1)}, bf16[2,2,2,4,48,384]{5,4,3,2,1,0:T(8,128)(2,1)}, u32[]{:S(2)}, u32[]{:S(2)}) collective-permute-start(bf16[2,2,2,4,48,384]{5,4,3,2,1,0:T(8,128)(2,1)} %maximum_select_fusion.6), channel_id=1, source_target_pairs={{0,4},{1,5},{2,6},{3,7},{4,0},{5,1},{6,2},{7,3},{8,12},{9,13},{10,... | collective-permute-start | bytes 3538952 | tf_op jit(solution)/shard_map/ppermute | solution.py:32
  107.6 13.7 %collective-permute-start.10 = (bf16[16,4,48,384]{3,2,1,0:T(8,128)(2,1)S(1)}, bf16[16,4,48,384]{3,2,1,0:T(8,128)(2,1)}, u32[]{:S(2)}, u32[]{:S(2)}) collective-permute-start(bf16[16,4,48,384]{3,2,1,0:T(8,128)(2,1)S(1)} %bitcast.200), channel_id=1, source_target_pairs={{0,1},{1,0},{2,3},{3,2},{4,5},{5,4},{6,7},{7,6},{8,9},{9,8},{10,11... | collective-permute-start | bytes 7077896 | tf_op jit(solution)/shard_map/ppermute | solution.py:32
  111.7 19.7 %collective-permute-start.15 = (bf16[16,4,48,384]{3,2,1,0:T(8,128)(2,1)}, bf16[16,4,48,384]{3,2,1,0:T(8,128)(2,1)}, u32[]{:S(2)}, u32[]{:S(2)}) collective-permute-start(bf16[16,4,48,384]{3,2,1,0:T(8,128)(2,1)} %bitcast.42.up_ref), channel_id=1, source_target_pairs={{0,1},{1,0},{2,3},{3,2},{4,5},{5,4},{6,7},{7,6},{8,9},{9,8},{10,11... | collective-permute-start | bytes 7077896 | tf_op jit(solution)/shard_map/ppermute | solution.py:32
  115.5 15.9 %collective-permute-start.16 = (bf16[16,4,48,384]{3,2,1,0:T(8,128)(2,1)}, bf16[16,4,48,384]{3,2,1,0:T(8,128)(2,1)}, u32[]{:S(2)}, u32[]{:S(2)}) collective-permute-start(bf16[16,4,48,384]{3,2,1,0:T(8,128)(2,1)} %bitcast.46.down_ref), channel_id=1, source_target_pairs={{0,1},{1,0},{2,3},{3,2},{4,5},{5,4},{6,7},{7,6},{8,9},{9,8},{10,11... | collective-permute-start | bytes 7077896 | tf_op jit(solution)/shard_map/ppermute | solution.py:32
  117.3 3.1 collective-permute-start.5
  131.0 27.3 %collective-permute-start.23 = (bf16[3,256,768]{2,1,0:T(8,128)(2,1)}, bf16[3,256,768]{2,1,0:T(8,128)(2,1)}, u32[]{:S(2)}, u32[]{:S(2)}) collective-permute-start(bf16[3,256,768]{2,1,0:T(8,128)(2,1)} %get-tuple-element.48.lefts_ref.left_ref), channel_id=1, source_target_pairs={{0,1},{1,0},{2,3},{3,2},{4,5},{5,4},{6,7},{7,6},{8,9},{9,8},{10,11... | collective-permute-start | bytes 3538952 | tf_op jit(solution)/shard_map/ppermute | solution.py:32
  142.4 15.9 %collective-permute-start.18 = (bf16[5,256,384]{2,1,0:T(8,128)(2,1)S(1)}, bf16[5,256,384]{2,1,0:T(8,128)(2,1)}, u32[]{:S(2)}, u32[]{:S(2)}) collective-permute-start(bf16[5,256,384]{2,1,0:T(8,128)(2,1)S(1)} %get-tuple-element.60), channel_id=1, source_target_pairs={{0,1},{1,0},{2,3},{3,2},{4,5},{5,4},{6,7},{7,6},{8,9},{9,8},{10,11... | collective-permute-start | bytes 2949128 | tf_op jit(solution)/shard_map/ppermute | solution.py:32
  142.6 75.6 %collective-permute-start.17 = (bf16[4,256,768]{2,1,0:T(8,128)(2,1)}, bf16[4,256,768]{2,1,0:T(8,128)(2,1)}, u32[]{:S(2)}, u32[]{:S(2)}) collective-permute-start(bf16[4,256,768]{2,1,0:T(8,128)(2,1)} %get-tuple-element.58.left_ref), channel_id=1, source_target_pairs={{0,1},{1,0},{2,3},{3,2},{4,5},{5,4},{6,7},{7,6},{8,9},{9,8},{10,11... | collective-permute-start | bytes 4718600 | tf_op jit(solution)/shard_map/ppermute | solution.py:32
  157.7 17.7 %collective-permute-start.24 = (bf16[4,256,384]{2,1,0:T(8,128)(2,1)}, bf16[4,256,384]{2,1,0:T(8,128)(2,1)S(1)}, u32[]{:S(2)}, u32[]{:S(2)}) collective-permute-start(bf16[4,256,384]{2,1,0:T(8,128)(2,1)} %get-tuple-element.68), channel_id=1, source_target_pairs={{0,1},{1,0},{2,3},{3,2},{4,5},{5,4},{6,7},{7,6},{8,9},{9,8},{10,11... | collective-permute-start | bytes 2359304 | tf_op jit(solution)/shard_map/ppermute | solution.py:32
  164.5 66.3 %collective-permute-start.29 = (bf16[4,384,384]{2,1,0:T(8,128)(2,1)}, bf16[4,384,384]{2,1,0:T(8,128)(2,1)}, u32[]{:S(2)}, u32[]{:S(2)}) collective-permute-start(bf16[4,384,384]{2,1,0:T(8,128)(2,1)} %get-tuple-element.72), channel_id=1, source_target_pairs={{0,4},{1,5},{2,6},{3,7},{4,0},{5,1},{6,2},{7,3},{8,12},{9,13},{10,... | collective-permute-start | bytes 3538952 | tf_op jit(solution)/shard_map/ppermute | solution.py:32
  168.1 49.2 %all-to-all-start.2 = ((bf16[32,2,2640]{2,1,0:T(2,128)(2,1)}), bf16[32,2,2640]{2,1,0:T(2,128)(2,1)S(1)}, u32[]{:S(2)}, u32[]{:S(2)}) async-start(bf16[32,2,2640]{2,1,0:T(2,128)(2,1)} %reshape.2060), calls=%async_computation.2 | async-start | bytes 688128 | tf_op jit(solution)/shard_map/all_to_all | solution.py:634
  172.6 14.4 %collective-permute-start.34 = (bf16[1,48,768]{2,1,0:T(8,128)(2,1)S(1)}, bf16[1,48,768]{2,1,0:T(8,128)(2,1)S(1)}, u32[]{:S(2)}, u32[]{:S(2)}) collective-permute-start(bf16[1,48,768]{2,1,0:T(8,128)(2,1)S(1)} %bitcast.254), channel_id=1, source_target_pairs={{0,16},{1,17},{2,18},{3,19},{4,20},{5,21},{6,22},{7,23},{8,24},{9,... | collective-permute-start | bytes 221192 | tf_op jit(solution)/shard_map/ppermute | solution.py:32
  182.4 52.0 %collective-permute-start.25 = (bf16[4,384,384]{2,1,0:T(8,128)(2,1)}, bf16[4,384,384]{2,1,0:T(8,128)(2,1)}, u32[]{:S(2)}, u32[]{:S(2)}) collective-permute-start(bf16[4,384,384]{2,1,0:T(8,128)(2,1)} %get-tuple-element.70), channel_id=1, source_target_pairs={{0,8},{1,9},{2,10},{3,11},{4,12},{5,13},{6,14},{7,15},{8,0},{9,1},... | collective-permute-start | bytes 3538952 | tf_op jit(solution)/shard_map/ppermute | solution.py:32
  187.0 28.2 %collective-permute-start.35 = (bf16[1,2,48,768]{3,2,1,0:T(8,128)(2,1)S(1)}, bf16[1,2,48,768]{3,2,1,0:T(8,128)(2,1)S(1)}, u32[]{:S(2)}, u32[]{:S(2)}) collective-permute-start(bf16[1,2,48,768]{3,2,1,0:T(8,128)(2,1)S(1)} %maximum_select_fusion.29), channel_id=1, source_target_pairs={{0,8},{1,9},{2,10},{3,11},{4,12},{5,13},{6,14},{7,15},{8,0},{9,1},... | collective-permute-start | bytes 442376 | tf_op jit(solution)/shard_map/ppermute | solution.py:32
  215.9 83.3 %collective-permute-start.36 = (bf16[1,2,2,48,768]{4,3,1,2,0:T(8,128)(2,1)}, bf16[1,2,2,48,768]{4,3,1,2,0:T(8,128)(2,1)}, u32[]{:S(2)}, u32[]{:S(2)}) collective-permute-start(bf16[1,2,2,48,768]{4,3,1,2,0:T(8,128)(2,1)} %maximum_select_fusion.27), channel_id=1, source_target_pairs={{0,4},{1,3},{2,6},{3,1},{4,0},{5,7},{6,2},{7,5},{8,12},{9,11},{10,... | collective-permute-start | bytes 884744 | tf_op jit(solution)/shard_map/ppermute | solution.py:67
  224.9 29.3 %collective-permute-start.19 = (bf16[4,384,384]{2,1,0:T(8,128)(2,1)}, bf16[4,384,384]{2,1,0:T(8,128)(2,1)}, u32[]{:S(2)}, u32[]{:S(2)}) collective-permute-start(bf16[4,384,384]{2,1,0:T(8,128)(2,1)} %get-tuple-element.62), channel_id=1, source_target_pairs={{0,2},{1,3},{2,0},{3,1},{4,6},{5,7},{6,4},{7,5},{8,10},{9,11},{10,... | collective-permute-start | bytes 3538952 | tf_op jit(solution)/shard_map/ppermute | solution.py:32
  228.3 61.1 %all-to-all-start.3 = ((f32[32,1,24]{2,1,0:T(1,128)}), f32[32,1,24]{2,1,0:T(1,128)S(1)}, u32[]{:S(2)}, u32[]{:S(2)}) async-start(f32[32,1,24]{2,1,0:T(1,128)} %bitcast.114), calls=%async_computation.3 | async-start | bytes 32768 | tf_op jit(solution)/shard_map/all_to_all | solution.py:634
  232.7 23.8 %collective-permute-start.30 = (bf16[4,2,2,48,384]{4,3,0,1,2:T(8,128)(2,1)S(1)}, bf16[4,2,2,48,384]{4,3,0,1,2:T(8,128)(2,1)S(1)}, u32[]{:S(2)}, u32[]{:S(2)}) collective-permute-start(bf16[4,2,2,48,384]{4,3,0,1,2:T(8,128)(2,1)S(1)} %fusion.3), channel_id=1, source_target_pairs={{0,8},{1,9},{2,10},{3,11},{4,12},{5,13},{6,14},{7,15},{8,0},{9,1},... | collective-permute-start | bytes 1769480 | tf_op jit(solution)/shard_map/ppermute | solution.py:32
  236.2 30.5 %collective-permute-start.26 = (bf16[4,2,2,48,384]{4,3,0,1,2:T(8,128)(2,1)S(1)}, bf16[4,2,2,48,384]{4,3,0,1,2:T(8,128)(2,1)S(1)}, u32[]{:S(2)}, u32[]{:S(2)}) collective-permute-start(bf16[4,2,2,48,384]{4,3,0,1,2:T(8,128)(2,1)S(1)} %fusion.2), channel_id=1, source_target_pairs={{0,2},{1,3},{2,0},{3,1},{4,6},{5,7},{6,4},{7,5},{8,10},{9,11},{10,... | collective-permute-start | bytes 1769480 | tf_op jit(solution)/shard_map/ppermute | solution.py:32
  255.8 20.0 %collective-permute-start.20 = (bf16[4,2,2,48,384]{4,3,0,1,2:T(8,128)(2,1)S(1)}, bf16[4,2,2,48,384]{4,3,0,1,2:T(8,128)(2,1)S(1)}, u32[]{:S(2)}, u32[]{:S(2)}) collective-permute-start(bf16[4,2,2,48,384]{4,3,0,1,2:T(8,128)(2,1)S(1)} %fusion.1), channel_id=1, source_target_pairs={{0,4},{1,5},{2,6},{3,7},{4,0},{5,1},{6,2},{7,3},{8,12},{9,13},{10,... | collective-permute-start | bytes 1769480 | tf_op jit(solution)/shard_map/ppermute | solution.py:32
  256.7 15.2 %collective-permute-start.31 = (bf16[4,2,48,384]{3,2,0,1:T(8,128)(2,1)S(1)}, bf16[4,2,48,384]{3,2,0,1:T(8,128)(2,1)S(1)}, u32[]{:S(2)}, u32[]{:S(2)}) collective-permute-start(bf16[4,2,48,384]{3,2,0,1:T(8,128)(2,1)S(1)} %fusion.7), channel_id=1, source_target_pairs={{0,2},{1,3},{2,0},{3,1},{4,6},{5,7},{6,4},{7,5},{8,10},{9,11},{10,... | collective-permute-start | bytes 884744 | tf_op jit(solution)/shard_map/ppermute | solution.py:32
  266.9 8.8 %collective-permute-start.27 = (bf16[4,2,48,384]{3,2,0,1:T(8,128)(2,1)S(1)}, bf16[4,2,48,384]{3,2,0,1:T(8,128)(2,1)S(1)}, u32[]{:S(2)}, u32[]{:S(2)}) collective-permute-start(bf16[4,2,48,384]{3,2,0,1:T(8,128)(2,1)S(1)} %fusion.6), channel_id=1, source_target_pairs={{0,4},{1,5},{2,6},{3,7},{4,0},{5,1},{6,2},{7,3},{8,12},{9,13},{10,... | collective-permute-start | bytes 884744 | tf_op jit(solution)/shard_map/ppermute | solution.py:32
  272.0 8.5 %collective-permute-start.32 = (bf16[4,48,384]{2,1,0:T(8,128)(2,1)S(1)}, bf16[4,48,384]{2,1,0:T(8,128)(2,1)S(1)}, u32[]{:S(2)}, u32[]{:S(2)}) collective-permute-start(bf16[4,48,384]{2,1,0:T(8,128)(2,1)S(1)} %fusion.19), channel_id=1, source_target_pairs={{0,16},{1,17},{2,18},{3,19},{4,20},{5,21},{6,22},{7,23},{8,24},{9,... | collective-permute-start | bytes 442376 | tf_op jit(solution)/shard_map/ppermute | solution.py:32
  276.0 13.1 %collective-permute-start.21 = (bf16[4,2,48,384]{3,2,0,1:T(8,128)(2,1)S(1)}, bf16[4,2,48,384]{3,2,0,1:T(8,128)(2,1)S(1)}, u32[]{:S(2)}, u32[]{:S(2)}) collective-permute-start(bf16[4,2,48,384]{3,2,0,1:T(8,128)(2,1)S(1)} %fusion.5), channel_id=1, source_target_pairs={{0,8},{1,9},{2,10},{3,11},{4,12},{5,13},{6,14},{7,15},{8,0},{9,1},... | collective-permute-start | bytes 884744 | tf_op jit(solution)/shard_map/ppermute | solution.py:32
  276.1 13.2 %collective-permute-start.28 = (bf16[4,48,384]{2,1,0:T(8,128)(2,1)S(1)}, bf16[4,48,384]{2,1,0:T(8,128)(2,1)S(1)}, u32[]{:S(2)}, u32[]{:S(2)}) collective-permute-start(bf16[4,48,384]{2,1,0:T(8,128)(2,1)S(1)} %fusion.18), channel_id=1, source_target_pairs={{0,16},{1,17},{2,18},{3,19},{4,20},{5,21},{6,22},{7,23},{8,24},{9,... | collective-permute-start | bytes 442376 | tf_op jit(solution)/shard_map/ppermute | solution.py:32
  289.2 8.8 %collective-permute-start.22 = (bf16[4,48,384]{2,1,0:T(8,128)(2,1)S(1)}, bf16[4,48,384]{2,1,0:T(8,128)(2,1)S(1)}, u32[]{:S(2)}, u32[]{:S(2)}) collective-permute-start(bf16[4,48,384]{2,1,0:T(8,128)(2,1)S(1)} %fusion.17), channel_id=1, source_target_pairs={{0,16},{1,17},{2,18},{3,19},{4,20},{5,21},{6,22},{7,23},{8,24},{9,... | collective-permute-start | bytes 442376 | tf_op jit(solution)/shard_map/ppermute | solution.py:32
  298.3 2.2 collective-permute-start.33
  300.2 9.9 %collective-permute-start.37 = (bf16[2,1,2,2,48,768]{5,4,2,3,1,0:T(8,128)(2,1)S(1)}, bf16[2,1,2,2,48,768]{5,4,2,3,1,0:T(8,128)(2,1)S(1)}, u32[]{:S(2)}, u32[]{:S(2)}) collective-permute-start(bf16[2,1,2,2,48,768]{5,4,2,3,1,0:T(8,128)(2,1)S(1)} %pad_maximum_fusion.1), channel_id=1, source_target_pairs={{0,2},{1,5},{2,0},{3,7},{4,6},{5,1},{6,4},{7,3},{8,10},{9,13},{10,... | collective-permute-start | bytes 1769480 | tf_op jit(solution)/shard_map/ppermute | solution.py:67
  304.2 21.0 %all-to-all-start.4 = ((bf16[32,24,384]{2,1,0:T(8,128)(2,1)}), bf16[32,24,384]{2,1,0:T(8,128)(2,1)S(1)}, u32[]{:S(2)}, u32[]{:S(2)}) async-start(bf16[32,24,384]{2,1,0:T(8,128)(2,1)} %bitcast.104), calls=%async_computation.4 | async-start | bytes 1179648 | tf_op jit(solution)/shard_map/all_to_all | solution.py:634
  325.2 2.7 collective-permute-start.39
  336.6 20.1 %all-to-all-start.5 = ((bf16[32,24,384]{2,1,0:T(8,128)(2,1)}), bf16[32,24,384]{2,1,0:T(8,128)(2,1)S(1)}, u32[]{:S(2)}, u32[]{:S(2)}) async-start(bf16[32,24,384]{2,1,0:T(8,128)(2,1)} %bitcast.106), calls=%async_computation.5 | async-start | bytes 1179648 | tf_op jit(solution)/shard_map/all_to_all | solution.py:634
  347.2 1.5 collective-permute-start.38
  (29 other events, 187.1 us)

commit v4 on v2

--- a/solution.py
+++ b/solution.py
@@ -548,29 +548,31 @@
     )(mine[None], lefts, lefts_other, rights, rights_other)
 
 
-def muon_steps(block):
+def muon_steps(block, scaled_ref):
     values = block.astype(jnp.float32)
-    scaled = (values / (jnp.sqrt(jnp.sum(values * values)) + 1e-07)).astype(jnp.bfloat16)
-    for _ in range(NS_ITERS):
+    scaled_ref[...] = (values / (jnp.sqrt(jnp.sum(values * values)) + 1e-07)).astype(jnp.bfloat16)
+
+    @pl.loop(0, NS_ITERS)
+    def _(iteration):
+        scaled = scaled_ref[...]
         gram = contract(scaled, scaled, 1, 1).astype(jnp.bfloat16)
         square = contract(gram, gram, 1, 0)
         mixed = (COEF_SECOND * gram.astype(jnp.float32) + COEF_THIRD * square).astype(jnp.bfloat16)
-        scaled = (
+        scaled_ref[...] = (
             COEF_FIRST * scaled.astype(jnp.float32) + contract(mixed, scaled, 1, 0)
         ).astype(jnp.bfloat16)
-    return scaled
-
-
-def orthogonalize_halves(place_ref, mine_ref, other_ref, out_ref):
+
+
+def orthogonalize_halves(place_ref, mine_ref, other_ref, out_ref, scaled_ref):
     core = place_ref[0]
     mine, other = mine_ref[...], other_ref[...]
     low, high = jnp.where(core == 1, other, mine), jnp.where(core == 1, mine, other)
-    scaled = muon_steps(jnp.concatenate([low, high], axis=1))
-    out_ref[...] = split_columns(scaled, core)[0]
+    muon_steps(jnp.concatenate([low, high], axis=1), scaled_ref)
+    out_ref[...] = split_columns(scaled_ref[...], core)[0]
 
 
 def orthogonalize_whole(block_ref, out_ref):
-    out_ref[0] = muon_steps(block_ref[0])
+    muon_steps(block_ref[0], out_ref.at[0])
 
 
 def muon_cost(count, rows):
@@ -586,6 +588,7 @@
         out_shape=struct(mine.shape, mine.dtype),
         in_specs=[SMEM, VMEM, VMEM],
         out_specs=VMEM,
+        scratch_shapes=[pltpu.VMEM((mine.shape[0], 2 * mine.shape[1]), mine.dtype)],
         compiler_params=pltpu.CompilerParams(vmem_limit_bytes=24 << 20),
         cost_estimate=muon_cost(1, mine.shape[0]),
     )(place, mine, other)
@@ -689,7 +692,8 @@
     if extra:
         spare = momenta[:extra].astype(jnp.bfloat16).reshape(2, extra // 2, share, features)
         spare_mine = lax.dynamic_index_in_dim(spare, core, 0, keepdims=False)
-        spare_other = flip(lax.dynamic_index_in_dim(spare, 1 - core, 0, keepdims=False), 0)
+        spare_other = lax.dynamic_index_in_dim(spare, 1 - core, 0, keepdims=False)
+        spare_other = flip(spare_other, 0)
         spare = joined(spare_mine, spare_other, core, 1).reshape(extra // 2, 2 * share, features)
         modulation, spare = lax.optimization_barrier((modulation, spare))
         spare = gather_step(spare, spare_bits, spare_bits[0], myself)

time: 355 us -> 355 us (level)
  no operation moved by 1% of the time
where the time goes in v4:
time: 355 us; the launch traced here: 351 us
  waiting for transfers between devices  162 us (46%)
  Pallas kernels  61.4 us (17%)
  starting transfers between devices  60.9 us (17%)
  other arithmetic  40.9 us (12%)
  local copies, waits for them, and re-layouts  17.7 us (5%)
  matrix products  4.4 us (1%)
    ppermute x38, waiting for transfers between devices, flip(): lax.ppermute(values, 'dp', [(i, i ^ 1 << bit) for i in range(devices)])  133 us
    ppermute x38, starting transfers between devices, flip(): lax.ppermute(values, 'dp', [(i, i ^ 1 << bit) for i in range(devices)])  36.8 us
    all_to_all x6, waiting for transfers between devices, all_to_all(): return lax.all_to_all(values, 'dp', split_axis=0, concat_axis=0, tiled=True)  28.7 us
    all_to_all x6, starting transfers between devices, all_to_all(): return lax.all_to_all(values, 'dp', split_axis=0, concat_axis=0, tiled=True)  22.6 us
    select_n x27, other arithmetic, joined(): jnp.where(taken == 1, jnp.stack([other, values], axis), jnp.stack([values...  21.8 us
    pallas_call x3, Pallas kernels, run_products(): pl.pallas_call(functools.partial(pair_products, chunk), name='pair_produc...  16.7 us
    pallas_call x1, Pallas kernels, run_mlp(): pl.pallas_call(functools.partial(mlp_both_ways, *mlp_orders), name='mlp_b...  11.6 us
    pallas_call x1, Pallas kernels, run_attention_backward(): pl.pallas_call(functools.partial(attention_backward, order), name='attent...  10.9 us
  transfers between devices with their start and end apart: 46, of which 23 were waited for; matrix products, arithmetic and copies ran while one was open for 15% of the time, Pallas kernels for 15%

profile of v4, /device:TPU:0, one launch (start us, length us, event | category | flops | bytes accessed | tf_op | source)
XLA Modules:
  0.0 350.9 jit_solution(14789765898685857303)
XLA Ops:
  4.8 3.9 %collective-permute-start.1 = (bf16[4,48,384]{2,1,0:T(8,128)(2,1)S(1)}, bf16[4,48,384]{2,1,0:T(8,128)(2,1)S(1)}, u32[]{:S(2)}, u32[]{:S(2)}) collective-permute-start(bf16[4,48,384]{2,1,0:T(8,128)(2,1)S(1)} %get-tuple-element.99), channel_id=1, source_target_pairs={{0,16},{1,17},{2,18},{3,19},{4,20},{5,21},{6,22},{7,23},{8,24},{9,... | collective-permute-start | bytes 442376 | tf_op jit(solution)/shard_map/ppermute | solution.py:32
  11.2 3.8 %all-to-all-start = ((bf16[32,2,552]{2,1,0:T(2,128)(2,1)}), bf16[32,2,552]{2,1,0:T(2,128)(2,1)S(1)}, u32[]{:S(2)}, u32[]{:S(2)}) async-start(bf16[32,2,552]{2,1,0:T(2,128)(2,1)} %reshape.2058), calls=%async_computation | async-start | bytes 163840 | tf_op jit(solution)/shard_map/all_to_all | solution.py:612
  15.1 7.6 %all-to-all-done = bf16[32,2,552]{2,1,0:T(2,128)(2,1)S(1)} async-done(((bf16[32,2,552]{2,1,0:T(2,128)(2,1)}), bf16[32,2,552]{2,1,0:T(2,128)(2,1)S(1)}, u32[]{:S(2)}, u32[]{:S(2)}) %all-to-all-start) | async-done | bytes 70688 | tf_op jit(solution)/shard_map/all_to_all | solution.py:612
  23.8 2.2 collective-permute-start.11
  26.9 8.7 %collective-permute-done.6 = bf16[4,48,384]{2,1,0:T(8,128)(2,1)S(1)} collective-permute-done((bf16[4,48,384]{2,1,0:T(8,128)(2,1)S(1)}, bf16[4,48,384]{2,1,0:T(8,128)(2,1)S(1)}, u32[]{:S(2)}, u32[]{:S(2)}) %collective-permute-start.6) | collective-permute-done | bytes 147488 | tf_op jit(solution)/shard_map/ppermute | solution.py:32
  40.6 3.6 %all-to-all-start.1 = ((f32[32,1,4608]{2,1,0:T(1,128)}), f32[32,1,4608]{2,1,0:T(1,128)}, u32[]{:S(2)}, u32[]{:S(2)}) async-start(f32[32,1,4608]{2,1,0:T(1,128)} %all_to_all.49), calls=%async_computation.1 | async-start | bytes 1179648 | tf_op jit(solution)/shard_map/all_to_all | solution.py:612
  44.3 1.9 collective-permute-start.7
  46.2 1.5 collective-permute-start.12
  48.5 14.1 %collective-permute-done.7 = bf16[2,4,48,384]{3,2,1,0:T(8,128)(2,1)S(1)} collective-permute-done((bf16[2,4,48,384]{3,2,1,0:T(8,128)(2,1)S(1)}, bf16[2,4,48,384]{3,2,1,0:T(8,128)(2,1)S(1)}, u32[]{:S(2)}, u32[]{:S(2)}) %collective-permute-start.7) | collective-permute-done | bytes 294944 | tf_op jit(solution)/shard_map/ppermute | solution.py:32
  62.7 1.6 collective-permute-start.8
  65.3 6.8 %collective-permute-done.3 = bf16[2,2,4,48,384]{4,3,2,1,0:T(8,128)(2,1)S(1)} collective-permute-done((bf16[2,2,4,48,384]{4,3,2,1,0:T(8,128)(2,1)S(1)}, bf16[2,2,4,48,384]{4,3,2,1,0:T(8,128)(2,1)S(1)}, u32[]{:S(2)}, u32[]{:S(2)}) %collective-permute-start.3) | collective-permute-done | bytes 589856 | tf_op jit(solution)/shard_map/ppermute | solution.py:32
  74.9 2.7 collective-permute-done.8
  88.8 15.7 %collective-permute-done.4 = bf16[2,2,2,4,48,384]{5,4,3,2,1,0:T(8,128)(2,1)} collective-permute-done((bf16[2,2,2,4,48,384]{5,4,3,2,1,0:T(8,128)(2,1)}, bf16[2,2,2,4,48,384]{5,4,3,2,1,0:T(8,128)(2,1)}, u32[]{:S(2)}, u32[]{:S(2)}) %collective-permute-start.4) | collective-permute-done | bytes 1179680 | tf_op jit(solution)/shard_map/ppermute | solution.py:32
  105.7 2.2 maximum_select_fusion
  108.3 3.7 %maximum_select_fusion.1 = bf16[2,2,2,2,4,48,384]{6,5,4,3,2,1,0:T(8,128)(2,1)} fusion(bf16[1,2,2,2,4,48,384]{6,5,4,3,2,1,0:T(8,128)(2,1)S(1)} %copy-done.7, bf16[1,2,2,2,4,48,384]{6,5,4,3,2,1,0:T(8,128)(2,1)} %bitcast.39, pred[]{:T(512)S(6)} %eq.21), kind=kLoop, calls=%fused_computation.1 | loop fusion | flops 3538944 | bytes 4718593 | tf_op jit(solution)/shard_map/jit(_where)/select_n | solution.py:40
  112.1 3.6 %maximum_select_fusion.2 = bf16[2,2,2,2,4,48,384]{6,5,4,3,2,1,0:T(8,128)(2,1)} fusion(bf16[1,2,2,2,4,48,384]{6,5,4,3,2,1,0:T(8,128)(2,1)S(1)} %copy-done.6, bf16[1,2,2,2,4,48,384]{6,5,4,3,2,1,0:T(8,128)(2,1)} %bitcast.43, pred[]{:T(512)S(6)} %eq.24), kind=kLoop, calls=%fused_computation.2 | loop fusion | flops 3538944 | bytes 4718593 | tf_op jit(solution)/shard_map/jit(_where)/select_n | solution.py:40
  121.7 6.4 %attention_forward.1 = (bf16[3,256,768]{2,1,0:T(8,128)(2,1)}, bf16[3,256,768]{2,1,0:T(8,128)(2,1)S(1)}, f32[256,768]{1,0:T(8,128)S(1)}, f32[256,768]{1,0:T(8,128)S(1)}) custom-call(s32[2]{0:T(128)S(1)} %pad_add_fusion.place_ref, bf16[256,768]{1,0:T(8,128)(2,1)S(1)} %bitcast.206, f32[6,768]{1,0:T(8,128)S(1)} %slice_add_fusion.mod_ref, ...), custom_call_target="tpu_custom_call" | custom-call | flops 2013265920 | bytes 8650752 | tf_op jit(solution)/shard_map/attention_forward/pallas_call | solution.py:410
  128.4 11.6 %mlp_both_ways.1 = (bf16[256,768]{1,0:T(8,128)(2,1)}, bf16[4,256,768]{2,1,0:T(8,128)(2,1)}, bf16[5,256,384]{2,1,0:T(8,128)(2,1)S(1)}, bf16[5,256,384]{2,1,0:T(8,...) custom-call(s32[2]{0:T(128)S(1)} %pad_add_fusion.place_ref, ...), custom_call_target="tpu_custom_call" | custom-call | flops 4831838208 | bytes 17301504 | tf_op jit(solution)/shard_map/mlp_both_ways/pallas_call | solution.py:435
  140.6 10.9 %attention_backward.1 = (f32[256,768]{1,0:T(8,128)}, bf16[4,256,384]{2,1,0:T(8,128)(2,1)S(1)}, bf16[4,256,384]{2,1,0:T(8,128)(2,1)}, f32[14,768]{1,0:T(8,128)S(1)}) custom-call(s32[2]{0:T(128)S(1)} %pad_add_fusion.place_ref, bf16[256,768]{1,0:T(8,128)(2,1)S(1)} %bitcast.207, f32[6,768]{1,0:T(8,128)S(1)} %slice_add_fusion.mod_ref, ...), custom_call_target="tpu_custom_call" | custom-call | flops 3221225472 | bytes 9437184 | tf_op jit(solution)/shard_map/attention_backward/pallas_call | solution.py:486
  153.1 5.5 %pair_products.5 = (f32[4,384,384]{2,1,0:T(8,128)}, bf16[4,384,384]{2,1,0:T(8,128)(2,1)}) custom-call(s32[1]{0:T(128)} %bitcast.71.mine_ref, bf16[3,256,768]{2,1,0:T(8,128)(2,1)} %get-tuple-element.48.lefts_ref.left_ref, bf16[3,256,768]{2,1,0:T(8,128)(2,1)} %collective-permute-done.23.left_other_ref, bf16[5,256,384]{2,1,0:T(8,128)(2,1)} %copy-done, ...), custom_call_target="tpu_custom_call" | custom-call | flops 1207959552 | bytes 7077888 | tf_op jit(solution)/shard_map/pair_products/pallas_call | solution.py:537
  162.1 4.6 %all-to-all-start.2 = ((bf16[32,2,2640]{2,1,0:T(2,128)(2,1)}), bf16[32,2,2640]{2,1,0:T(2,128)(2,1)S(1)}, u32[]{:S(2)}, u32[]{:S(2)}) async-start(bf16[32,2,2640]{2,1,0:T(2,128)(2,1)} %reshape.2060), calls=%async_computation.2 | async-start | bytes 688128 | tf_op jit(solution)/shard_map/all_to_all | solution.py:612
  166.7 2.7 collective-permute-start.34
  170.4 5.6 %pair_products.4 = (f32[4,384,384]{2,1,0:T(8,128)}, bf16[4,384,384]{2,1,0:T(8,128)(2,1)}) custom-call(s32[1]{0:T(128)} %bitcast.63.mine_ref, bf16[3,256,768]{2,1,0:T(8,128)(2,1)} %get-tuple-element.48.lefts_ref.left_ref, bf16[3,256,768]{2,1,0:T(8,128)(2,1)} %collective-permute-done.23.left_other_ref, bf16[4,256,384]{2,1,0:T(8,128)(2,1)} %copy-done.4, ...), custom_call_target="tpu_custom_call" | custom-call | flops 1207959552 | bytes 7077888 | tf_op jit(solution)/shard_map/pair_products/pallas_call | solution.py:537
  177.4 3.5 %collective-permute-done.34 = bf16[1,48,768]{2,1,0:T(8,128)(2,1)S(1)} collective-permute-done((bf16[1,48,768]{2,1,0:T(8,128)(2,1)S(1)}, bf16[1,48,768]{2,1,0:T(8,128)(2,1)S(1)}, u32[]{:S(2)}, u32[]{:S(2)}) %collective-permute-start.34) | collective-permute-done | bytes 73760 | tf_op jit(solution)/shard_map/ppermute | solution.py:32
  182.5 26.6 %collective-permute-done.35 = bf16[1,2,48,768]{3,2,1,0:T(8,128)(2,1)S(1)} collective-permute-done((bf16[1,2,48,768]{3,2,1,0:T(8,128)(2,1)S(1)}, bf16[1,2,48,768]{3,2,1,0:T(8,128)(2,1)S(1)}, u32[]{:S(2)}, u32[]{:S(2)}) %collective-permute-start.35) | collective-permute-done | bytes 147488 | tf_op jit(solution)/shard_map/ppermute | solution.py:32
  212.6 5.6 %pair_products.3 = (f32[4,384,384]{2,1,0:T(8,128)}, bf16[4,384,384]{2,1,0:T(8,128)(2,1)}) custom-call(s32[1]{0:T(128)} %bitcast.49.mine_ref, bf16[4,256,768]{2,1,0:T(8,128)(2,1)} %get-tuple-element.58.left_ref, bf16[4,256,768]{2,1,0:T(8,128)(2,1)} %collective-permute-done.17.left_other_ref, bf16[5,256,384]{2,1,0:T(8,128)(2,1)} %copy-done, ...), custom_call_target="tpu_custom_call" | custom-call | flops 1207959552 | bytes 7077888 | tf_op jit(solution)/shard_map/pair_products/pallas_call | solution.py:537
  219.7 1.8 fusion.8
  221.5 2.7 all-to-all-start.3
  224.3 1.7 convert_add_fusion
  226.1 1.9 collective-permute-start.30
  228.0 1.7 convert_add_fusion.1
  231.3 16.2 %collective-permute-done.19 = bf16[4,384,384]{2,1,0:T(8,128)(2,1)} collective-permute-done((bf16[4,384,384]{2,1,0:T(8,128)(2,1)}, bf16[4,384,384]{2,1,0:T(8,128)(2,1)}, u32[]{:S(2)}, u32[]{:S(2)}) %collective-permute-start.19) | collective-permute-done | bytes 1179680 | tf_op jit(solution)/shard_map/ppermute | solution.py:32
  247.5 1.6 convert_add_fusion.2
  251.5 8.6 %collective-permute-done.26 = bf16[4,2,2,48,384]{4,3,0,1,2:T(8,128)(2,1)S(1)} collective-permute-done((bf16[4,2,2,48,384]{4,3,0,1,2:T(8,128)(2,1)S(1)}, bf16[4,2,2,48,384]{4,3,0,1,2:T(8,128)(2,1)S(1)}, u32[]{:S(2)}, u32[]{:S(2)}) %collective-permute-start.26) | collective-permute-done | bytes 589856 | tf_op jit(solution)/shard_map/ppermute | solution.py:32
  261.0 3.9 %collective-permute-done.31 = bf16[4,2,48,384]{3,2,0,1:T(8,128)(2,1)S(1)} collective-permute-done((bf16[4,2,48,384]{3,2,0,1:T(8,128)(2,1)S(1)}, bf16[4,2,48,384]{3,2,0,1:T(8,128)(2,1)S(1)}, u32[]{:S(2)}, u32[]{:S(2)}) %collective-permute-start.31) | collective-permute-done | bytes 294944 | tf_op jit(solution)/shard_map/ppermute | solution.py:32
  265.1 3.4 collective-permute-done.27
  270.4 3.4 collective-permute-done.32
  273.8 7.3 %collective-permute-done.21 = bf16[4,2,48,384]{3,2,0,1:T(8,128)(2,1)S(1)} collective-permute-done((bf16[4,2,48,384]{3,2,0,1:T(8,128)(2,1)S(1)}, bf16[4,2,48,384]{3,2,0,1:T(8,128)(2,1)S(1)}, u32[]{:S(2)}, u32[]{:S(2)}) %collective-permute-start.21) | collective-permute-done | bytes 294944 | tf_op jit(solution)/shard_map/ppermute | solution.py:32
  281.3 7.9 %collective-permute-done.22 = bf16[4,48,384]{2,1,0:T(8,128)(2,1)S(1)} collective-permute-done((bf16[4,48,384]{2,1,0:T(8,128)(2,1)S(1)}, bf16[4,48,384]{2,1,0:T(8,128)(2,1)S(1)}, u32[]{:S(2)}, u32[]{:S(2)}) %collective-permute-start.22) | collective-permute-done | bytes 147488 | tf_op jit(solution)/shard_map/ppermute | solution.py:32
  292.6 1.8 fusion.36
  295.3 4.4 %all-to-all-start.4 = ((bf16[32,24,384]{2,1,0:T(8,128)(2,1)}), bf16[32,24,384]{2,1,0:T(8,128)(2,1)S(1)}, u32[]{:S(2)}, u32[]{:S(2)}) async-start(bf16[32,24,384]{2,1,0:T(8,128)(2,1)} %bitcast.104), calls=%async_computation.4 | async-start | bytes 1179648 | tf_op jit(solution)/shard_map/all_to_all | solution.py:612
  301.5 1.7 convert_multiply_fusion
  303.3 13.2 %all-to-all-done.4 = bf16[32,24,384]{2,1,0:T(8,128)(2,1)S(1)} async-done(((bf16[32,24,384]{2,1,0:T(8,128)(2,1)}), bf16[32,24,384]{2,1,0:T(8,128)(2,1)S(1)}, u32[]{:S(2)}, u32[]{:S(2)}) %all-to-all-start.4) | async-done | bytes 589856 | tf_op jit(solution)/shard_map/all_to_all | solution.py:612
  317.1 2.1 fusion.block_ref
  319.2 8.6 %orthogonalize_halves.1 = bf16[768,384]{1,0:T(8,128)(2,1)} custom-call(s32[2]{0:T(128)S(1)} %pad_add_fusion.place_ref, bf16[768,384]{1,0:T(8,128)(2,1)S(1)} %bitcast.204, bf16[768,384]{1,0:T(8,128)(2,1)S(1)} %collective-permute-done.39.other_ref), custom_call_target="tpu_custom_call" | custom-call | flops 5435817984 | bytes 2359296 | tf_op jit(solution)/shard_map/orthogonalize_halves/pallas_call | solution.py:585
  327.9 3.5 %all-to-all-start.5 = ((bf16[32,24,384]{2,1,0:T(8,128)(2,1)}), bf16[32,24,384]{2,1,0:T(8,128)(2,1)S(1)}, u32[]{:S(2)}, u32[]{:S(2)}) async-start(bf16[32,24,384]{2,1,0:T(8,128)(2,1)} %bitcast.106), calls=%async_computation.5 | async-start | bytes 1179648 | tf_op jit(solution)/shard_map/all_to_all | solution.py:612
  331.4 7.2 %orthogonalize_whole.1 = bf16[1,768,768]{2,1,0:T(8,128)(2,1)S(1)} custom-call(bf16[1,768,768]{2,1,0:T(8,128)(2,1)S(1)} %fusion.block_ref), custom_call_target="tpu_custom_call" | custom-call | flops 5435817984 | bytes 2359296 | tf_op jit(solution)/shard_map/orthogonalize_whole/pallas_call | solution.py:599
  340.3 7.8 %all-to-all-done.5 = bf16[32,24,384]{2,1,0:T(8,128)(2,1)S(1)} async-done(((bf16[32,24,384]{2,1,0:T(8,128)(2,1)}), bf16[32,24,384]{2,1,0:T(8,128)(2,1)S(1)}, u32[]{:S(2)}, u32[]{:S(2)}) %all-to-all-start.5) | async-done | bytes 589856 | tf_op jit(solution)/shard_map/all_to_all | solution.py:612
  (243 shorter events, 68.6 us)
Async XLA Ops:
  2.0 36.5 %copy-start.9 = (bf16[18,24,768]{2,1,0:T(8,128)(2,1)}, bf16[18,24,768]{2,1,0:T(8,128)(2,1)S(1)}, u32[]{:S(2)}) copy-start(bf16[18,24,768]{2,1,0:T(8,128)(2,1)S(1)} %convert_element_type.152) | copy-start | bytes 1990660
  2.2 1.7 collective-permute-start
  4.8 21.2 %collective-permute-start.1 = (bf16[4,48,384]{2,1,0:T(8,128)(2,1)S(1)}, bf16[4,48,384]{2,1,0:T(8,128)(2,1)S(1)}, u32[]{:S(2)}, u32[]{:S(2)}) collective-permute-start(bf16[4,48,384]{2,1,0:T(8,128)(2,1)S(1)} %get-tuple-element.99), channel_id=1, source_target_pairs={{0,16},{1,17},{2,18},{3,19},{4,20},{5,21},{6,22},{7,23},{8,24},{9,... | collective-permute-start | bytes 442376 | tf_op jit(solution)/shard_map/ppermute | solution.py:32
  11.2 11.4 %all-to-all-start = ((bf16[32,2,552]{2,1,0:T(2,128)(2,1)}), bf16[32,2,552]{2,1,0:T(2,128)(2,1)S(1)}, u32[]{:S(2)}, u32[]{:S(2)}) async-start(bf16[32,2,552]{2,1,0:T(2,128)(2,1)} %reshape.2058), calls=%async_computation | async-start | bytes 163840 | tf_op jit(solution)/shard_map/all_to_all | solution.py:612
  23.0 60.1 %copy-start.15 = (bf16[32,1,1104]{0,2,1:T(8,128)(2,1)}, bf16[32,1,1104]{0,2,1:T(8,128)(2,1)S(1)}, u32[]{:S(2)}) copy-start(bf16[32,1,1104]{0,2,1:T(8,128)(2,1)S(1)} %copy.94) | copy-start | bytes 211972
  23.1 12.5 %collective-permute-start.6 = (bf16[4,48,384]{2,1,0:T(8,128)(2,1)S(1)}, bf16[4,48,384]{2,1,0:T(8,128)(2,1)S(1)}, u32[]{:S(2)}, u32[]{:S(2)}) collective-permute-start(bf16[4,48,384]{2,1,0:T(8,128)(2,1)S(1)} %get-tuple-element.98), channel_id=1, source_target_pairs={{0,16},{1,17},{2,18},{3,19},{4,20},{5,21},{6,22},{7,23},{8,24},{9,... | collective-permute-start | bytes 442376 | tf_op jit(solution)/shard_map/ppermute | solution.py:32
  23.8 22.3 %collective-permute-start.11 = (bf16[4,48,384]{2,1,0:T(8,128)(2,1)}, bf16[4,48,384]{2,1,0:T(8,128)(2,1)S(1)}, u32[]{:S(2)}, u32[]{:S(2)}) collective-permute-start(bf16[4,48,384]{2,1,0:T(8,128)(2,1)} %get-tuple-element.97), channel_id=1, source_target_pairs={{0,16},{1,17},{2,18},{3,19},{4,20},{5,21},{6,22},{7,23},{8,24},{9,... | collective-permute-start | bytes 442376 | tf_op jit(solution)/shard_map/ppermute | solution.py:32
  37.1 10.7 %collective-permute-start.2 = (bf16[2,4,48,384]{3,2,1,0:T(8,128)(2,1)}, bf16[2,4,48,384]{3,2,1,0:T(8,128)(2,1)S(1)}, u32[]{:S(2)}, u32[]{:S(2)}) collective-permute-start(bf16[2,4,48,384]{3,2,1,0:T(8,128)(2,1)} %maximum_select_fusion.20), channel_id=1, source_target_pairs={{0,4},{1,5},{2,6},{3,7},{4,0},{5,1},{6,2},{7,3},{8,12},{9,13},{10,... | collective-permute-start | bytes 884744 | tf_op jit(solution)/shard_map/ppermute | solution.py:32
  40.6 47.0 %all-to-all-start.1 = ((f32[32,1,4608]{2,1,0:T(1,128)}), f32[32,1,4608]{2,1,0:T(1,128)}, u32[]{:S(2)}, u32[]{:S(2)}) async-start(f32[32,1,4608]{2,1,0:T(1,128)} %all_to_all.49), calls=%async_computation.1 | async-start | bytes 1179648 | tf_op jit(solution)/shard_map/all_to_all | solution.py:612
  44.3 18.4 %collective-permute-start.7 = (bf16[2,4,48,384]{3,2,1,0:T(8,128)(2,1)S(1)}, bf16[2,4,48,384]{3,2,1,0:T(8,128)(2,1)S(1)}, u32[]{:S(2)}, u32[]{:S(2)}) collective-permute-start(bf16[2,4,48,384]{3,2,1,0:T(8,128)(2,1)S(1)} %maximum_select_fusion.22), channel_id=1, source_target_pairs={{0,8},{1,9},{2,10},{3,11},{4,12},{5,13},{6,14},{7,15},{8,0},{9,1},... | collective-permute-start | bytes 884744 | tf_op jit(solution)/shard_map/ppermute | solution.py:32
  46.2 18.2 %collective-permute-start.12 = (bf16[2,4,48,384]{3,2,1,0:T(8,128)(2,1)S(1)}, bf16[2,4,48,384]{3,2,1,0:T(8,128)(2,1)S(1)}, u32[]{:S(2)}, u32[]{:S(2)}) collective-permute-start(bf16[2,4,48,384]{3,2,1,0:T(8,128)(2,1)S(1)} %maximum_select_fusion.24), channel_id=1, source_target_pairs={{0,2},{1,3},{2,0},{3,1},{4,6},{5,7},{6,4},{7,5},{8,10},{9,11},{10,... | collective-permute-start | bytes 884744 | tf_op jit(solution)/shard_map/ppermute | solution.py:32
  47.9 24.1 %collective-permute-start.3 = (bf16[2,2,4,48,384]{4,3,2,1,0:T(8,128)(2,1)S(1)}, bf16[2,2,4,48,384]{4,3,2,1,0:T(8,128)(2,1)S(1)}, u32[]{:S(2)}, u32[]{:S(2)}) collective-permute-start(bf16[2,2,4,48,384]{4,3,2,1,0:T(8,128)(2,1)S(1)} %maximum_select_fusion.11), channel_id=1, source_target_pairs={{0,2},{1,3},{2,0},{3,1},{4,6},{5,7},{6,4},{7,5},{8,10},{9,11},{10,... | collective-permute-start | bytes 1769480 | tf_op jit(solution)/shard_map/ppermute | solution.py:32
  62.7 14.8 %collective-permute-start.8 = (bf16[2,2,4,48,384]{4,3,2,1,0:T(8,128)(2,1)S(1)}, bf16[2,2,4,48,384]{4,3,2,1,0:T(8,128)(2,1)S(1)}, u32[]{:S(2)}, u32[]{:S(2)}) collective-permute-start(bf16[2,2,4,48,384]{4,3,2,1,0:T(8,128)(2,1)S(1)} %maximum_select_fusion.13), channel_id=1, source_target_pairs={{0,4},{1,5},{2,6},{3,7},{4,0},{5,1},{6,2},{7,3},{8,12},{9,13},{10,... | collective-permute-start | bytes 1769480 | tf_op jit(solution)/shard_map/ppermute | solution.py:32
  64.5 16.3 %collective-permute-start.13 = (bf16[2,2,4,48,384]{4,3,2,1,0:T(8,128)(2,1)S(1)}, bf16[2,2,4,48,384]{4,3,2,1,0:T(8,128)(2,1)S(1)}, u32[]{:S(2)}, u32[]{:S(2)}) collective-permute-start(bf16[2,2,4,48,384]{4,3,2,1,0:T(8,128)(2,1)S(1)} %maximum_select_fusion.15), channel_id=1, source_target_pairs={{0,8},{1,9},{2,10},{3,11},{4,12},{5,13},{6,14},{7,15},{8,0},{9,1},... | collective-permute-start | bytes 1769480 | tf_op jit(solution)/shard_map/ppermute | solution.py:32
  73.3 31.1 %collective-permute-start.4 = (bf16[2,2,2,4,48,384]{5,4,3,2,1,0:T(8,128)(2,1)}, bf16[2,2,2,4,48,384]{5,4,3,2,1,0:T(8,128)(2,1)}, u32[]{:S(2)}, u32[]{:S(2)}) collective-permute-start(bf16[2,2,2,4,48,384]{5,4,3,2,1,0:T(8,128)(2,1)} %maximum_select_fusion.3), channel_id=1, source_target_pairs={{0,8},{1,9},{2,10},{3,11},{4,12},{5,13},{6,14},{7,15},{8,0},{9,1},... | collective-permute-start | bytes 3538952 | tf_op jit(solution)/shard_map/ppermute | solution.py:32
  78.8 26.9 %collective-permute-start.9 = (bf16[2,2,2,4,48,384]{5,4,3,2,1,0:T(8,128)(2,1)}, bf16[2,2,2,4,48,384]{5,4,3,2,1,0:T(8,128)(2,1)}, u32[]{:S(2)}, u32[]{:S(2)}) collective-permute-start(bf16[2,2,2,4,48,384]{5,4,3,2,1,0:T(8,128)(2,1)} %maximum_select_fusion.4), channel_id=1, source_target_pairs={{0,2},{1,3},{2,0},{3,1},{4,6},{5,7},{6,4},{7,5},{8,10},{9,11},{10,... | collective-permute-start | bytes 3538952 | tf_op jit(solution)/shard_map/ppermute | solution.py:32
  82.0 26.3 %collective-permute-start.14 = (bf16[2,2,2,4,48,384]{5,4,3,2,1,0:T(8,128)(2,1)}, bf16[2,2,2,4,48,384]{5,4,3,2,1,0:T(8,128)(2,1)}, u32[]{:S(2)}, u32[]{:S(2)}) collective-permute-start(bf16[2,2,2,4,48,384]{5,4,3,2,1,0:T(8,128)(2,1)} %maximum_select_fusion.6), channel_id=1, source_target_pairs={{0,4},{1,5},{2,6},{3,7},{4,0},{5,1},{6,2},{7,3},{8,12},{9,13},{10,... | collective-permute-start | bytes 3538952 | tf_op jit(solution)/shard_map/ppermute | solution.py:32
  107.9 13.7 %collective-permute-start.10 = (bf16[16,4,48,384]{3,2,1,0:T(8,128)(2,1)S(1)}, bf16[16,4,48,384]{3,2,1,0:T(8,128)(2,1)}, u32[]{:S(2)}, u32[]{:S(2)}) collective-permute-start(bf16[16,4,48,384]{3,2,1,0:T(8,128)(2,1)S(1)} %bitcast.200), channel_id=1, source_target_pairs={{0,1},{1,0},{2,3},{3,2},{4,5},{5,4},{6,7},{7,6},{8,9},{9,8},{10,11... | collective-permute-start | bytes 7077896 | tf_op jit(solution)/shard_map/ppermute | solution.py:32
  112.0 16.4 %collective-permute-start.15 = (bf16[16,4,48,384]{3,2,1,0:T(8,128)(2,1)}, bf16[16,4,48,384]{3,2,1,0:T(8,128)(2,1)}, u32[]{:S(2)}, u32[]{:S(2)}) collective-permute-start(bf16[16,4,48,384]{3,2,1,0:T(8,128)(2,1)} %bitcast.42.up_ref), channel_id=1, source_target_pairs={{0,1},{1,0},{2,3},{3,2},{4,5},{5,4},{6,7},{7,6},{8,9},{9,8},{10,11... | collective-permute-start | bytes 7077896 | tf_op jit(solution)/shard_map/ppermute | solution.py:32
  115.7 12.7 %collective-permute-start.16 = (bf16[16,4,48,384]{3,2,1,0:T(8,128)(2,1)}, bf16[16,4,48,384]{3,2,1,0:T(8,128)(2,1)}, u32[]{:S(2)}, u32[]{:S(2)}) collective-permute-start(bf16[16,4,48,384]{3,2,1,0:T(8,128)(2,1)} %bitcast.46.down_ref), channel_id=1, source_target_pairs={{0,1},{1,0},{2,3},{3,2},{4,5},{5,4},{6,7},{7,6},{8,9},{9,8},{10,11... | collective-permute-start | bytes 7077896 | tf_op jit(solution)/shard_map/ppermute | solution.py:32
  117.7 3.0 collective-permute-start.5
  128.0 25.0 %collective-permute-start.23 = (bf16[3,256,768]{2,1,0:T(8,128)(2,1)}, bf16[3,256,768]{2,1,0:T(8,128)(2,1)}, u32[]{:S(2)}, u32[]{:S(2)}) collective-permute-start(bf16[3,256,768]{2,1,0:T(8,128)(2,1)} %get-tuple-element.48.lefts_ref.left_ref), channel_id=1, source_target_pairs={{0,1},{1,0},{2,3},{3,2},{4,5},{5,4},{6,7},{7,6},{8,9},{9,8},{10,11... | collective-permute-start | bytes 3538952 | tf_op jit(solution)/shard_map/ppermute | solution.py:32
  140.0 13.0 %collective-permute-start.18 = (bf16[5,256,384]{2,1,0:T(8,128)(2,1)S(1)}, bf16[5,256,384]{2,1,0:T(8,128)(2,1)}, u32[]{:S(2)}, u32[]{:S(2)}) collective-permute-start(bf16[5,256,384]{2,1,0:T(8,128)(2,1)S(1)} %get-tuple-element.60), channel_id=1, source_target_pairs={{0,1},{1,0},{2,3},{3,2},{4,5},{5,4},{6,7},{7,6},{8,9},{9,8},{10,11... | collective-permute-start | bytes 2949128 | tf_op jit(solution)/shard_map/ppermute | solution.py:32
  140.2 72.0 %collective-permute-start.17 = (bf16[4,256,768]{2,1,0:T(8,128)(2,1)}, bf16[4,256,768]{2,1,0:T(8,128)(2,1)}, u32[]{:S(2)}, u32[]{:S(2)}) collective-permute-start(bf16[4,256,768]{2,1,0:T(8,128)(2,1)} %get-tuple-element.58.left_ref), channel_id=1, source_target_pairs={{0,1},{1,0},{2,3},{3,2},{4,5},{5,4},{6,7},{7,6},{8,9},{9,8},{10,11... | collective-permute-start | bytes 4718600 | tf_op jit(solution)/shard_map/ppermute | solution.py:32
  152.4 17.0 %collective-permute-start.24 = (bf16[4,256,384]{2,1,0:T(8,128)(2,1)}, bf16[4,256,384]{2,1,0:T(8,128)(2,1)S(1)}, u32[]{:S(2)}, u32[]{:S(2)}) collective-permute-start(bf16[4,256,384]{2,1,0:T(8,128)(2,1)} %get-tuple-element.68), channel_id=1, source_target_pairs={{0,1},{1,0},{2,3},{3,2},{4,5},{5,4},{6,7},{7,6},{8,9},{9,8},{10,11... | collective-permute-start | bytes 2359304 | tf_op jit(solution)/shard_map/ppermute | solution.py:32
  158.6 65.7 %collective-permute-start.29 = (bf16[4,384,384]{2,1,0:T(8,128)(2,1)}, bf16[4,384,384]{2,1,0:T(8,128)(2,1)}, u32[]{:S(2)}, u32[]{:S(2)}) collective-permute-start(bf16[4,384,384]{2,1,0:T(8,128)(2,1)} %get-tuple-element.72), channel_id=1, source_target_pairs={{0,4},{1,5},{2,6},{3,7},{4,0},{5,1},{6,2},{7,3},{8,12},{9,13},{10,... | collective-permute-start | bytes 3538952 | tf_op jit(solution)/shard_map/ppermute | solution.py:32
  162.1 49.1 %all-to-all-start.2 = ((bf16[32,2,2640]{2,1,0:T(2,128)(2,1)}), bf16[32,2,2640]{2,1,0:T(2,128)(2,1)S(1)}, u32[]{:S(2)}, u32[]{:S(2)}) async-start(bf16[32,2,2640]{2,1,0:T(2,128)(2,1)} %reshape.2060), calls=%async_computation.2 | async-start | bytes 688128 | tf_op jit(solution)/shard_map/all_to_all | solution.py:612
  166.7 14.3 %collective-permute-start.34 = (bf16[1,48,768]{2,1,0:T(8,128)(2,1)S(1)}, bf16[1,48,768]{2,1,0:T(8,128)(2,1)S(1)}, u32[]{:S(2)}, u32[]{:S(2)}) collective-permute-start(bf16[1,48,768]{2,1,0:T(8,128)(2,1)S(1)} %bitcast.254), channel_id=1, source_target_pairs={{0,16},{1,17},{2,18},{3,19},{4,20},{5,21},{6,22},{7,23},{8,24},{9,... | collective-permute-start | bytes 221192 | tf_op jit(solution)/shard_map/ppermute | solution.py:32
  175.9 52.0 %collective-permute-start.25 = (bf16[4,384,384]{2,1,0:T(8,128)(2,1)}, bf16[4,384,384]{2,1,0:T(8,128)(2,1)}, u32[]{:S(2)}, u32[]{:S(2)}) collective-permute-start(bf16[4,384,384]{2,1,0:T(8,128)(2,1)} %get-tuple-element.70), channel_id=1, source_target_pairs={{0,8},{1,9},{2,10},{3,11},{4,12},{5,13},{6,14},{7,15},{8,0},{9,1},... | collective-permute-start | bytes 3538952 | tf_op jit(solution)/shard_map/ppermute | solution.py:32
  181.0 28.2 %collective-permute-start.35 = (bf16[1,2,48,768]{3,2,1,0:T(8,128)(2,1)S(1)}, bf16[1,2,48,768]{3,2,1,0:T(8,128)(2,1)S(1)}, u32[]{:S(2)}, u32[]{:S(2)}) collective-permute-start(bf16[1,2,48,768]{3,2,1,0:T(8,128)(2,1)S(1)} %maximum_select_fusion.29), channel_id=1, source_target_pairs={{0,8},{1,9},{2,10},{3,11},{4,12},{5,13},{6,14},{7,15},{8,0},{9,1},... | collective-permute-start | bytes 442376 | tf_op jit(solution)/shard_map/ppermute | solution.py:32
  209.9 80.4 %collective-permute-start.36 = (bf16[1,2,2,48,768]{4,3,1,2,0:T(8,128)(2,1)}, bf16[1,2,2,48,768]{4,3,1,2,0:T(8,128)(2,1)}, u32[]{:S(2)}, u32[]{:S(2)}) collective-permute-start(bf16[1,2,2,48,768]{4,3,1,2,0:T(8,128)(2,1)} %maximum_select_fusion.27), channel_id=1, source_target_pairs={{0,4},{1,3},{2,6},{3,1},{4,0},{5,7},{6,2},{7,5},{8,12},{9,11},{10,... | collective-permute-start | bytes 884744 | tf_op jit(solution)/shard_map/ppermute | solution.py:67
  218.2 29.3 %collective-permute-start.19 = (bf16[4,384,384]{2,1,0:T(8,128)(2,1)}, bf16[4,384,384]{2,1,0:T(8,128)(2,1)}, u32[]{:S(2)}, u32[]{:S(2)}) collective-permute-start(bf16[4,384,384]{2,1,0:T(8,128)(2,1)} %get-tuple-element.62), channel_id=1, source_target_pairs={{0,2},{1,3},{2,0},{3,1},{4,6},{5,7},{6,4},{7,5},{8,10},{9,11},{10,... | collective-permute-start | bytes 3538952 | tf_op jit(solution)/shard_map/ppermute | solution.py:32
  221.5 59.8 %all-to-all-start.3 = ((f32[32,1,24]{2,1,0:T(1,128)}), f32[32,1,24]{2,1,0:T(1,128)S(1)}, u32[]{:S(2)}, u32[]{:S(2)}) async-start(f32[32,1,24]{2,1,0:T(1,128)} %bitcast.114), calls=%async_computation.3 | async-start | bytes 32768 | tf_op jit(solution)/shard_map/all_to_all | solution.py:612
  226.1 23.8 %collective-permute-start.30 = (bf16[4,2,2,48,384]{4,3,0,1,2:T(8,128)(2,1)S(1)}, bf16[4,2,2,48,384]{4,3,0,1,2:T(8,128)(2,1)S(1)}, u32[]{:S(2)}, u32[]{:S(2)}) collective-permute-start(bf16[4,2,2,48,384]{4,3,0,1,2:T(8,128)(2,1)S(1)} %fusion.3), channel_id=1, source_target_pairs={{0,8},{1,9},{2,10},{3,11},{4,12},{5,13},{6,14},{7,15},{8,0},{9,1},... | collective-permute-start | bytes 1769480 | tf_op jit(solution)/shard_map/ppermute | solution.py:32
  229.8 30.3 %collective-permute-start.26 = (bf16[4,2,2,48,384]{4,3,0,1,2:T(8,128)(2,1)S(1)}, bf16[4,2,2,48,384]{4,3,0,1,2:T(8,128)(2,1)S(1)}, u32[]{:S(2)}, u32[]{:S(2)}) collective-permute-start(bf16[4,2,2,48,384]{4,3,0,1,2:T(8,128)(2,1)S(1)} %fusion.2), channel_id=1, source_target_pairs={{0,2},{1,3},{2,0},{3,1},{4,6},{5,7},{6,4},{7,5},{8,10},{9,11},{10,... | collective-permute-start | bytes 1769480 | tf_op jit(solution)/shard_map/ppermute | solution.py:32
  249.2 19.4 %collective-permute-start.20 = (bf16[4,2,2,48,384]{4,3,0,1,2:T(8,128)(2,1)S(1)}, bf16[4,2,2,48,384]{4,3,0,1,2:T(8,128)(2,1)S(1)}, u32[]{:S(2)}, u32[]{:S(2)}) collective-permute-start(bf16[4,2,2,48,384]{4,3,0,1,2:T(8,128)(2,1)S(1)} %fusion.1), channel_id=1, source_target_pairs={{0,4},{1,5},{2,6},{3,7},{4,0},{5,1},{6,2},{7,3},{8,12},{9,13},{10,... | collective-permute-start | bytes 1769480 | tf_op jit(solution)/shard_map/ppermute | solution.py:32
  250.0 14.9 %collective-permute-start.31 = (bf16[4,2,48,384]{3,2,0,1:T(8,128)(2,1)S(1)}, bf16[4,2,48,384]{3,2,0,1:T(8,128)(2,1)S(1)}, u32[]{:S(2)}, u32[]{:S(2)}) collective-permute-start(bf16[4,2,48,384]{3,2,0,1:T(8,128)(2,1)S(1)} %fusion.7), channel_id=1, source_target_pairs={{0,2},{1,3},{2,0},{3,1},{4,6},{5,7},{6,4},{7,5},{8,10},{9,11},{10,... | collective-permute-start | bytes 884744 | tf_op jit(solution)/shard_map/ppermute | solution.py:32
  260.3 8.2 %collective-permute-start.27 = (bf16[4,2,48,384]{3,2,0,1:T(8,128)(2,1)S(1)}, bf16[4,2,48,384]{3,2,0,1:T(8,128)(2,1)S(1)}, u32[]{:S(2)}, u32[]{:S(2)}) collective-permute-start(bf16[4,2,48,384]{3,2,0,1:T(8,128)(2,1)S(1)} %fusion.6), channel_id=1, source_target_pairs={{0,4},{1,5},{2,6},{3,7},{4,0},{5,1},{6,2},{7,3},{8,12},{9,13},{10,... | collective-permute-start | bytes 884744 | tf_op jit(solution)/shard_map/ppermute | solution.py:32
  265.0 8.8 %collective-permute-start.32 = (bf16[4,48,384]{2,1,0:T(8,128)(2,1)S(1)}, bf16[4,48,384]{2,1,0:T(8,128)(2,1)S(1)}, u32[]{:S(2)}, u32[]{:S(2)}) collective-permute-start(bf16[4,48,384]{2,1,0:T(8,128)(2,1)S(1)} %fusion.19), channel_id=1, source_target_pairs={{0,16},{1,17},{2,18},{3,19},{4,20},{5,21},{6,22},{7,23},{8,24},{9,... | collective-permute-start | bytes 442376 | tf_op jit(solution)/shard_map/ppermute | solution.py:32
  268.8 12.3 %collective-permute-start.21 = (bf16[4,2,48,384]{3,2,0,1:T(8,128)(2,1)S(1)}, bf16[4,2,48,384]{3,2,0,1:T(8,128)(2,1)S(1)}, u32[]{:S(2)}, u32[]{:S(2)}) collective-permute-start(bf16[4,2,48,384]{3,2,0,1:T(8,128)(2,1)S(1)} %fusion.5), channel_id=1, source_target_pairs={{0,8},{1,9},{2,10},{3,11},{4,12},{5,13},{6,14},{7,15},{8,0},{9,1},... | collective-permute-start | bytes 884744 | tf_op jit(solution)/shard_map/ppermute | solution.py:32
  268.9 12.4 %collective-permute-start.28 = (bf16[4,48,384]{2,1,0:T(8,128)(2,1)S(1)}, bf16[4,48,384]{2,1,0:T(8,128)(2,1)S(1)}, u32[]{:S(2)}, u32[]{:S(2)}) collective-permute-start(bf16[4,48,384]{2,1,0:T(8,128)(2,1)S(1)} %fusion.18), channel_id=1, source_target_pairs={{0,16},{1,17},{2,18},{3,19},{4,20},{5,21},{6,22},{7,23},{8,24},{9,... | collective-permute-start | bytes 442376 | tf_op jit(solution)/shard_map/ppermute | solution.py:32
  281.2 8.0 %collective-permute-start.22 = (bf16[4,48,384]{2,1,0:T(8,128)(2,1)S(1)}, bf16[4,48,384]{2,1,0:T(8,128)(2,1)S(1)}, u32[]{:S(2)}, u32[]{:S(2)}) collective-permute-start(bf16[4,48,384]{2,1,0:T(8,128)(2,1)S(1)} %fusion.17), channel_id=1, source_target_pairs={{0,16},{1,17},{2,18},{3,19},{4,20},{5,21},{6,22},{7,23},{8,24},{9,... | collective-permute-start | bytes 442376 | tf_op jit(solution)/shard_map/ppermute | solution.py:32
  289.4 2.2 collective-permute-start.33
  291.3 9.9 %collective-permute-start.37 = (bf16[2,1,2,2,48,768]{5,4,2,3,1,0:T(8,128)(2,1)S(1)}, bf16[2,1,2,2,48,768]{5,4,2,3,1,0:T(8,128)(2,1)S(1)}, u32[]{:S(2)}, u32[]{:S(2)}) collective-permute-start(bf16[2,1,2,2,48,768]{5,4,2,3,1,0:T(8,128)(2,1)S(1)} %pad_maximum_fusion.1), channel_id=1, source_target_pairs={{0,2},{1,5},{2,0},{3,7},{4,6},{5,1},{6,4},{7,3},{8,10},{9,13},{10,... | collective-permute-start | bytes 1769480 | tf_op jit(solution)/shard_map/ppermute | solution.py:67
  295.3 21.2 %all-to-all-start.4 = ((bf16[32,24,384]{2,1,0:T(8,128)(2,1)}), bf16[32,24,384]{2,1,0:T(8,128)(2,1)S(1)}, u32[]{:S(2)}, u32[]{:S(2)}) async-start(bf16[32,24,384]{2,1,0:T(8,128)(2,1)} %bitcast.104), calls=%async_computation.4 | async-start | bytes 1179648 | tf_op jit(solution)/shard_map/all_to_all | solution.py:612
  316.5 2.7 collective-permute-start.39
  327.9 20.3 %all-to-all-start.5 = ((bf16[32,24,384]{2,1,0:T(8,128)(2,1)}), bf16[32,24,384]{2,1,0:T(8,128)(2,1)S(1)}, u32[]{:S(2)}, u32[]{:S(2)}) async-start(bf16[32,24,384]{2,1,0:T(8,128)(2,1)} %bitcast.106), calls=%async_computation.5 | async-start | bytes 1179648 | tf_op jit(solution)/shard_map/all_to_all | solution.py:612
  338.7 1.7 collective-permute-start.38
  (29 other events, 181.3 us)
